TPU v7x, 32 devices: a whole 2x2x4 slice. The times are simulated.
32 devices in a mesh: dp: 8 (over z, y), ctx: 4 (over x, core).
Axes of the slice: x: 2, y: 2, z: 4, core: 2. Of those that a mesh axis runs over, the one named last changes fastest.
Arguments:
- tokens: bfloat16 [8, 1024, 2048], P('dp', 'ctx'), may hold values from -6 to 6
- cotangent: bfloat16 [8, 1024, 2048], P('dp', 'ctx'), may hold values from -6 to 6
- domain_ids: int32 [8], P('dp'), may hold values from 0 to 31
- domain_counts: int32 [32], replicated, may hold values from 1024 to 4096
- domain_numer: int32 [32], replicated, may hold values from 1 to 8
- domain_denom: int32 [32], replicated, may hold values from 1 to 8
- attention_gain: bfloat16 [2048], replicated, may hold values from 0.5 to 1.5
- query_gain: bfloat16 [128], replicated, may hold values from 0.796875 to 1.796875
- key_gain: bfloat16 [128], replicated, may hold values from 0.796875 to 1.796875
- query_proj: bfloat16 [2048, 2048], P('dp', 'ctx'), may hold values from -0.125 to 0.125
- key_proj: bfloat16 [2048, 1024], P('dp', 'ctx'), may hold values from -0.125 to 0.125
- value_proj: bfloat16 [2048, 1024], P('dp', 'ctx'), may hold values from -0.125 to 0.125
- gating_proj: bfloat16 [2048, 2048], P('dp', 'ctx'), may hold values from -0.125 to 0.125
- output_proj: bfloat16 [2048, 2048], P('ctx', 'dp'), may hold values from -1 to 1
- swiglu_gain: bfloat16 [2048], replicated, may hold values from 0.5 to 1.5
- swiglu_gate: bfloat16 [2048, 6144], P('dp', 'ctx'), may hold values from -0.125 to 0.125
- swiglu_up: bfloat16 [2048, 6144], P('dp', 'ctx'), may hold values from -0.125 to 0.125
- swiglu_down: bfloat16 [6144, 2048], P('ctx', 'dp'), may hold values from -0.109375 to 0.109375
Outputs:
- layer_out: bfloat16 [8, 1024, 2048], P('dp', 'ctx')
- input_grad: bfloat16 [8, 1024, 2048], P('dp', 'ctx')
- attention_gain_grad: float32 [2048], replicated
- query_gain_grad: float32 [128], replicated
- key_gain_grad: float32 [128], replicated
- query_proj_grad: float32 [2048, 2048], P('dp', 'ctx')
- key_proj_grad: float32 [2048, 1024], P('dp', 'ctx')
- value_proj_grad: float32 [2048, 1024], P('dp', 'ctx')
- gating_proj_grad: float32 [2048, 2048], P('dp', 'ctx')
- output_proj_grad: float32 [2048, 2048], P('ctx', 'dp')
- swiglu_gain_grad: float32 [2048], replicated
- swiglu_gate_grad: float32 [2048, 6144], P('dp', 'ctx')
- swiglu_up_grad: float32 [2048, 6144], P('dp', 'ctx')
- swiglu_down_grad: float32 [6144, 2048], P('ctx', 'dp')
All inputs are finite; a program needn't handle non-finite values.
Results may differ from a plain program's by a relative error of at most 0.019.
Values may be sent and summed in bfloat16 or wider, within the bound.
A program may use at most 192 MiB of HBM per device.

v0:
```python
import functools

import jax
import jax.numpy as jnp
from jax import lax
from jax.experimental import pallas as pl
from jax.experimental.pallas import tpu as pltpu
from jax.sharding import Mesh
from jax.sharding import PartitionSpec as P

LENGTH = 1024

EPSILON = 1e-06
ROPE_BASE = 1000000.0
MESH = pl.DeviceIdType.MESH
BF16 = jnp.bfloat16
F32 = jnp.float32
VMEM_BYTES = 62 * 2**20


def micros(count):
    return pl.CostEstimate(flops=0, transcendentals=0, bytes_accessed=count * 3_300_000)


def dot_nn(left, right):
    return jnp.dot(left, right, preferred_element_type=F32)


def dot_tn(left, right):
    return lax.dot_general(left, right, (((0,), (0,)), ((), ())), preferred_element_type=F32)


def dot_nt(left, right):
    return lax.dot_general(left, right, (((1,), (1,)), ((), ())), preferred_element_type=F32)


def rope_tables(positions, head_width):
    halfway = head_width // 2
    inverse = 1.0 / ROPE_BASE ** (jnp.arange(halfway, dtype=F32) * (2.0 / head_width))
    angles = positions.astype(F32)[:, None] * inverse[None, :]
    return (jnp.cos(angles), jnp.sin(angles))


def rotate(tensor, cosine, sine):
    halfway = tensor.shape[-1] // 2
    first_half = tensor[..., :halfway]
    second_half = tensor[..., halfway:]
    return jnp.concatenate(
        [first_half * cosine - second_half * sine, second_half * cosine + first_half * sine], -1
    )


def unrotate(grads_in, cosine, sine):
    halfway = grads_in.shape[-1] // 2
    first_half = grads_in[..., :halfway]
    second_half = grads_in[..., halfway:]
    return jnp.concatenate(
        [first_half * cosine + second_half * sine, second_half * cosine - first_half * sine], -1
    )


def norm_back(grads_in, values_in, inverse, gain_vec):
    scaled = grads_in * gain_vec
    return inverse * scaled - values_in * (inverse * inverse * inverse) * jnp.mean(
        scaled * values_in, -1, keepdims=True
    )


def greet(neighbours):
    barrier = pltpu.get_barrier_semaphore()
    for neighbour in neighbours:
        pl.semaphore_signal(barrier, inc=1, device_id=neighbour, device_id_type=MESH)
    pl.semaphore_wait(barrier, len(neighbours))


def remote_copies(send, recv, device):
    def remote(index, source, target, axis):
        return pltpu.make_async_remote_copy(
            src_ref=source,
            dst_ref=target,
            send_sem=send.at[index],
            recv_sem=recv.at[index],
            device_id=device[axis],
            device_id_type=MESH,
        )

    return remote


def place():
    y, x, c = lax.axis_index("y"), lax.axis_index("x"), lax.axis_index("c")
    return y, x, c, {"y": {"y": 1 - y}, "x": {"x": 1 - x}, "c": {"c": 1 - c}}


def gather_steps(s_ref, out_ref, local_sem, send, recv, split=True):
    y, x, c, device = place()
    remote = remote_copies(send, recv, device)
    half = s_ref.shape[0] // 2
    low, high = pl.ds(0, half), pl.ds(half, half)
    mine = out_ref.at[y, x, c]
    from_x = out_ref.at[y, 1 - x, c]
    from_y = out_ref.at[1 - y, x, c]
    diagonal = out_ref.at[1 - y, 1 - x, c]
    x_low = remote(0, s_ref.at[low], mine.at[low], "x")
    y_high = remote(1, s_ref.at[high], mine.at[high], "y")
    x_high = remote(2, s_ref.at[high], mine.at[high], "x")
    y_low = remote(3, s_ref.at[low], mine.at[low], "y")
    c_own = remote(4, s_ref, mine, "c")
    local = pltpu.make_async_copy(s_ref, mine, local_sem)
    forward_y = remote(5, from_x.at[low], from_x.at[low], "y")
    over_x = from_y.at[high] if split else from_y
    forward_x = remote(6, over_x, over_x, "x")
    c_x = remote(7, from_x, from_x, "c")
    c_y = remote(8, from_y, from_y, "c")
    c_low = remote(9, diagonal.at[low], diagonal.at[low], "c")
    over_c = diagonal.at[high] if split else diagonal
    c_high = remote(10, over_c, over_c, "c")

    def begin():
        for copy in (x_low, y_high, x_high, y_low, c_own, local):
            copy.start()

    def forward():
        x_low.wait_recv()
        if split:
            forward_y.start()
        y_high.wait_recv()
        if split:
            forward_x.start()

    def across():
        if not split:
            y_low.wait_recv()
            forward_x.start()
        x_high.wait_recv()
        c_x.start()
        if split:
            y_low.wait_recv()
        c_y.start()

    def finish():
        if split:
            forward_y.wait_recv()
            c_low.start()
        forward_x.wait_recv()
        c_high.start()
        for copy in (c_own, c_x, c_y, *((c_low,) if split else ()), c_high):
            copy.wait()
        for copy in (x_low, y_high, x_high, y_low, *((forward_y,) if split else ()), forward_x):
            copy.wait_send()
        local.wait()

    return begin, forward, across, finish


GATHER_SEMAPHORES = (
    pltpu.SemaphoreType.DMA,
    pltpu.SemaphoreType.DMA((11,)),
    pltpu.SemaphoreType.DMA((11,)),
)


def swap_steps(pieces, sources, outs, local_sem, send, recv, wanted=None):
    y, _, _, device = place()
    remote = remote_copies(send, recv, device)
    copies, locals_ = [], []
    for i, (source, out, first, count, at) in enumerate(pieces):
        if wanted is not None and not wanted(out):
            continue
        rows, cols = sources[source].shape
        target = outs[out].at[pl.ds(pl.multiple_of(y * rows, rows), rows), pl.ds(at, count)]

        def half(which):
            start = pl.multiple_of(which * (cols // 2) + first, 128)
            return sources[source].at[:, pl.ds(start, count)]

        copies.append(remote(i, half(1 - y), target, "y"))
        locals_.append(pltpu.make_async_copy(half(y), target, local_sem.at[i]))

    def begin():
        for copy in (*copies, *locals_):
            copy.start()

    def finish():
        for copy in (*copies, *locals_):
            copy.wait()

    return begin, finish


def swap_plan(groups):
    weights, pieces, widths = [], [], []
    for group in groups:
        width = 0
        for weight, first, count in group:
            index = next((i for i, w in enumerate(weights) if w is weight), len(weights))
            if index == len(weights):
                weights.append(weight)
            pieces.append((index, len(widths), first, count, width))
            width += count
        widths.append(width)
    rows = 2 * weights[0].shape[0]
    shapes = tuple(jax.ShapeDtypeStruct((rows, width), BF16) for width in widths)
    count = len(pieces)
    semaphores = [pltpu.SemaphoreType.DMA((count,))] * 3
    return weights, pieces, shapes, semaphores


def swap_kernel(pieces, count, *refs):
    begin, finish = swap_steps(pieces, refs[:count], refs[count:-3], *refs[-3:])
    greet((place()[3]["y"],))
    begin()
    finish()


def swap_weights(*groups):
    weights, pieces, shapes, semaphores = swap_plan(groups)
    return pl.pallas_call(
        functools.partial(swap_kernel, pieces, len(weights)),
        out_shape=shapes,
        in_specs=[pl.BlockSpec(memory_space=pltpu.VMEM)] * len(weights),
        out_specs=(pl.BlockSpec(memory_space=pl.ANY),) * len(shapes),
        scratch_shapes=semaphores,
        compiler_params=pltpu.CompilerParams(collective_id=4, has_side_effects=True),
        cost_estimate=micros(15),
        name="swap_weights",
    )(*weights)


def gather_kernel(split, *refs):
    source, out, *sems = refs
    begin, forward, across, finish = gather_steps(source, out, *sems, split)
    greet(tuple(place()[3].values()))
    begin()
    forward()
    across()
    finish()


def gather_tokens(shard):
    rows, width = shard.shape
    return pl.pallas_call(
        functools.partial(gather_kernel, True),
        out_shape=jax.ShapeDtypeStruct((2, 2, 2, rows, width), shard.dtype),
        in_specs=[pl.BlockSpec(memory_space=pltpu.VMEM)],
        out_specs=pl.BlockSpec(memory_space=pl.ANY),
        scratch_shapes=list(GATHER_SEMAPHORES),
        compiler_params=pltpu.CompilerParams(collective_id=1, has_side_effects=True),
        cost_estimate=micros(42),
        name="gather_tokens",
    )(shard).reshape(8 * rows, width)


def line_steps(rows_ref, out_ref, local_sem, send, recv):
    z = lax.axis_index("z")
    rows = rows_ref.shape[0]
    pair, middle = z + 1 - 2 * lax.rem(z, 2), 3 - z
    inner = (z == 1) | (z == 2)

    def at(index):
        return out_ref.at[pl.ds(pl.multiple_of(index * rows, rows), rows)]

    def remote(index, source, target, peer):
        return pltpu.make_async_remote_copy(
            src_ref=source,
            dst_ref=target,
            send_sem=send.at[index],
            recv_sem=recv.at[index],
            device_id={"z": peer},
            device_id_type=MESH,
        )

    far = middle + 1 - 2 * lax.rem(middle, 2)
    own_pair = remote(0, rows_ref, at(z), pair)
    own_middle = remote(1, rows_ref, at(z), middle)
    pair_middle = remote(2, at(pair), at(pair), middle)
    middle_pair = remote(3, at(middle), at(middle), pair)
    far_pair = remote(4, at(far), at(far), pair)
    local = pltpu.make_async_copy(rows_ref, at(z), local_sem)

    def begin():
        local.start()
        own_pair.start()
        pl.when(inner)(own_middle.start)

    def second():
        own_pair.wait_recv()

        @pl.when(inner)
        def _():
            pair_middle.start()
            own_middle.wait_recv()
            middle_pair.start()

    def third():
        @pl.when(inner)
        def _():
            pair_middle.wait_recv()
            far_pair.start()

    def finish():
        @pl.when(inner)
        def _():
            for copy in (own_middle, pair_middle, middle_pair, far_pair):
                copy.wait_send()

        @pl.when(jnp.logical_not(inner))
        def _():
            middle_pair.wait_recv()
            far_pair.wait_recv()

        own_pair.wait_send()
        local.wait()

    def peers():
        return pair, middle, inner

    return begin, second, third, finish, peers


def greet_line(others, pair, middle, inner):
    barrier = pltpu.get_barrier_semaphore()
    for other in (*others, {"z": pair}):
        pl.semaphore_signal(barrier, inc=1, device_id=other, device_id_type=MESH)

    @pl.when(inner)
    def _():
        pl.semaphore_signal(barrier, inc=1, device_id={"z": middle}, device_id_type=MESH)

    count = len(others) + 1
    pl.semaphore_wait(barrier, jnp.where(inner, count + 1, count))


def gather_swap_kernel(pieces, count, source, *refs):
    out, line_out, outs, scratch = refs[count], refs[count + 1], refs[count + 2 : -10], refs[-10:]
    line, sems = scratch[0], scratch[1:]
    begin, forward, across, finish = gather_steps(source, out, *sems[:3], False)
    line_begin, line_second, line_third, line_finish, peers = line_steps(line, line_out, *sems[3:6])
    targets = (line, *outs)
    early, early_done = swap_steps(pieces, refs[:count], targets, *sems[6:], lambda out: out == 0)
    swap, swapped = swap_steps(pieces, refs[:count], targets, *sems[6:], lambda out: out > 0)
    greet_line(tuple(place()[3].values()), *peers())
    early()
    begin()
    early_done()
    line_begin()
    line_second()
    forward()
    across()
    swap()
    line_third()
    finish()
    line_finish()
    swapped()


def gather_and_swap(shard, *groups):
    rows, width = shard.shape
    weights, pieces, shapes, semaphores = swap_plan(groups)
    line, shapes = shapes[0], shapes[1:]
    whole = jax.ShapeDtypeStruct((4 * line.shape[0], line.shape[1]), line.dtype)
    gathered, lined, *swapped = pl.pallas_call(
        functools.partial(gather_swap_kernel, pieces, len(weights)),
        out_shape=(jax.ShapeDtypeStruct((2, 2, 2, rows, width), shard.dtype), whole, *shapes),
        in_specs=[pl.BlockSpec(memory_space=pltpu.VMEM)] * (1 + len(weights)),
        out_specs=(pl.BlockSpec(memory_space=pl.ANY),) * (2 + len(shapes)),
        scratch_shapes=[
            pltpu.VMEM(line.shape, line.dtype),
            *GATHER_SEMAPHORES,
            pltpu.SemaphoreType.DMA,
            pltpu.SemaphoreType.DMA((5,)),
            pltpu.SemaphoreType.DMA((5,)),
            *semaphores,
        ],
        compiler_params=pltpu.CompilerParams(collective_id=2, has_side_effects=True),
        cost_estimate=micros(65),
        name="gather_and_swap",
    )(shard, *weights)
    return gathered.reshape(8 * rows, width), lined, swapped


def scatter_steps(windows, lefts, rights, out_ref, left_vmem, right_vmem, own, away, got, x_diag, y_diag, x_got, y_got, load_sem, send, recv):
    y, x, c, device = place()
    remote = remote_copies(send, recv, device)
    rows, width = own.shape[1:]
    half, both = rows // 2, 2 * rows
    low, high = pl.ds(0, half), pl.ds(half, half)
    targets = ((1 - y, 1 - x), (1 - y, x), (y, 1 - x), (y, x))
    starts = [pl.multiple_of((a * 2 + b) * both, both) for a, b in targets]
    count = len(lefts)
    right_loads = [
        pltpu.make_async_copy(
            rights[j].at[:, pl.ds(windows[j], right_vmem[j].shape[1])], right_vmem[j], load_sem.at[j]
        )
        for j in range(count)
    ]
    left_loads = [
        [
            pltpu.make_async_copy(
                lefts[j].at[pl.ds(start, both)], left_vmem[j].at[i], load_sem.at[count * (i + 1) + j]
            )
            for j in range(count)
        ]
        for i, start in enumerate(starts)
    ]
    crossing = [remote(i, away.at[i], got.at[i], "c") for i in range(4)]
    diag_x = remote(4, own.at[0, low], x_diag, "x")
    diag_y = remote(5, own.at[0, high], y_diag, "y")
    y_high = remote(6, own.at[1, high], y_got.at[high], "y")
    x_low = remote(7, own.at[2, low], x_got.at[low], "x")
    y_low = remote(8, own.at[1, low], y_got.at[low], "y")
    x_high = remote(9, own.at[2, high], x_got.at[high], "x")
    step, tile = 64, 512

    def add_into(target, start, size, other, base):
        @pl.loop(0, size // step)
        def _(i):
            at, there = pl.ds(start + i * step, step), pl.ds(base + i * step, step)
            target[at] = (target[at].astype(F32) + other[there].astype(F32)).astype(target.dtype)

    mine, others = pl.ds(c * rows, rows), pl.ds((1 - c) * rows, rows)

    def product(i):
        for load in left_loads[i]:
            load.wait()

        @pl.loop(0, width // tile)
        def _(n):
            cols = pl.ds(pl.multiple_of(n * tile, tile), tile)
            for part, target in ((others, away), (mine, own)):
                total = dot_nt(left_vmem[0][i, part], right_vmem[0][cols])
                for j in range(1, count):
                    total = total + dot_nt(left_vmem[j][i, part], right_vmem[j][cols])
                target[i, :, cols] = total.astype(target.dtype)

        crossing[i].start()

    def cores(i):
        crossing[i].wait_recv()
        add_into(own.at[i], 0, rows, got.at[i], 0)

    def load():
        for copy in right_loads:
            copy.start()
        for copies in left_loads:
            for copy in copies:
                copy.start()

    def first_a():
        for copy in right_loads:
            copy.wait()
        product(0)
        product(1)

    def first_b():
        cores(0)
        diag_x.start()
        diag_y.start()
        product(2)
        cores(1)
        y_high.start()

    def first_c():
        product(3)
        cores(2)
        x_low.start()

    def first():
        first_a()
        first_b()
        first_c()

    first.parts = (first_a, first_b, first_c)

    def second():
        diag_x.wait_recv()
        add_into(own.at[1], 0, half, x_diag, 0)
        y_low.start()
        diag_y.wait_recv()
        add_into(own.at[2], half, half, y_diag, 0)
        x_high.start()
        cores(3)

    def finish():
        for copy in (y_high, x_low, y_low, x_high):
            copy.wait_recv()

        @pl.loop(0, rows // step)
        def _(i):
            at = pl.ds(i * step, step)
            out_ref[at] = own[3, at].astype(F32) + x_got[at].astype(F32) + y_got[at].astype(F32)

        for copy in (*crossing, diag_x, diag_y, y_high, x_low, y_low, x_high):
            copy.wait_send()

    return load, first, second, finish


def scatter_scratch(group):
    lefts, rights = [item[0] for item in group], [item[1] for item in group]
    rows, width = lefts[0].shape[0] // 8, rights[0].shape[0]
    scratch = [
        *[pltpu.VMEM((4, 2 * rows, left.shape[1]), BF16) for left in lefts],
        *[pltpu.VMEM((width, left.shape[1]), BF16) for left in lefts],
        pltpu.VMEM((4, rows, width), BF16),
        pltpu.VMEM((4, rows, width), BF16),
        pltpu.VMEM((4, rows, width), BF16),
        pltpu.VMEM((rows // 2, width), BF16),
        pltpu.VMEM((rows // 2, width), BF16),
        pltpu.VMEM((rows, width), BF16),
        pltpu.VMEM((rows, width), BF16),
        pltpu.SemaphoreType.DMA((5 * len(group),)),
        pltpu.SemaphoreType.DMA((10,)),
        pltpu.SemaphoreType.DMA((10,)),
    ]
    return lefts + rights, scratch, jax.ShapeDtypeStruct((rows, width), F32)


def scatter_kernel(windows, *refs):
    count = len(windows)
    lefts, rights, out_ref, scratch = refs[:count], refs[count : 2 * count], refs[2 * count], refs[2 * count + 1 :]
    load, first, second, finish = scatter_steps(
        windows, lefts, rights, out_ref, scratch[:count], scratch[count : 2 * count], *scratch[2 * count :]
    )
    load()
    greet(tuple(place()[3].values()))
    first()
    second()
    finish()


def scatter_products(*group):
    operands, scratch, total = scatter_scratch(group)
    return pl.pallas_call(
        functools.partial(scatter_kernel, [item[2] for item in group]),
        out_shape=total,
        in_specs=[pl.BlockSpec(memory_space=pl.ANY)] * len(operands),
        out_specs=pl.BlockSpec(memory_space=pltpu.VMEM),
        scratch_shapes=scratch,
        compiler_params=pltpu.CompilerParams(
            collective_id=10 + sum(item[0].shape[1] for item in group) // 256, has_side_effects=True
        ),
        cost_estimate=micros(48),
        name="scatter_products",
    )(*operands)


def line_scatter_steps(grad_ref, own, from_edge, from_middle, inward, load_sem, send, recv):
    z = lax.axis_index("z")
    rows = own.shape[1]
    pair, middle = z + 1 - 2 * lax.rem(z, 2), 3 - z
    inner = (z == 1) | (z == 2)
    edge = jnp.logical_not(inner)
    far = middle + 1 - 2 * lax.rem(middle, 2)

    def block(index):
        return grad_ref.at[pl.ds(pl.multiple_of(index * rows, rows), rows)]

    def remote(index, source, target, peer):
        return pltpu.make_async_remote_copy(
            src_ref=source,
            dst_ref=target,
            send_sem=send.at[index],
            recv_sem=recv.at[index],
            device_id={"z": peer},
            device_id_type=MESH,
        )

    indices = (far, middle, pair, z)
    loads = [
        pltpu.make_async_copy(block(index), own.at[i], load_sem.at[i])
        for i, index in enumerate(indices)
    ]
    edge_far = remote(0, own.at[1], from_edge.at[0], pair)
    edge_near = remote(1, own.at[0], from_edge.at[1], pair)
    edge_pair = remote(2, own.at[2], from_edge.at[2], pair)
    inner_far = remote(3, own.at[0], from_middle.at[0], middle)
    inner_near = remote(4, own.at[1], from_middle.at[1], middle)
    outward = remote(5, own.at[2], inward, pair)
    step = 128

    def add_into(target, other):
        @pl.loop(0, rows // step)
        def _(i):
            at = pl.ds(i * step, step)
            target[at] = (target[at].astype(F32) + other[at].astype(F32)).astype(target.dtype)

    def load():
        for copy in loads:
            copy.start()

    def begin():
        for copy in loads:
            copy.wait()

        @pl.when(edge)
        def _():
            for copy in (edge_far, edge_near, edge_pair):
                copy.start()

    def second():
        @pl.when(inner)
        def _():
            edge_far.wait_recv()
            add_into(own.at[0], from_edge.at[0])
            inner_far.start()

    def third():
        @pl.when(inner)
        def _():
            edge_near.wait_recv()
            add_into(own.at[1], from_edge.at[1])
            inner_near.start()
            inner_far.wait_recv()
            add_into(own.at[2], from_middle.at[0])
            outward.start()

    def finish():
        @pl.when(inner)
        def _():
            edge_pair.wait_recv()
            add_into(own.at[3], from_edge.at[2])
            inner_near.wait_recv()
            add_into(own.at[3], from_middle.at[1])
            for copy in (inner_far, inner_near, outward):
                copy.wait_send()

        @pl.when(edge)
        def _():
            outward.wait_recv()
            add_into(own.at[3], inward)
            for copy in (edge_far, edge_near, edge_pair):
                copy.wait_send()

    return load, begin, second, third, finish, (pair, middle, inner)


def total_steps(near, far, near_send, near_recv, far_send, far_recv):
    z, y, x, c = (lax.axis_index(name) for name in "zyxc")
    here = (y * 2 + x) * 2 + c
    others = [
        {"y": lax.rem(y + i // 4, 2), "x": lax.rem(x + i // 2 % 2, 2), "c": lax.rem(c + i % 2, 2)}
        for i in range(1, 8)
    ]
    levels = [{"z": lax.rem(z + i, 4)} for i in range(1, 4)]

    def remote(index, source, target, send, recv, device):
        return pltpu.make_async_remote_copy(
            src_ref=source,
            dst_ref=target,
            send_sem=send.at[index],
            recv_sem=recv.at[index],
            device_id=device,
            device_id_type=MESH,
        )

    around = [
        remote(i, near.at[here], near.at[here], near_send, near_recv, other)
        for i, other in enumerate(others)
    ]
    along = [
        remote(i, far.at[z], far.at[z], far_send, far_recv, level) for i, level in enumerate(levels)
    ]

    def begin():
        for copy in around:
            copy.start()

    def second():
        for copy in around:
            copy.wait()
        total = near[0]
        for i in range(1, 8):
            total = total + near[i]
        far[z] = total
        for copy in along:
            copy.start()

    def finish():
        for copy in along:
            copy.wait()
        total = far[0]
        for i in range(1, 4):
            total = total + far[i]
        return total

    return begin, second, finish, here, others, levels


def tail_kernel(windows, *refs):
    count = len(windows)
    lefts, rights, refs = refs[:count], refs[count : 2 * count], refs[2 * count :]
    grad_ref, tokens_ref, inverse_ref, *refs = refs
    gains, (out_ref, mine_ref, theirs_ref, total_ref), scratch = refs[:3], refs[3:7], refs[7:]
    size = 2 * count + 10
    load, first, second, finish = scatter_steps(
        windows, lefts, rights, out_ref, scratch[:count], scratch[count : 2 * count], *scratch[2 * count : size]
    )
    line, (swap_sem,), total = scratch[size : size + 7], scratch[size + 7 : size + 8], scratch[size + 8 :]
    line_load, line_begin, line_second, line_third, line_finish, peers = line_scatter_steps(grad_ref, *line)
    near, far = total[:2]
    total_begin, total_second, total_finish, here, others, levels = total_steps(*total)
    y = lax.axis_index("y")
    load()
    line_load()
    width = out_ref.shape[1]
    near[here, :, pl.ds(width, width)] = gains[0][...]
    head = gains[1].shape[1]
    near[here, :, pl.ds(2 * width, head)] = gains[1][...]
    near[here, :, pl.ds(2 * width + head, head)] = gains[2][...]
    greet(others + levels)
    line_begin()
    first()
    line_second()
    second()
    line_third()
    finish()
    rows, step = out_ref.shape[0], 32

    def gain_part(i, part):
        at = pl.ds(i * step, step)
        return part + jnp.sum(
            out_ref[at] * tokens_ref[at].astype(F32) * inverse_ref[at], 0, keepdims=True
        )

    near[here, :, pl.ds(0, width)] = lax.fori_loop(
        0, rows // step, gain_part, jnp.zeros((1, width), F32)
    )
    total_begin()
    line_finish()
    summed = line[0].at[3]
    half = theirs_ref.shape[0]
    swap = pltpu.make_async_remote_copy(
        src_ref=summed.at[pl.ds(pl.multiple_of((1 - y) * half, half), half)],
        dst_ref=theirs_ref,
        send_sem=swap_sem.at[0],
        recv_sem=swap_sem.at[1],
        device_id={"y": 1 - y},
        device_id_type=MESH,
    )
    swap.start()
    total_second()
    mine_ref[...] = summed[pl.ds(pl.multiple_of(y * half, half), half)]
    total_ref[...] = total_finish()
    swap.wait()


def tail(group, grad, tokens, inverse, gains):
    operands, scratch, total = scatter_scratch(group)
    rows, cols = grad.shape[0] // 4, grad.shape[1]
    length = 2 * total.shape[1] + 2 * gains[1].size
    half = jax.ShapeDtypeStruct((rows // 2, cols), BF16)
    whole = pl.BlockSpec(memory_space=pltpu.VMEM)
    block = lambda count: pltpu.VMEM((count, rows, cols), BF16)
    dma = pltpu.SemaphoreType.DMA
    return pl.pallas_call(
        functools.partial(tail_kernel, [item[2] for item in group]),
        out_shape=(total, half, half, jax.ShapeDtypeStruct((1, length), F32)),
        in_specs=[pl.BlockSpec(memory_space=pl.ANY)] * (len(operands) + 1) + [whole] * 5,
        out_specs=(whole,) * 4,
        scratch_shapes=[
            *scratch,
            block(4), block(3), block(2), pltpu.VMEM((rows, cols), BF16), dma((4,)), dma((6,)), dma((6,)),
            dma((2,)),
            pltpu.VMEM((8, 1, length), F32), pltpu.VMEM((4, 1, length), F32), dma((7,)), dma((7,)), dma((3,)), dma((3,)),
        ],
        compiler_params=pltpu.CompilerParams(
            collective_id=0, has_side_effects=True, vmem_limit_bytes=VMEM_BYTES
        ),
        cost_estimate=micros(52),
        name="tail",
    )(*operands, grad, tokens, inverse, *(gain.reshape(1, -1) for gain in gains))


def swap_y(value):
    return lax.ppermute(value, "y", [(0, 1), (1, 0)])


def in_y_order(mine, theirs, axis):
    count = mine.shape[axis]
    return lax.dynamic_slice_in_dim(
        jnp.concatenate([mine, theirs, mine], axis), lax.axis_index("y") * count, 2 * count, axis
    )


def gather_rows(rows):
    return lax.all_gather(rows, "z", axis=0, tiled=True)


def scatter_grads(grad):
    return lax.psum_scatter(grad.astype(BF16), "z", scatter_dimension=0, tiled=True)


def their_rows(part):
    half = part.shape[0] // 2
    return swap_y(
        lax.dynamic_slice_in_dim(part, (1 - lax.axis_index("y")) * half, half, 0)
    )


def join_pieces(plan, y, mine_of, theirs_of, outs):
    for source, first, width, out, at, turned in plan:
        half = outs[out].shape[0 if turned else 1] // 2
        cols = pl.ds(first, width)
        for which, piece in ((y, mine_of(source, cols)), (1 - y, theirs_of(source, cols))):
            target = pl.ds(pl.multiple_of(which * half + at, 128), width)
            if turned:
                outs[out][target, :] = piece.astype(F32).T
            else:
                outs[out][:, target] = piece.astype(F32)


def join_kernel(plan, count, y_rows, *refs):
    y = lax.axis_index("y")
    parts, theirs, outs = refs[:count], refs[count : 2 * count], refs[2 * count :]
    mine = pl.ds(pl.multiple_of(y * y_rows, y_rows), y_rows)
    own = lambda source, cols: parts[source][mine, cols]
    got = lambda source, cols: theirs[source][:, cols]
    join_pieces(plan, y, own, got, outs)


def join_grads(parts, theirs, plan, shapes):
    whole = pl.BlockSpec(memory_space=pltpu.VMEM)
    return pl.pallas_call(
        functools.partial(join_kernel, plan, len(parts), theirs[0].shape[0]),
        out_shape=tuple(jax.ShapeDtypeStruct(shape, F32) for shape in shapes),
        in_specs=[whole] * (2 * len(parts)),
        out_specs=(whole,) * len(shapes),
        compiler_params=pltpu.CompilerParams(vmem_limit_bytes=VMEM_BYTES),
        cost_estimate=micros(5),
        name="join_grads",
    )(*parts, *theirs)


def last_join_kernel(plan, mine, theirs, total, *outs):
    gains, grads, start = outs[:4], outs[4:], 0
    for gain in gains:
        gain[...] = total[:, pl.ds(start, gain.shape[1])]
        start += gain.shape[1]
    y = lax.axis_index("y")
    join_pieces(plan, y, lambda _, cols: mine[:, cols], lambda _, cols: theirs[:, cols], grads)


def join_last(mine, theirs, total, plan, sizes, shapes):
    whole = pl.BlockSpec(memory_space=pltpu.VMEM)
    outs = (*((1, size) for size in sizes), *shapes)
    return pl.pallas_call(
        functools.partial(last_join_kernel, plan),
        out_shape=tuple(jax.ShapeDtypeStruct(shape, F32) for shape in outs),
        in_specs=[whole] * 3,
        out_specs=(whole,) * len(outs),
        cost_estimate=micros(4),
        name="join_last",
    )(mine, theirs, total)


def normed_rope(raw, gain, cosine, sine):
    inverse = lax.rsqrt(jnp.mean(raw * raw, -1, keepdims=True) + EPSILON)
    scaled = raw * inverse * gain
    turned = pltpu.roll(scaled, scaled.shape[-1] // 2, 1)
    return (scaled * cosine + turned * sine).astype(BF16)


def normed_rope_back(grad, raw, gain, cosine, sine):
    inverse = lax.rsqrt(jnp.mean(raw * raw, -1, keepdims=True) + EPSILON)
    straight = grad * cosine - pltpu.roll(grad, grad.shape[-1] // 2, 1) * sine
    gain_part = jnp.sum(straight * (raw * inverse), 0, keepdims=True)
    return norm_back(straight, raw, inverse, gain).astype(BF16), gain_part


def causal_scores(query, keys, first, scaling):
    scores = dot_nt(query, keys) * scaling
    rows = lax.broadcasted_iota(jnp.int32, scores.shape, 0) + first
    columns = lax.broadcasted_iota(jnp.int32, scores.shape, 1)
    return jnp.where(rows >= columns, scores, -1e30)


def attend_kernel(
    heads, head, block, normed_ref, w_ref, wg_ref, low_ref, qg_ref, kg_ref, cos_ref, sin_ref,
    raw_ref, out_ref, log_ref, gate_ref, mixed_ref, all_ref, key_ref, value_ref, *sems,
):
    seq, step, steps = pl.program_id(0), pl.program_id(1), pl.num_programs(1)
    tick = seq * steps + step
    scaling = head**-0.5
    at = heads * head
    begin, forward, across, finish = gather_steps(low_ref, all_ref, *sems)

    @pl.when(tick == 0)
    def _():
        greet(tuple(place()[3].values()))
        begin()

    pl.when(tick == 3)(forward)
    pl.when(tick == 6)(across)
    raw_ref[...] = dot_nn(normed_ref[...], w_ref[...])
    here = pl.ds(pl.multiple_of(step * block, block), block)
    cosine, sine = cos_ref[here], sin_ref[here]
    key_ref[here] = normed_rope(raw_ref[:, at : at + head], kg_ref[...], cosine, sine)
    value_ref[here] = raw_ref[:, at + head :].astype(BF16)

    for i in range(key_ref.shape[0] // block):

        @pl.when(step == i)
        def _():
            seen = pl.ds(0, (i + 1) * block)

            @pl.loop(0, heads)
            def _(h):
                cols = pl.ds(pl.multiple_of(h * head, head), head)
                query = normed_rope(raw_ref[:, cols], qg_ref[...], cosine, sine)
                scores = causal_scores(query, key_ref[seen], i * block, scaling)
                highest = jnp.max(scores, -1, keepdims=True)
                exp_vals = jnp.exp(scores - highest)
                total = jnp.sum(exp_vals, -1, keepdims=True)
                probs = (exp_vals / total).astype(BF16)
                out_ref[:, cols] = dot_nn(probs, value_ref[seen])
                log_ref[h] = highest + jnp.log(total)

    gate = jax.nn.sigmoid(dot_nn(normed_ref[...], wg_ref[...]))
    gate_ref[...] = gate
    mixed_ref[...] = (out_ref[...] * gate).astype(BF16)
    pl.when(tick == pl.num_programs(0) * steps - 1)(finish)


def attend(normed, weights, gates, low, query_gain, key_gain, cosine, sine, heads, head, length, block=256):
    rows, width = normed.shape
    cols = weights.shape[1]
    seqs, steps = rows // length, length // block
    whole = lambda shape: pl.BlockSpec(
        shape, lambda s, i: (0,) * len(shape), pipeline_mode=pl.Buffered(1)
    )
    part = lambda cols: pl.BlockSpec((block, cols), lambda s, i: (s * steps + i, 0))
    *outs, gathered = pl.pallas_call(
        functools.partial(attend_kernel, heads, head, block),
        out_shape=(
            jax.ShapeDtypeStruct((rows, cols), F32),
            jax.ShapeDtypeStruct((rows, heads * head), F32),
            jax.ShapeDtypeStruct((heads, rows, 1), F32),
            jax.ShapeDtypeStruct((rows, heads * head), F32),
            jax.ShapeDtypeStruct((rows, heads * head), BF16),
            jax.ShapeDtypeStruct((2, 2, 2, *low.shape), low.dtype),
        ),
        grid=(seqs, steps),
        in_specs=[
            part(width),
            whole((width, cols)),
            whole((width, heads * head)),
            pl.BlockSpec(memory_space=pl.ANY),
            whole((1, head)),
            whole((1, head)),
            whole((length, head)),
            whole((length, head)),
        ],
        out_specs=(
            part(cols),
            part(heads * head),
            pl.BlockSpec((heads, block, 1), lambda s, i: (0, s * steps + i, 0)),
            part(heads * head),
            part(heads * head),
            pl.BlockSpec(memory_space=pl.ANY),
        ),
        scratch_shapes=[
            pltpu.VMEM((length, head), BF16),
            pltpu.VMEM((length, head), BF16),
            *GATHER_SEMAPHORES,
        ],
        compiler_params=pltpu.CompilerParams(collective_id=3, has_side_effects=True),
        cost_estimate=micros(42),
        name="attend",
    )(normed, weights, gates, low, query_gain, key_gain, cosine, sine)
    return *outs, gathered.reshape(rows, width)


def add_products(step, total_ref, start, left_ref, right, tile=1024):
    cols = slice(start, start + right.shape[1])

    @pl.loop(0, left_ref.shape[1] // tile)
    def _(m):
        at = pl.ds(pl.multiple_of(m * tile, tile), tile)
        part = dot_tn(left_ref[:, at], right)

        @pl.when(step == 0)
        def _():
            total_ref[at, cols] = part

        @pl.when(step > 0)
        def _():
            total_ref[at, cols] += part


def store_low(step, total_ref, out_ref, tile=256):
    @pl.when(step == pl.num_programs(0) - 1)
    def _():
        @pl.loop(0, total_ref.shape[0] // tile)
        def _(m):
            at = pl.ds(m * tile, tile)
            out_ref[at] = total_ref[at].astype(BF16)


def gate_back_kernel(
    normed_ref, branch_ref, w_ref, attended_ref, gate_ref, mixed_ref,
    dattended_ref, dgating_ref, grad_ref, total_ref,
):
    step = pl.program_id(0)
    dmixed = dot_nn(branch_ref[...], w_ref[...])
    gate = gate_ref[...]
    dattended_ref[...] = (dmixed * gate).astype(BF16)
    dgating = (dmixed * attended_ref[...] * gate * (1.0 - gate)).astype(BF16)
    dgating_ref[...] = dgating
    add_products(step, total_ref, 0, normed_ref, dgating)
    add_products(step, total_ref, dgating.shape[1], branch_ref, mixed_ref[...])
    store_low(step, total_ref, grad_ref)


def gate_back(normed, branch, weights, attended, gate, mixed, block=1024):
    rows, width = normed.shape
    cols = attended.shape[1]
    part = lambda cols: pl.BlockSpec((block, cols), lambda i: (i, 0))
    return pl.pallas_call(
        gate_back_kernel,
        out_shape=(
            jax.ShapeDtypeStruct((rows, cols), BF16),
            jax.ShapeDtypeStruct((rows, cols), BF16),
            jax.ShapeDtypeStruct((width, 2 * cols), BF16),
        ),
        grid=(rows // block,),
        in_specs=[
            part(width),
            part(width),
            pl.BlockSpec((width, cols), lambda i: (0, 1)),
            part(cols),
            part(cols),
            part(cols),
        ],
        out_specs=(part(cols), part(cols), pl.BlockSpec((width, 2 * cols), lambda i: (0, 0))),
        scratch_shapes=[pltpu.VMEM((width, 2 * cols), F32)],
        compiler_params=pltpu.CompilerParams(vmem_limit_bytes=VMEM_BYTES),
        cost_estimate=micros(25),
        name="gate_back",
    )(normed, branch, weights, attended, gate, mixed)


def feed_kernel(count, tile, mid_ref, low_ref, w_ref, act_ref, dgu_ref, grad_ref, total_ref):
    step = pl.program_id(0)

    @pl.loop(0, count // tile)
    def _(j):
        start = pl.multiple_of(j * tile, tile)
        at, after = pl.ds(start, tile), pl.ds(pl.multiple_of(count + start, tile), tile)
        last = pl.ds(pl.multiple_of(2 * count + start, tile), tile)
        gate = dot_nn(mid_ref[...], w_ref[:, at])
        up = dot_nn(mid_ref[...], w_ref[:, after])
        dact = dot_nn(low_ref[...], w_ref[:, last])
        sigma = jax.nn.sigmoid(gate)
        silu = gate * sigma
        act_ref[:, at] = (silu * up).astype(BF16)
        dgu_ref[:, at] = (dact * up * sigma * (1.0 + gate * (1.0 - sigma))).astype(BF16)
        dgu_ref[:, after] = (dact * silu).astype(BF16)

    add_products(step, total_ref, 0, mid_ref, dgu_ref[...])
    add_products(step, total_ref, 2 * count, low_ref, act_ref[...])
    store_low(step, total_ref, grad_ref)


def feed_forward(mid, low, weights, block=1024):
    rows, width = mid.shape
    count = weights.shape[1] // 3
    part = lambda cols: pl.BlockSpec((block, cols), lambda i: (i, 0))
    whole = pl.BlockSpec(weights.shape, lambda i: (0, 0), pipeline_mode=pl.Buffered(1))
    return pl.pallas_call(
        functools.partial(feed_kernel, count, 256),
        out_shape=(
            jax.ShapeDtypeStruct((rows, count), BF16),
            jax.ShapeDtypeStruct((rows, 2 * count), BF16),
            jax.ShapeDtypeStruct(weights.shape, BF16),
        ),
        grid=(rows // block,),
        in_specs=[part(width), part(width), whole],
        out_specs=(part(count), part(2 * count), whole),
        scratch_shapes=[pltpu.VMEM(weights.shape, F32)],
        compiler_params=pltpu.CompilerParams(vmem_limit_bytes=VMEM_BYTES),
        cost_estimate=micros(40),
        name="feed_forward",
    )(mid, low, weights)


def attend_back_kernel(
    heads, head, block, windows, raw_ref, up_ref, log_ref, qg_ref, kg_ref, cos_ref, sin_ref, *refs
):
    count = len(windows)
    lefts, rights, refs = refs[:count], refs[count : 2 * count], refs[2 * count :]
    out_ref, qg_out, kg_out, sum_ref, key_ref, value_ref, dkey_ref, dvalue_ref, *scratch = refs
    seq, step, steps = pl.program_id(0), pl.program_id(1), pl.num_programs(1)
    tick = seq * steps + step
    scaling = head**-0.5
    at = heads * head
    blocks = raw_ref.shape[0] // block
    load, first, second, finish = scatter_steps(
        windows, lefts, rights, sum_ref, scratch[:count], scratch[count : 2 * count], *scratch[2 * count :]
    )

    @pl.when(tick == 0)
    def _():
        load()
        greet(tuple(place()[3].values()))
        qg_out[...] = jnp.zeros_like(qg_out)
        kg_out[...] = jnp.zeros_like(kg_out)

    for i, part in enumerate(first.parts):
        pl.when(tick == i)(part)
    pl.when(tick == 5)(second)

    @pl.when(step == 0)
    def _():
        key_ref[...] = normed_rope(
            raw_ref[:, at : at + head], kg_ref[...], cos_ref[...], sin_ref[...]
        )
        value_ref[...] = raw_ref[:, at + head :].astype(BF16)
        dkey_ref[...] = jnp.zeros_like(dkey_ref)
        dvalue_ref[...] = jnp.zeros_like(dvalue_ref)

    for i in range(blocks):

        @pl.when(step == i)
        def _():
            rows, seen = pl.ds(i * block, block), pl.ds(0, (i + 1) * block)

            @pl.loop(0, heads)
            def _(h):
                cols = pl.ds(pl.multiple_of(h * head, head), head)
                raw = raw_ref[rows, cols]
                query = normed_rope(raw, qg_ref[...], cos_ref[rows], sin_ref[rows])
                scores = causal_scores(query, key_ref[seen], i * block, scaling)
                probs = jnp.exp(scores - log_ref[h])
                upstream = up_ref[:, cols]
                dprobs = dot_nt(upstream, value_ref[seen])
                centre = jnp.sum(dprobs * probs, -1, keepdims=True)
                dscores = (probs * (dprobs - centre)).astype(BF16)
                dkey_ref[seen] += dot_tn(dscores, query)
                dvalue_ref[seen] += dot_tn(probs.astype(BF16), upstream)
                dquery = dot_nn(dscores, key_ref[seen]) * scaling
                grad, part = normed_rope_back(
                    dquery, raw, qg_ref[...], cos_ref[rows], sin_ref[rows]
                )
                out_ref[rows, cols] = grad
                qg_out[...] += part

    @pl.when(step == blocks - 1)
    def _():
        grad, part = normed_rope_back(
            dkey_ref[...] * scaling,
            raw_ref[:, at : at + head],
            kg_ref[...],
            cos_ref[...],
            sin_ref[...],
        )
        out_ref[:, at : at + head] = grad
        out_ref[:, at + head :] = dvalue_ref[...].astype(BF16)
        kg_out[...] += part

    pl.when(tick == pl.num_programs(0) * steps - 1)(finish)


def attend_back(
    raw, upstream, logs, query_gain, key_gain, cosine, sine, heads, head, length, group, block=256
):
    rows = raw.shape[0]
    operands, scratch, total = scatter_scratch(group)
    seqs, steps = rows // length, length // block
    whole = lambda shape: pl.BlockSpec(shape, lambda s, i: (0,) * len(shape))
    return pl.pallas_call(
        functools.partial(attend_back_kernel, heads, head, block, [item[2] for item in group]),
        out_shape=(
            jax.ShapeDtypeStruct(raw.shape, BF16),
            jax.ShapeDtypeStruct((1, head), F32),
            jax.ShapeDtypeStruct((1, head), F32),
            total,
        ),
        grid=(seqs, steps),
        in_specs=[
            pl.BlockSpec((length, raw.shape[1]), lambda s, i: (s, 0)),
            pl.BlockSpec((block, heads * head), lambda s, i: (s * steps + i, 0)),
            pl.BlockSpec((heads, block, 1), lambda s, i: (0, s * steps + i, 0)),
            whole((1, head)),
            whole((1, head)),
            whole((length, head)),
            whole((length, head)),
            *[pl.BlockSpec(memory_space=pl.ANY)] * len(operands),
        ],
        out_specs=(
            pl.BlockSpec((length, raw.shape[1]), lambda s, i: (s, 0)),
            whole((1, head)),
            whole((1, head)),
            whole(total.shape),
        ),
        scratch_shapes=[
            pltpu.VMEM((length, head), BF16),
            pltpu.VMEM((length, head), BF16),
            pltpu.VMEM((length, head), F32),
            pltpu.VMEM((length, head), F32),
            *scratch,
        ],
        compiler_params=pltpu.CompilerParams(
            collective_id=5, has_side_effects=True, vmem_limit_bytes=VMEM_BYTES
        ),
        cost_estimate=micros(48),
        name="attend_back",
    )(raw, upstream, logs, query_gain, key_gain, cosine, sine, *operands)


def attention_weights(query_proj, key_proj, value_proj, gating_proj, output_proj):
    return (
        lax.all_gather(query_proj, "dp", axis=0, tiled=True),
        lax.all_gather(key_proj, "dp", axis=0, tiled=True),
        lax.all_gather(value_proj, "dp", axis=0, tiled=True),
        lax.all_gather(gating_proj, "dp", axis=0, tiled=True),
        lax.all_gather(output_proj, "dp", axis=1, tiled=True),
    )


def swiglu_weights(swiglu_gate, swiglu_up, swiglu_down):
    return (
        lax.all_gather(swiglu_gate, "dp", axis=0, tiled=True),
        lax.all_gather(swiglu_up, "dp", axis=0, tiled=True),
        lax.all_gather(swiglu_down, "dp", axis=1, tiled=True),
    )


def softmax_forward_mapped(seq_items, causal):
    queries, keys_seq, values_seq = seq_items
    scaling = queries.shape[-1] ** (-0.5)
    scores = (
        jnp.einsum("qgjd,kgd->gjqk", queries, keys_seq, preferred_element_type=jnp.float32)
        * scaling
    )
    scores = jnp.where(causal, scores, -1e30)
    highest = jnp.max(scores, -1, keepdims=True)
    exp_vals = jnp.exp(scores - highest)
    row_totals = jnp.sum(exp_vals, -1, keepdims=True)
    attn_probs = (exp_vals / row_totals).astype(jnp.bfloat16)
    attended = jnp.einsum(
        "gjqk,kgd->qgjd", attn_probs, values_seq, preferred_element_type=jnp.float32
    )
    return (attended, highest[..., 0] + jnp.log(row_totals[..., 0]))


def softmax_backward_mapped(seq_items, causal):
    queries, keys_seq, values_seq, log_total, upstream = seq_items
    scaling = queries.shape[-1] ** (-0.5)
    scores = (
        jnp.einsum("qgjd,kgd->gjqk", queries, keys_seq, preferred_element_type=jnp.float32)
        * scaling
    )
    scores = jnp.where(causal, scores, -1e30)
    attn_probs = jnp.exp(scores - log_total[..., None])
    dprobs = jnp.einsum("qgjd,kgd->gjqk", upstream, values_seq, preferred_element_type=jnp.float32)
    centre = jnp.sum(dprobs * attn_probs, -1, keepdims=True)
    dscores = (attn_probs * (dprobs - centre)).astype(jnp.bfloat16)
    dqueries = (
        jnp.einsum("gjqk,kgd->qgjd", dscores, keys_seq, preferred_element_type=jnp.float32)
        * scaling
    )
    key_grads = (
        jnp.einsum("gjqk,qgjd->kgd", dscores, queries, preferred_element_type=jnp.float32) * scaling
    )
    value_grads = jnp.einsum(
        "gjqk,qgjd->kgd",
        attn_probs.astype(jnp.bfloat16),
        upstream,
        preferred_element_type=jnp.float32,
    )
    key_rows = key_grads.shape[0]
    return (dqueries, key_grads.reshape(key_rows, -1), value_grads.reshape(key_rows, -1))


def per_device_wide(
    tokens,
    cotangent,
    domain_ids,
    domain_counts,
    domain_numer,
    domain_denom,
    attention_gain,
    query_gain,
    key_gain,
    query_proj,
    key_proj,
    value_proj,
    gating_proj,
    output_proj,
    swiglu_gain,
    swiglu_gate,
    swiglu_up,
    swiglu_down,
):
    seq_count, local_len, model_width = tokens.shape
    full_len = local_len * lax.axis_size("ctx")
    local_rows = seq_count * local_len
    all_rows = seq_count * full_len
    head_dim = query_gain.shape[0]
    local_heads = query_proj.shape[1] // head_dim
    local_kv = key_proj.shape[1] // head_dim
    group_size = local_heads // local_kv
    positions = jnp.arange(full_len, dtype=jnp.int32)
    causal = positions[:, None] >= positions[None, :]
    cosine, sine = rope_tables(positions, head_dim)
    cos_rows = cosine[:, None, :]
    sin_rows = sine[:, None, :]
    inputs = tokens.reshape(local_rows, model_width).astype(jnp.float32)
    inverse_in = lax.rsqrt(jnp.mean(inputs * inputs, -1, keepdims=True) + EPSILON)
    gain_in = attention_gain.astype(jnp.float32)
    normed = (inputs * inverse_in * gain_in).astype(jnp.bfloat16)
    normed_all = lax.all_gather(
        normed.reshape(seq_count, local_len, model_width), "ctx", axis=1, tiled=True
    ).reshape(all_rows, model_width)
    attn_full = attention_weights(query_proj, key_proj, value_proj, gating_proj, output_proj)
    query_raw = dot_nn(normed_all, attn_full[0]).reshape(
        seq_count, full_len, local_heads, head_dim
    )
    key_raw = dot_nn(normed_all, attn_full[1]).reshape(seq_count, full_len, local_kv, head_dim)
    value_low = (
        dot_nn(normed_all, attn_full[2])
        .astype(jnp.bfloat16)
        .reshape(seq_count, full_len, local_kv, head_dim)
    )
    gate_pre = dot_nn(normed_all, attn_full[3])
    query_scale = query_gain.astype(jnp.float32)
    key_scale = key_gain.astype(jnp.float32)
    query_inv = lax.rsqrt(jnp.mean(query_raw * query_raw, -1, keepdims=True) + EPSILON)
    key_inv = lax.rsqrt(jnp.mean(key_raw * key_raw, -1, keepdims=True) + EPSILON)
    query_low = rotate(query_raw * query_inv * query_scale, cos_rows, sin_rows).astype(jnp.bfloat16)
    key_low = rotate(key_raw * key_inv * key_scale, cos_rows, sin_rows).astype(jnp.bfloat16)
    query_groups = query_low.reshape(seq_count, full_len, local_kv, group_size, head_dim)
    attended, log_total = lax.map(
        lambda seq_items: softmax_forward_mapped(seq_items, causal), (query_groups, key_low, value_low)
    )
    attended = attended.reshape(all_rows, local_heads * head_dim)
    gate_sig = jax.nn.sigmoid(gate_pre)
    mixed = (attended * gate_sig).astype(jnp.bfloat16)
    branch_part = dot_nn(mixed, attn_full[4]).reshape(seq_count, full_len, model_width)
    branch = lax.psum_scatter(branch_part, "ctx", scatter_dimension=1, tiled=True).reshape(
        local_rows, model_width
    )
    hidden = inputs + branch
    inverse_mid = lax.rsqrt(jnp.mean(hidden * hidden, -1, keepdims=True) + EPSILON)
    gain_mid = swiglu_gain.astype(jnp.float32)
    normed_mid = (hidden * inverse_mid * gain_mid).astype(jnp.bfloat16)
    normed_mid_all = lax.all_gather(
        normed_mid.reshape(seq_count, local_len, model_width), "ctx", axis=1, tiled=True
    ).reshape(all_rows, model_width)
    swiglu_full = swiglu_weights(swiglu_gate, swiglu_up, swiglu_down)
    gate_ff = dot_nn(normed_mid_all, swiglu_full[0])
    up_val = dot_nn(normed_mid_all, swiglu_full[1])
    gate_sigma = jax.nn.sigmoid(gate_ff)
    silu_val = gate_ff * gate_sigma
    activation = (silu_val * up_val).astype(jnp.bfloat16)
    down_part = dot_nn(activation, swiglu_full[2]).reshape(seq_count, full_len, model_width)
    ffn_branch = (
        lax.psum_scatter(down_part.astype(jnp.bfloat16), "ctx", scatter_dimension=1, tiled=True)
        .astype(jnp.float32)
        .reshape(local_rows, model_width)
    )
    layer_out = (hidden + ffn_branch).astype(jnp.bfloat16)
    domain_table = (
        domain_ids[:, None] == jnp.arange(domain_counts.shape[0], dtype=jnp.int32)[None, :]
    ).astype(jnp.float32)
    ratio = (
        domain_numer.astype(jnp.float32)
        / domain_denom.astype(jnp.float32)
        * LENGTH
        / domain_counts.astype(jnp.float32)
    )
    factor = jnp.sum(domain_table * ratio[None, :], 1)
    upstream = (cotangent.astype(jnp.float32) * factor[:, None, None]).reshape(
        local_rows, model_width
    )
    swiglu_back = swiglu_weights(swiglu_gate, swiglu_up, swiglu_down)
    out_low = upstream.astype(jnp.bfloat16)
    out_all = lax.all_gather(
        out_low.reshape(seq_count, local_len, model_width), "ctx", axis=1, tiled=True
    ).reshape(all_rows, model_width)
    dactivation = dot_nt(out_all, swiglu_back[2])
    dgate_low = (dactivation * up_val * gate_sigma * (1.0 + gate_ff * (1.0 - gate_sigma))).astype(
        jnp.bfloat16
    )
    dup_low = (dactivation * silu_val).astype(jnp.bfloat16)
    grad_down = dot_tn(activation, out_all)
    grad_gate = dot_tn(normed_mid_all, dgate_low)
    grad_up = dot_tn(normed_mid_all, dup_low)
    dmid_part = dot_nt(dgate_low, swiglu_back[0]) + dot_nt(dup_low, swiglu_back[1])
    dnormed_mid = lax.psum_scatter(
        dmid_part.reshape(seq_count, full_len, model_width), "ctx", scatter_dimension=1, tiled=True
    ).reshape(local_rows, model_width)
    grad_gain_mid = jnp.sum(dnormed_mid * hidden * inverse_mid, 0)
    dhidden = upstream + norm_back(dnormed_mid, hidden, inverse_mid, gain_mid)
    swiglu_grads = (
        lax.psum_scatter(
            grad_gate.astype(jnp.bfloat16), "dp", scatter_dimension=0, tiled=True
        ).astype(jnp.float32),
        lax.psum_scatter(
            grad_up.astype(jnp.bfloat16), "dp", scatter_dimension=0, tiled=True
        ).astype(jnp.float32),
        lax.psum_scatter(
            grad_down.astype(jnp.bfloat16), "dp", scatter_dimension=1, tiled=True
        ).astype(jnp.float32),
    )
    attn_back = attention_weights(query_proj, key_proj, value_proj, gating_proj, output_proj)
    dbranch_low = dhidden.astype(jnp.bfloat16)
    dbranch_all = lax.all_gather(
        dbranch_low.reshape(seq_count, local_len, model_width), "ctx", axis=1, tiled=True
    ).reshape(all_rows, model_width)
    grad_output = dot_tn(mixed, dbranch_all)
    dmixed = dot_nt(dbranch_all, attn_back[4])
    dattended_low = (dmixed * gate_sig).astype(jnp.bfloat16)
    dgating_low = (dmixed * attended * gate_sig * (1.0 - gate_sig)).astype(jnp.bfloat16)
    upstream_heads = dattended_low.reshape(seq_count, full_len, local_kv, group_size, head_dim)
    dquery_rot, dkey_rot, dvalue_sum = lax.map(
        lambda seq_items: softmax_backward_mapped(seq_items, causal),
        (query_groups, key_low, value_low, log_total, upstream_heads),
    )
    dvalue_low = dvalue_sum.reshape(all_rows, local_kv * head_dim).astype(jnp.bfloat16)
    dquery_normed = unrotate(
        dquery_rot.reshape(seq_count, full_len, local_heads, head_dim), cos_rows, sin_rows
    )
    dkey_normed = unrotate(
        dkey_rot.reshape(seq_count, full_len, local_kv, head_dim), cos_rows, sin_rows
    )
    grad_query_gain = jnp.sum(dquery_normed * query_raw * query_inv, (0, 1, 2))
    grad_key_gain = jnp.sum(dkey_normed * key_raw * key_inv, (0, 1, 2))
    dquery_low = (
        norm_back(dquery_normed, query_raw, query_inv, query_scale)
        .reshape(all_rows, -1)
        .astype(jnp.bfloat16)
    )
    dkey_low = (
        norm_back(dkey_normed, key_raw, key_inv, key_scale)
        .reshape(all_rows, -1)
        .astype(jnp.bfloat16)
    )
    dnormed_part = (
        dot_nt(dquery_low, attn_back[0])
        + dot_nt(dkey_low, attn_back[1])
        + dot_nt(dvalue_low, attn_back[2])
        + dot_nt(dgating_low, attn_back[3])
    )
    dnormed = (
        lax.psum_scatter(
            dnormed_part.reshape(seq_count, full_len, model_width).astype(jnp.bfloat16),
            "ctx",
            scatter_dimension=1,
            tiled=True,
        )
        .astype(jnp.float32)
        .reshape(local_rows, model_width)
    )
    grad_gain_in = jnp.sum(dnormed * inputs * inverse_in, 0)
    input_grad = (dhidden + norm_back(dnormed, inputs, inverse_in, gain_in)).astype(jnp.bfloat16)
    grad_query = dot_tn(normed_all, dquery_low)
    grad_key = dot_tn(normed_all, dkey_low)
    grad_value = dot_tn(normed_all, dvalue_low)
    grad_gating = dot_tn(normed_all, dgating_low)
    attention_grads = (
        lax.psum_scatter(
            grad_query.astype(jnp.bfloat16), "dp", scatter_dimension=0, tiled=True
        ).astype(jnp.float32),
        lax.psum_scatter(
            grad_key.astype(jnp.bfloat16), "dp", scatter_dimension=0, tiled=True
        ).astype(jnp.float32),
        lax.psum_scatter(
            grad_value.astype(jnp.bfloat16), "dp", scatter_dimension=0, tiled=True
        ).astype(jnp.float32),
        lax.psum_scatter(
            grad_gating.astype(jnp.bfloat16), "dp", scatter_dimension=0, tiled=True
        ).astype(jnp.float32),
        lax.psum_scatter(
            grad_output.astype(jnp.bfloat16), "dp", scatter_dimension=1, tiled=True
        ).astype(jnp.float32),
    )
    gain_grads = lax.psum(
        (grad_gain_in, grad_gain_mid, grad_query_gain, grad_key_gain), ("dp", "ctx")
    )
    return (
        layer_out.reshape(seq_count, local_len, model_width),
        input_grad.reshape(seq_count, local_len, model_width),
        gain_grads[0],
        gain_grads[2],
        gain_grads[3],
        attention_grads[0],
        attention_grads[1],
        attention_grads[2],
        attention_grads[3],
        attention_grads[4],
        gain_grads[1],
        swiglu_grads[0],
        swiglu_grads[1],
        swiglu_grads[2],
    )


def per_device(
    tokens,
    cotangent,
    domain_ids,
    domain_counts,
    domain_numer,
    domain_denom,
    attention_gain,
    query_gain,
    key_gain,
    query_proj,
    key_proj,
    value_proj,
    gating_proj,
    output_proj,
    swiglu_gain,
    swiglu_gate,
    swiglu_up,
    swiglu_down,
):
    seq_count, local_len, width = tokens.shape
    rows = seq_count * local_len
    full_len = local_len * lax.axis_size("x") * lax.axis_size("c")
    seqs = seq_count * lax.axis_size("y")
    head = query_gain.shape[0]
    kv_cols = key_proj.shape[1] // 2
    q_cols = query_proj.shape[1] // 2
    ff_cols = swiglu_gate.shape[1] // 2
    heads = q_cols // head
    cosine, sine = rope_tables(jnp.arange(full_len, dtype=jnp.int32), head)
    cos_rows = jnp.concatenate([cosine, cosine], 1)
    sin_rows = jnp.concatenate([-sine, sine], 1)

    inputs = tokens.reshape(rows, width).astype(F32)
    inverse_in = lax.rsqrt(jnp.mean(inputs * inputs, -1, keepdims=True) + EPSILON)
    gain_in = attention_gain.astype(F32)
    normed = (inputs * inverse_in * gain_in).astype(BF16)

    domain_table = (
        domain_ids[:, None] == jnp.arange(domain_counts.shape[0], dtype=jnp.int32)[None, :]
    ).astype(F32)
    ratio = (
        domain_numer.astype(F32) / domain_denom.astype(F32) * LENGTH / domain_counts.astype(F32)
    )
    factor = jnp.sum(domain_table * ratio[None, :], 1)
    upstream = (cotangent.astype(F32) * factor[:, None, None]).reshape(rows, width)
    out_low = upstream.astype(BF16)

    down_t, output_t = swiglu_down.T, output_proj.T
    split, rest = ff_cols * 2 // 3, ff_cols - ff_cols * 2 // 3
    (rows_go,) = swap_weights([(gating_proj, 0, q_cols), (output_t, 0, q_cols)])
    w_go = gather_rows(rows_go)
    feed = (swiglu_gate, swiglu_up, down_t)
    normed, out_low, cos_rows, sin_rows, rows_go = lax.optimization_barrier(
        (normed, out_low, cos_rows, sin_rows, rows_go)
    )
    normed_all, w_qkv, (rows_first, rows_last) = gather_and_swap(
        normed,
        [(query_proj, 0, q_cols), (key_proj, 0, kv_cols), (value_proj, 0, kv_cols)],
        [(w, 0, split) for w in feed], [(w, split, rest) for w in feed]
    )
    w_first = gather_rows(rows_first)
    w_last = gather_rows(rows_last)

    query_scale, key_scale = query_gain.astype(F32)[None], key_gain.astype(F32)[None]
    qkv, attended, logs, gate_sig, mixed, out_all = attend(
        normed_all, w_qkv, w_go, out_low, query_scale, key_scale, cos_rows, sin_rows, heads, head, full_len
    )
    branch = scatter_products((mixed, w_go, q_cols))
    hidden = inputs + branch
    inverse_mid = lax.rsqrt(jnp.mean(hidden * hidden, -1, keepdims=True) + EPSILON)
    gain_mid = swiglu_gain.astype(F32)
    normed_mid = (hidden * inverse_mid * gain_mid).astype(BF16)
    mid_all = gather_tokens(normed_mid)

    act_first, dgu_first, grad_first = feed_forward(mid_all, out_all, w_first)
    part_first = scatter_grads(grad_first)
    w_last, grad_first = lax.optimization_barrier((w_last, grad_first))
    act_last, dgu_last, grad_last = feed_forward(mid_all, out_all, w_last)
    dgu_last, grad_last = lax.optimization_barrier((dgu_last, grad_last))
    part_last = scatter_grads(grad_last)
    dnormed_mid = scatter_products((dgu_first, w_first, 0), (dgu_last, w_last, 0))
    grad_gain_mid = jnp.sum(dnormed_mid * hidden * inverse_mid, 0)
    dhidden = upstream + norm_back(dnormed_mid, hidden, inverse_mid, gain_mid)
    dbranch_all = gather_tokens(dhidden.astype(BF16))
    dbranch_all, part_first = lax.optimization_barrier((dbranch_all, part_first))

    theirs_first = their_rows(part_first)
    dattended, dgating, grad_go = gate_back(
        normed_all, dbranch_all, w_go, attended, gate_sig, mixed
    )
    dattended, theirs_first, grad_go = lax.optimization_barrier((dattended, theirs_first, grad_go))
    part_go = scatter_grads(grad_go)
    dqkv, grad_query_gain, grad_key_gain, ffn_branch = attend_back(
        qkv, dattended, logs, query_scale, key_scale, cos_rows, sin_rows, heads, head, full_len,
        ((act_first, w_first, 2 * split), (act_last, w_last, 2 * rest)),
    )
    grad_query_gain, grad_key_gain = grad_query_gain[0], grad_key_gain[0]
    grad_qkv = dot_tn(normed_all, dqkv).astype(BF16)
    dqkv, grad_qkv, part_last = lax.optimization_barrier((dqkv, grad_qkv, part_last))
    theirs_last = their_rows(part_last)
    dnormed, mine_qkv, theirs_qkv, totals = tail(
        ((dqkv, w_qkv, 0), (dgating, w_go, 0)),
        grad_qkv,
        tokens.reshape(rows, width),
        inverse_in,
        (grad_gain_mid, grad_query_gain, grad_key_gain),
    )
    dnormed, part_go = lax.optimization_barrier((dnormed, part_go))
    input_grad = (dhidden + norm_back(dnormed, inputs, inverse_in, gain_in)).astype(BF16)
    layer_out = (hidden + ffn_branch).astype(BF16)

    plan = [(0, i * split, split, i, 0, i == 2) for i in range(3)]
    plan += [(1, i * rest, rest, i, split, i == 2) for i in range(3)]
    plan += [(2, 0, q_cols, 3, 0, False), (2, q_cols, q_cols, 4, 0, True)]
    weights = (swiglu_gate, swiglu_up, swiglu_down, gating_proj, output_proj)
    grad_gate, grad_up, grad_down, grad_gating, grad_output = join_grads(
        (part_first, part_last, part_go),
        (theirs_first, theirs_last, their_rows(part_go)),
        plan,
        [weight.shape for weight in weights],
    )
    widths, starts = (q_cols, kv_cols, kv_cols), (0, q_cols, q_cols + kv_cols)
    *gain_grads, grad_query, grad_key, grad_value = join_last(
        mine_qkv,
        theirs_qkv,
        totals,
        [(0, starts[i], widths[i], i, 0, False) for i in range(3)],
        (width, width, head, head),
        [weight.shape for weight in (query_proj, key_proj, value_proj)],
    )
    gain_grads = [gain.reshape(-1) for gain in gain_grads]
    shape = (seq_count, local_len, width)
    return (
        layer_out.reshape(shape),
        input_grad.reshape(shape),
        gain_grads[0],
        gain_grads[2],
        gain_grads[3],
        grad_query,
        grad_key,
        grad_value,
        grad_gating,
        grad_output,
        gain_grads[1],
        grad_gate,
        grad_up,
        grad_down,
    )


def solution(mesh):
    if (mesh.shape["dp"], mesh.shape["ctx"]) == (8, 4):
        body = per_device
        mesh = Mesh(mesh.devices.reshape(4, 2, 2, 2), ("z", "y", "x", "c"))
        dp, ctx = ("z", "y"), ("x", "c")
    else:
        body = per_device_wide
        dp, ctx = "dp", "ctx"
    tokens, weight, turned = P(dp, ctx, None), P(dp, ctx), P(ctx, dp)
    return jax.shard_map(
        body,
        mesh=mesh,
        in_specs=(tokens, tokens, P(dp), *[P()] * 6, *[weight] * 4, turned, P(), weight, weight, turned),
        out_specs=(tokens, tokens, *[P()] * 3, *[weight] * 4, turned, P(), weight, weight, turned),
        check_vma=False,
    )
```

profile of v0, /device:TPU:0, one launch (start us, length us, event | category | flops | bytes accessed | tf_op | source)
XLA Modules:
  0.0 569.4 jit_solution(15249723800664818426)
XLA Ops:
  9.1 10.5 %swap_weights.1 = bf16[512,512]{1,0:T(8,128)(2,1)} custom-call(bf16[256,512]{1,0:T(8,128)(2,1)} %refs_0_.2, bf16[256,512]{1,0:T(8,128)(2,1)} %bitcast.47), custom_call_target="tpu_custom_call" | custom-call | bytes 49500000 | tf_op jit(solution)/shard_map/swap_weights/pallas_call | solution.py:218
  20.9 1.9 fusion.10
  24.5 1.9 bitcast_convert_fusion.low_ref
  28.8 74.4 %gather_and_swap.1 = (bf16[2,2,2,256,2048]{4,3,2,1,0:T(8,128)(2,1)}, bf16[2048,512]{1,0:T(8,128)(2,1)}, bf16[512,1536]{1,0:T(8,128)(2,1)}, bf16[512,768]{1,0:T(8,128)(2,1)}) custom-call(bf16[256,2048]{1,0:T(8,128)(2,1)} %fusion.2.source, bf16[256,512]{1,0:T(8,128)(2,1)} %refs_0_.3, bf16[256,256]{1,0:T(8,128)(2,1)} %refs_1_.1, bf16[256,256]{1,0:T(8,128)(2,1)} %refs_2_.1, ...), custom_call_target="tpu_custom_call" | custom-call | bytes 214500000 | tf_op jit(solution)/shard_map/gather_and_swap/pallas_call | solution.py:362
  104.8 43.5 %attend.1 = (f32[2048,512]{1,0:T(8,128)}, f32[2048,256]{1,0:T(8,128)}, f32[2,2048,1]{2,1,0:T(8,128)}, f32[2048,256]{1,0:T(8,128)}, bf16[2048,256]{1,0:T(8,128)(2,1)}, /*index=5*/bf16[2,2,2,256,2048]{4,3,2,1,0:T(8,128)(2,1)}) custom-call(bf16[2048,2048]{1,0:T(8,128)(2,1)} %bitcast.40, bf16[2048,512]{1,0:T(8,128)(2,1)} %get-tuple-element.72.w_ref.refs_2_, ...), custom_call_target="tpu_custom_call" | custom-call | bytes 138600000 | tf_op jit(solution)/shard_map/attend/pallas_call | solution.py:933
  148.3 42.9 %scatter_products.2 = f32[256,2048]{1,0:T(8,128)} custom-call(bf16[2048,256]{1,0:T(8,128)(2,1)} %get-tuple-element.76.refs_0_.mixed_ref, bf16[2048,512]{1,0:T(8,128)(2,1)} %all-gather.4.cloned.1.call-done.wg_ref.refs_1_.w_ref.refs_3_), custom_call_target="tpu_custom_call" | custom-call | bytes 158400000 | tf_op jit(solution)/shard_map/scatter_products/pallas_call | solution.py:534
  191.1 1.9 multiply_reduce_fusion.2
  195.7 40.5 %gather_tokens.2 = bf16[2,2,2,256,2048]{4,3,2,1,0:T(8,128)(2,1)} custom-call(bf16[256,2048]{1,0:T(8,128)(2,1)} %multiply_convert_fusion.refs_0_), custom_call_target="tpu_custom_call" | custom-call | bytes 138600000 | tf_op jit(solution)/shard_map/gather_tokens/pallas_call | solution.py:242
  236.2 41.0 %feed_forward.2 = (bf16[2048,512]{1,0:T(8,128)(2,1)}, bf16[2048,1024]{1,0:T(8,128)(2,1)}, bf16[2048,1536]{1,0:T(8,128)(2,1)}) custom-call(bf16[2048,2048]{1,0:T(8,128)(2,1)} %bitcast.37, bf16[2048,2048]{1,0:T(8,128)(2,1)} %bitcast.44, bf16[2048,1536]{1,0:T(8,128)(2,1)} %all-gather.6.cloned.1.call-done.w_ref.refs_2_), custom_call_target="tpu_custom_call" | custom-call | bytes 132000000 | tf_op jit(solution)/shard_map/feed_forward/pallas_call | solution.py:1070
  277.7 3.0 all-gather.8.cloned.1.call-done.w_ref.refs_3_
  280.6 23.2 %feed_forward.3 = (bf16[2048,256]{1,0:T(8,128)(2,1)}, bf16[2048,512]{1,0:T(8,128)(2,1)}, bf16[2048,768]{1,0:T(8,128)(2,1)}) custom-call(bf16[2048,2048]{1,0:T(8,128)(2,1)} %bitcast.38, bf16[2048,2048]{1,0:T(8,128)(2,1)} %bitcast.45, bf16[2048,768]{1,0:T(8,128)(2,1)} %all-gather.8.cloned.1.call-done.w_ref.refs_3_), custom_call_target="tpu_custom_call" | custom-call | bytes 132000000 | tf_op jit(solution)/shard_map/feed_forward/pallas_call | solution.py:1070
  304.0 49.5 %scatter_products.3 = f32[256,2048]{1,0:T(8,128)} custom-call(bf16[2048,1024]{1,0:T(8,128)(2,1)} %get-tuple-element.80.refs_0_, bf16[2048,512]{1,0:T(8,128)(2,1)} %get-tuple-element.86.refs_1_, bf16[2048,1536]{1,0:T(8,128)(2,1)} %all-gather.6.cloned.1.call-done.w_ref.refs_2_, bf16[2048,768]{1,0:T(8,128)(2,1)} %all-gather.8.cloned.1.call-done.w_ref.refs_3_), custom_call_target="tpu_custom_call" | custom-call | bytes 158400000 | tf_op jit(solution)/shard_map/scatter_products/pallas_call | solution.py:534
  353.5 2.9 multiply_reduce_fusion
  356.4 3.0 fusion.12
  359.4 40.7 %gather_tokens.3 = bf16[2,2,2,256,2048]{4,3,2,1,0:T(8,128)(2,1)} custom-call(bf16[256,2048]{1,0:T(8,128)(2,1)} %get-tuple-element.128.refs_0_), custom_call_target="tpu_custom_call" | custom-call | bytes 138600000 | tf_op jit(solution)/shard_map/gather_tokens/pallas_call | solution.py:242
  402.0 17.5 %gate_back.1 = (bf16[2048,256]{1,0:T(8,128)(2,1)}, bf16[2048,256]{1,0:T(8,128)(2,1)}, bf16[2048,512]{1,0:T(8,128)(2,1)}) custom-call(bf16[2048,2048]{1,0:T(8,128)(2,1)} %bitcast.41, bf16[2048,2048]{1,0:T(8,128)(2,1)} %bitcast.43, bf16[2048,512]{1,0:T(8,128)(2,1)} %all-gather.4.cloned.1.call-done.wg_ref.refs_1_.w_ref.refs_3_, ...), custom_call_target="tpu_custom_call" | custom-call | bytes 82500000 | tf_op jit(solution)/shard_map/gate_back/pallas_call | solution.py:1019
  419.5 1.9 collective-permute-done.refs_3_
  422.4 49.0 %attend_back.1 = (bf16[2048,512]{1,0:T(8,128)(2,1)}, f32[1,128]{1,0:T(1,128)}, f32[1,128]{1,0:T(1,128)}, f32[256,2048]{1,0:T(8,128)}) custom-call(f32[2048,512]{1,0:T(8,128)} %get-tuple-element.77.raw_ref, bf16[2048,256]{1,0:T(8,128)(2,1)} %get-tuple-element.93.up_ref, f32[2,2048,1]{2,1,0:T(8,128)} %get-tuple-element.94.log_ref, ...), custom_call_target="tpu_custom_call" | custom-call | bytes 158400000 | tf_op jit(solution)/shard_map/attend_back/pallas_call | solution.py:1171
  471.4 9.9 %convolution_convert_fusion.refs_4_ = bf16[2048,512]{1,0:T(8,128)(2,1)} fusion(bf16[2048,2048]{1,0:T(8,128)(2,1)} %bitcast.42, bf16[2048,512]{1,0:T(8,128)(2,1)} %get-tuple-element.100.refs_0_), kind=kOutput, calls=%fused_computation.5 | convolution fusion | flops 4296015872 | bytes 12582912 | tf_op jit(solution)/shard_map/dot_general | solution.py:30
  484.8 59.0 %tail.1 = (f32[256,2048]{1,0:T(8,128)}, bf16[256,512]{1,0:T(8,128)(2,1)}, bf16[256,512]{1,0:T(8,128)(2,1)}, f32[1,4352]{1,0:T(1,128)}) custom-call(bf16[2048,512]{1,0:T(8,128)(2,1)} %get-tuple-element.100.refs_0_, bf16[2048,256]{1,0:T(8,128)(2,1)} %get-tuple-element.101.refs_1_, bf16[2048,512]{1,0:T(8,128)(2,1)} %get-tuple-element.72.w_ref.refs_2_, ...), custom_call_target="tpu_custom_call" | custom-call | bytes 171600000 | tf_op jit(solution)/shard_map/tail/pallas_call | solution.py:756
  543.8 2.1 join_last.1
  545.9 3.6 fusion.8
  553.4 3.8 collective-permute-done.2.refs_5_
  557.2 5.1 join_grads.1
  (79 shorter events, 21.4 us)
Async XLA Ops:
  7.2 12.4 %copy-start.11 = (bf16[2048]{0:T(1024)(128)(2,1)S(1)}, bf16[2048]{0:T(1024)(128)(2,1)}, u32[]{:S(2)}) copy-start(bf16[2048]{0:T(1024)(128)(2,1)} %param.24) | copy-start | bytes 12292
  7.2 13.1 %copy-start.13 = (s32[32]{0:T(128)S(1)}, s32[32]{0:T(128)}, u32[]{:S(2)}) copy-start(s32[32]{0:T(128)} %param.21) | copy-start | bytes 388
  7.2 13.1 %copy-start.15 = (s32[32]{0:T(128)S(1)}, s32[32]{0:T(128)}, u32[]{:S(2)}) copy-start(s32[32]{0:T(128)} %param.22) | copy-start | bytes 388
  7.2 13.1 %copy-start.14 = (s32[32]{0:T(128)S(1)}, s32[32]{0:T(128)}, u32[]{:S(2)}) copy-start(s32[32]{0:T(128)} %param.23) | copy-start | bytes 388
  7.2 97.6 %all-gather.4.cloned.1.call-start = ((), (), s32[]{:S(2)}) async-start(), calls=%async_computation.3 | async-start | bytes 2621440 | tf_op jit(solution)/shard_map/all_gather | solution.py:787
  19.6 216.6 %all-gather.6.cloned.1.call-start = ((), (), s32[]{:S(2)}) async-start(), calls=%async_computation.4 | async-start | bytes 7864320 | tf_op jit(solution)/shard_map/all_gather | solution.py:787
  20.9 3.2 copy-start.2
  22.8 1.6 copy-start.7
  24.5 3.2 copy-start.8
  103.3 177.4 %all-gather.8.cloned.1.call-start = ((), (), s32[]{:S(2)}) async-start(), calls=%async_computation.5 | async-start | bytes 3932160 | tf_op jit(solution)/shard_map/all_gather | solution.py:787
  104.0 296.2 %reduce-scatter.4.cloned.1.call-start = ((), (), s32[]{:S(2)}) async-start(), calls=%async_computation.6 | async-start | bytes 7864320 | tf_op jit(solution)/shard_map/reduce_scatter | solution.py:791
  193.1 1.4 copy-start
  277.2 204.1 %reduce-scatter.6.cloned.1.call-start = ((), (), s32[]{:S(2)}) async-start(), calls=%async_computation.7 | async-start | bytes 3932160 | tf_op jit(solution)/shard_map/reduce_scatter | solution.py:791
  303.9 245.6 %reduce-scatter.8.cloned.1.call-start = ((), (), s32[]{:S(2)}) async-start(), calls=%async_computation.8 | async-start | bytes 2621440 | tf_op jit(solution)/shard_map/reduce_scatter | solution.py:791
  303.9 49.5 %copy-start.1 = (f32[256,2048]{1,0:T(8,128)S(1)}, f32[256,2048]{1,0:T(8,128)}, u32[]{:S(2)}) copy-start(f32[256,2048]{1,0:T(8,128)} %copy-done) | copy-start | bytes 6291460
  353.5 2.9 copy-start.4
  401.6 19.9 %collective-permute-start = (bf16[256,1536]{1,0:T(8,128)(2,1)S(1)}, bf16[256,1536]{1,0:T(8,128)(2,1)S(1)}, u32[]{:S(2)}, u32[]{:S(2)}) collective-permute-start(bf16[256,1536]{1,0:T(8,128)(2,1)S(1)} %constant_dynamic-slice_fusion.2), channel_id=1, source_target_pairs={{0,4},{4,0},{1,5},{5,1},{2,6},{6,2},{3,7},{7,3},{8,12},{12,8},{9,1... | collective-permute-start | bytes 2359304 | tf_op jit(solution)/shard_map/ppermute | solution.py:776
  421.5 49.9 %copy-start.9 = (bf16[256,1536]{1,0:T(8,128)(2,1)}, bf16[256,1536]{1,0:T(8,128)(2,1)S(1)}, u32[]{:S(2)}) copy-start(bf16[256,1536]{1,0:T(8,128)(2,1)S(1)} %collective-permute-done.refs_3_) | copy-start | bytes 2359300
  483.1 70.3 %collective-permute-start.1 = (bf16[256,768]{1,0:T(8,128)(2,1)}, bf16[256,768]{1,0:T(8,128)(2,1)S(1)}, u32[]{:S(2)}, u32[]{:S(2)}) collective-permute-start(bf16[256,768]{1,0:T(8,128)(2,1)} %constant_dynamic-slice_fusion.1), channel_id=1, source_target_pairs={{0,4},{4,0},{1,5},{5,1},{2,6},{6,2},{3,7},{7,3},{8,12},{12,8},{9,1... | collective-permute-start | bytes 1179656 | tf_op jit(solution)/shard_map/ppermute | solution.py:776
  545.9 5.5 copy-start.3
  545.9 5.5 copy-start.5
  549.5 2.3 copy-start.6
  550.6 6.5 %collective-permute-start.2 = (bf16[256,512]{1,0:T(8,128)(2,1)S(1)}, bf16[256,512]{1,0:T(8,128)(2,1)}, u32[]{:S(2)}, u32[]{:S(2)}) collective-permute-start(bf16[256,512]{1,0:T(8,128)(2,1)S(1)} %constant_dynamic-slice_fusion), channel_id=1, source_target_pairs={{0,4},{4,0},{1,5},{5,1},{2,6},{6,2},{3,7},{7,3},{8,12},{12,8},{9,1... | collective-permute-start | bytes 786440 | tf_op jit(solution)/shard_map/ppermute | solution.py:776
  553.4 3.8 copy-start.10
  (3 other events, 3.1 us)
Sparse Core Ops, SparseCore 0:
  19.7 58.8 all-gather.3
  103.4 113.8 all-gather.5
  218.9 61.7 all-gather.7
  282.8 109.3 reduce-scatter.3
  394.4 60.7 reduce-scatter.5
  457.3 52.7 reduce-scatter.7
where the time goes:
time: 574 us; the launch traced here: 569 us
  Pallas kernels  499 us (87%)
  other arithmetic  22.5 us (4%)
  between operations  15.3 us (3%)
  matrix products  9.94 us (2%)
  local copies, waits for them, and re-layouts  9.58 us (2%)
  waiting for transfers between devices  9.5 us (2%)
    pallas_call x2, Pallas kernels, scatter_products(): pl.pallas_call(functools.partial(scatter_kernel, [item[2] for item in gro...  92.4 us
    pallas_call x2, Pallas kernels, gather_tokens(): pl.pallas_call(functools.partial(gather_kernel, True), out_shape=jax.Shap...  81.2 us
    pallas_call x1, Pallas kernels, gather_and_swap(): pl.pallas_call(functools.partial(gather_swap_kernel, pieces, len(weights)...  74.4 us
    pallas_call x2, Pallas kernels, feed_forward(): pl.pallas_call(functools.partial(feed_kernel, count, 256), out_shape=(jax...  64.3 us
    pallas_call x1, Pallas kernels, tail(): pl.pallas_call(functools.partial(tail_kernel, [item[2] for item in group]...  59 us
    pallas_call x1, Pallas kernels, attend_back(): pl.pallas_call(functools.partial(attend_back_kernel, heads, head, block,...  49 us
    pallas_call x1, Pallas kernels, attend(): pl.pallas_call(functools.partial(attend_kernel, heads, head, block), out_...  43.5 us
    pallas_call x1, Pallas kernels, gate_back(): pl.pallas_call(gate_back_kernel, out_shape=(jax.ShapeDtypeStruct((rows, c...  17.5 us
  transfers between devices with their start and end apart: 9, of which 3 were waited for; matrix products, arithmetic and copies ran while one was open for 7% of the time, Pallas kernels for 85%

commit v1 on v0

--- a/solution.py
+++ b/solution.py
@@ -2,6 +2,7 @@
 
 import jax
 import jax.numpy as jnp
+import numpy as np
 from jax import lax
 from jax.experimental import pallas as pl
 from jax.experimental.pallas import tpu as pltpu
@@ -181,50 +182,15 @@
         for copy in (*copies, *locals_):
             copy.start()
 
+    def here():
+        for copy in locals_:
+            copy.wait()
+
     def finish():
-        for copy in (*copies, *locals_):
+        for copy in copies:
             copy.wait()
 
-    return begin, finish
-
-
-def swap_plan(groups):
-    weights, pieces, widths = [], [], []
-    for group in groups:
-        width = 0
-        for weight, first, count in group:
-            index = next((i for i, w in enumerate(weights) if w is weight), len(weights))
-            if index == len(weights):
-                weights.append(weight)
-            pieces.append((index, len(widths), first, count, width))
-            width += count
-        widths.append(width)
-    rows = 2 * weights[0].shape[0]
-    shapes = tuple(jax.ShapeDtypeStruct((rows, width), BF16) for width in widths)
-    count = len(pieces)
-    semaphores = [pltpu.SemaphoreType.DMA((count,))] * 3
-    return weights, pieces, shapes, semaphores
-
-
-def swap_kernel(pieces, count, *refs):
-    begin, finish = swap_steps(pieces, refs[:count], refs[count:-3], *refs[-3:])
-    greet((place()[3]["y"],))
-    begin()
-    finish()
-
-
-def swap_weights(*groups):
-    weights, pieces, shapes, semaphores = swap_plan(groups)
-    return pl.pallas_call(
-        functools.partial(swap_kernel, pieces, len(weights)),
-        out_shape=shapes,
-        in_specs=[pl.BlockSpec(memory_space=pltpu.VMEM)] * len(weights),
-        out_specs=(pl.BlockSpec(memory_space=pl.ANY),) * len(shapes),
-        scratch_shapes=semaphores,
-        compiler_params=pltpu.CompilerParams(collective_id=4, has_side_effects=True),
-        cost_estimate=micros(15),
-        name="swap_weights",
-    )(*weights)
+    return begin, here, finish
 
 
 def gather_kernel(split, *refs):
@@ -251,32 +217,34 @@
     )(shard).reshape(8 * rows, width)
 
 
-def line_steps(rows_ref, out_ref, local_sem, send, recv):
+def line_steps(rows_ref, out_ref, local_sem, send, recv, part, which):
     z = lax.axis_index("z")
-    rows = rows_ref.shape[0]
+    rows, half = rows_ref.shape[0], rows_ref.shape[0] // 2
+    first = which * half
     pair, middle = z + 1 - 2 * lax.rem(z, 2), 3 - z
     inner = (z == 1) | (z == 2)
 
     def at(index):
-        return out_ref.at[pl.ds(pl.multiple_of(index * rows, rows), rows)]
+        return out_ref.at[pl.ds(pl.multiple_of(index * rows + first, half), half)]
 
     def remote(index, source, target, peer):
         return pltpu.make_async_remote_copy(
             src_ref=source,
             dst_ref=target,
-            send_sem=send.at[index],
-            recv_sem=recv.at[index],
+            send_sem=send.at[5 * part + index],
+            recv_sem=recv.at[5 * part + index],
             device_id={"z": peer},
             device_id_type=MESH,
         )
 
     far = middle + 1 - 2 * lax.rem(middle, 2)
-    own_pair = remote(0, rows_ref, at(z), pair)
-    own_middle = remote(1, rows_ref, at(z), middle)
+    own = rows_ref.at[pl.ds(pl.multiple_of(first, half), half)]
+    own_pair = remote(0, own, at(z), pair)
+    own_middle = remote(1, own, at(z), middle)
     pair_middle = remote(2, at(pair), at(pair), middle)
     middle_pair = remote(3, at(middle), at(middle), pair)
     far_pair = remote(4, at(far), at(far), pair)
-    local = pltpu.make_async_copy(rows_ref, at(z), local_sem)
+    local = pltpu.make_async_copy(own, at(z), local_sem.at[part])
 
     def begin():
         local.start()
@@ -331,62 +299,157 @@
     pl.semaphore_wait(barrier, jnp.where(inner, count + 1, count))
 
 
-def gather_swap_kernel(pieces, count, source, *refs):
-    out, line_out, outs, scratch = refs[count], refs[count + 1], refs[count + 2 : -10], refs[-10:]
-    line, sems = scratch[0], scratch[1:]
-    begin, forward, across, finish = gather_steps(source, out, *sems[:3], False)
-    line_begin, line_second, line_third, line_finish, peers = line_steps(line, line_out, *sems[3:6])
-    targets = (line, *outs)
-    early, early_done = swap_steps(pieces, refs[:count], targets, *sems[6:], lambda out: out == 0)
-    swap, swapped = swap_steps(pieces, refs[:count], targets, *sems[6:], lambda out: out > 0)
-    greet_line(tuple(place()[3].values()), *peers())
-    early()
+def opening_kernel(pieces, tokens, cotangent, gain, ids, counts, numer, denom, turns, *refs):
+    sources, refs = list(refs[:8]), refs[8:]
+    out, line_q, line_g, first, last, inverse, low, factor, cosine, sine, *refs = refs
+    rows_q, rows_g, normed, output_t, down_t, *sems = refs
+    begin, forward, across, finish = gather_steps(normed, out, *sems[:3], False)
+    y = lax.axis_index("y")
+    steps = [
+        line_steps(rows, line, *sems[3 * i + 3 : 3 * i + 6], part, which)
+        for part, which in ((0, y), (1, 1 - y))
+        for i, (rows, line) in enumerate(((rows_q, line_q), (rows_g, line_g)))
+    ]
+    output_ref, down_ref = sources[4], sources[7]
+    sources[4], sources[7] = output_t, down_t
+    swaps = [
+        swap_steps(pieces, sources, (rows_q, rows_g, first, last), *sems[9:], wanted)
+        for wanted in (lambda out: out == 0, lambda out: out == 1, lambda out: out > 1)
+    ]
+    step = 64
+
+    def norm(i):
+        at = pl.ds(i * step, step)
+        x = tokens[at].astype(F32)
+        inv = lax.rsqrt(jnp.mean(x * x, -1, keepdims=True) + EPSILON)
+        inverse[at] = inv
+        normed[at] = (x * inv * gain[...].astype(F32)).astype(BF16)
+
+    def weigh(i):
+        at = pl.ds(i * step, step)
+        low[at] = (cotangent[at].astype(F32) * factor[...]).astype(BF16)
+
+    def turn(i):
+        at = pl.ds(i * 128, 128)
+        places = lax.broadcasted_iota(jnp.int32, (128, cosine.shape[1]), 0) + i * 128
+        angles = places.astype(F32) * turns[0:1]
+        cosine[at] = jnp.cos(angles)
+        sine[at] = jnp.sin(angles) * turns[1:2]
+
+    greet_line(tuple(place()[3].values()), *steps[0][4]())
+    swaps[0][0]()
+    output_t[...] = output_ref[...].astype(F32).T.astype(BF16)
+    swaps[1][0]()
+    for i in range(2):
+        swaps[i][1]()
+        steps[i][0]()
+    pl.loop(0, tokens.shape[0] // step)(norm)
     begin()
-    early_done()
-    line_begin()
-    line_second()
+    for i in range(2):
+        swaps[i][2]()
+        steps[i + 2][0]()
+    steps[0][1]()
+    steps[1][1]()
+    chosen = lax.broadcasted_iota(jnp.int32, counts.shape, 1) == ids[...]
+    ratio = numer[...].astype(F32) / denom[...].astype(F32) * LENGTH / counts[...].astype(F32)
+    factor[...] = jnp.sum(jnp.where(chosen, ratio, 0.0), -1, keepdims=True)
+
+    @pl.loop(0, down_ref.shape[0] // 256)
+    def _(i):
+        at = pl.ds(pl.multiple_of(i * 256, 256), 256)
+        down_t[:, at] = down_ref[at].astype(F32).T.astype(BF16)
+
     forward()
     across()
-    swap()
-    line_third()
+    swaps[2][0]()
+    steps[2][1]()
+    steps[3][1]()
+    steps[0][2]()
+    steps[1][2]()
+    pl.loop(0, tokens.shape[0] // step)(weigh)
+    steps[2][2]()
+    steps[3][2]()
+    pl.loop(0, cosine.shape[0] // 128)(turn)
     finish()
-    line_finish()
-    swapped()
-
-
-def gather_and_swap(shard, *groups):
-    rows, width = shard.shape
-    weights, pieces, shapes, semaphores = swap_plan(groups)
-    line, shapes = shapes[0], shapes[1:]
-    whole = jax.ShapeDtypeStruct((4 * line.shape[0], line.shape[1]), line.dtype)
-    gathered, lined, *swapped = pl.pallas_call(
-        functools.partial(gather_swap_kernel, pieces, len(weights)),
-        out_shape=(jax.ShapeDtypeStruct((2, 2, 2, rows, width), shard.dtype), whole, *shapes),
-        in_specs=[pl.BlockSpec(memory_space=pltpu.VMEM)] * (1 + len(weights)),
-        out_specs=(pl.BlockSpec(memory_space=pl.ANY),) * (2 + len(shapes)),
+    for step_set in steps:
+        step_set[3]()
+    swaps[2][1]()
+    swaps[2][2]()
+
+
+def opening(tokens, cotangent, gain, domains, weights, split, full_len, head):
+    rows, width = tokens.shape
+    halves = [weight.shape[0 if i in (4, 7) else 1] // 2 for i, weight in enumerate(weights)]
+    groups = (
+        [(i, 0, halves[i]) for i in (0, 1, 2)],
+        [(i, 0, halves[i]) for i in (3, 4)],
+        [(i, 0, split) for i in (5, 6, 7)],
+        [(i, split, halves[i] - split) for i in (5, 6, 7)],
+    )
+    pieces, widths = [], []
+    for group in groups:
+        at = 0
+        for source, first, count in group:
+            pieces.append((source, len(widths), first, count, at))
+            at += count
+        widths.append(at)
+    inverse = 1.0 / np.float32(ROPE_BASE) ** (np.arange(head // 2, dtype=np.float32) * np.float32(2.0 / head))
+    turns = np.stack([np.tile(inverse, 2), np.repeat(np.float32([-1.0, 1.0]), head // 2)]).astype(np.float32)
+    whole, loose = pl.BlockSpec(memory_space=pltpu.VMEM), pl.BlockSpec(memory_space=pl.ANY)
+    shape = jax.ShapeDtypeStruct
+    dma = pltpu.SemaphoreType.DMA
+    gathered, *outs = pl.pallas_call(
+        functools.partial(opening_kernel, pieces),
+        out_shape=(
+            shape((2, 2, 2, rows, width), BF16),
+            *[shape((8 * rows, size), BF16) for size in widths[:2]],
+            *[shape((2 * rows, size), BF16) for size in widths[2:]],
+            shape((rows, 1), F32),
+            shape((rows, width), BF16),
+            shape((1, 1), F32),
+            shape((full_len, head), F32),
+            shape((full_len, head), F32),
+        ),
+        in_specs=[whole] * (8 + len(weights)),
+        out_specs=(*[loose] * 5, *[whole] * 5),
         scratch_shapes=[
-            pltpu.VMEM(line.shape, line.dtype),
+            *[pltpu.VMEM((2 * rows, size), BF16) for size in widths[:2]],
+            pltpu.VMEM((rows, width), BF16),
+            *[pltpu.VMEM(weights[i].shape[::-1], BF16) for i in (4, 7)],
             *GATHER_SEMAPHORES,
-            pltpu.SemaphoreType.DMA,
-            pltpu.SemaphoreType.DMA((5,)),
-            pltpu.SemaphoreType.DMA((5,)),
-            *semaphores,
+            *[dma((2,)), dma((10,)), dma((10,))] * 2,
+            *[dma((len(pieces),))] * 3,
         ],
-        compiler_params=pltpu.CompilerParams(collective_id=2, has_side_effects=True),
-        cost_estimate=micros(65),
-        name="gather_and_swap",
-    )(shard, *weights)
-    return gathered.reshape(8 * rows, width), lined, swapped
-
-
-def scatter_steps(windows, lefts, rights, out_ref, left_vmem, right_vmem, own, away, got, x_diag, y_diag, x_got, y_got, load_sem, send, recv):
+        compiler_params=pltpu.CompilerParams(
+            collective_id=2, has_side_effects=True, vmem_limit_bytes=VMEM_BYTES
+        ),
+        cost_estimate=micros(80),
+        name="opening",
+    )(
+        tokens,
+        cotangent,
+        gain.reshape(1, -1),
+        *(domain.reshape(1, -1) for domain in domains),
+        jnp.asarray(turns),
+        *weights,
+    )
+    return gathered.reshape(8 * rows, width), *outs
+
+
+def add_rows(target, start, size, other, base, step=64):
+    @pl.loop(0, size // step)
+    def _(i):
+        at, there = pl.ds(start + i * step, step), pl.ds(base + i * step, step)
+        target[at] = (target[at].astype(F32) + other[there].astype(F32)).astype(target.dtype)
+
+
+def product_steps(windows, lefts, rights, left_vmem, right_vmem, own, pairs, got, load_sem, send, recv):
     y, x, c, device = place()
     remote = remote_copies(send, recv, device)
     rows, width = own.shape[1:]
-    half, both = rows // 2, 2 * rows
-    low, high = pl.ds(0, half), pl.ds(half, half)
+    half, both, tile = rows // 2, 2 * rows, 512
     targets = ((1 - y, 1 - x), (1 - y, x), (y, 1 - x), (y, x))
-    starts = [pl.multiple_of((a * 2 + b) * both, both) for a, b in targets]
+    pieces = ((0, 0, half), (0, half, half), (1, 0, rows), (2, 0, rows), (3, 0, rows))
     count = len(lefts)
     right_loads = [
         pltpu.make_async_copy(
@@ -394,50 +457,21 @@
         )
         for j in range(count)
     ]
-    left_loads = [
-        [
-            pltpu.make_async_copy(
-                lefts[j].at[pl.ds(start, both)], left_vmem[j].at[i], load_sem.at[count * (i + 1) + j]
-            )
-            for j in range(count)
-        ]
-        for i, start in enumerate(starts)
+    left_loads = []
+    for i, (a, b) in enumerate(targets):
+        start = pl.multiple_of((a * 2 + b) * both, both)
+        left_loads.append(
+            [
+                pltpu.make_async_copy(
+                    lefts[j].at[pl.ds(start, both)], left_vmem[j].at[i], load_sem.at[count * (i + 1) + j]
+                )
+                for j in range(count)
+            ]
+        )
+    crossing = [
+        remote(k, pairs.at[i, 1 - c, pl.ds(first, size)], got.at[i, pl.ds(first, size)], "c")
+        for k, (i, first, size) in enumerate(pieces)
     ]
-    crossing = [remote(i, away.at[i], got.at[i], "c") for i in range(4)]
-    diag_x = remote(4, own.at[0, low], x_diag, "x")
-    diag_y = remote(5, own.at[0, high], y_diag, "y")
-    y_high = remote(6, own.at[1, high], y_got.at[high], "y")
-    x_low = remote(7, own.at[2, low], x_got.at[low], "x")
-    y_low = remote(8, own.at[1, low], y_got.at[low], "y")
-    x_high = remote(9, own.at[2, high], x_got.at[high], "x")
-    step, tile = 64, 512
-
-    def add_into(target, start, size, other, base):
-        @pl.loop(0, size // step)
-        def _(i):
-            at, there = pl.ds(start + i * step, step), pl.ds(base + i * step, step)
-            target[at] = (target[at].astype(F32) + other[there].astype(F32)).astype(target.dtype)
-
-    mine, others = pl.ds(c * rows, rows), pl.ds((1 - c) * rows, rows)
-
-    def product(i):
-        for load in left_loads[i]:
-            load.wait()
-
-        @pl.loop(0, width // tile)
-        def _(n):
-            cols = pl.ds(pl.multiple_of(n * tile, tile), tile)
-            for part, target in ((others, away), (mine, own)):
-                total = dot_nt(left_vmem[0][i, part], right_vmem[0][cols])
-                for j in range(1, count):
-                    total = total + dot_nt(left_vmem[j][i, part], right_vmem[j][cols])
-                target[i, :, cols] = total.astype(target.dtype)
-
-        crossing[i].start()
-
-    def cores(i):
-        crossing[i].wait_recv()
-        add_into(own.at[i], 0, rows, got.at[i], 0)
 
     def load():
         for copy in right_loads:
@@ -446,143 +480,351 @@
             for copy in copies:
                 copy.start()
 
-    def first_a():
+    def ready():
         for copy in right_loads:
             copy.wait()
-        product(0)
-        product(1)
-
-    def first_b():
-        cores(0)
-        diag_x.start()
-        diag_y.start()
-        product(2)
-        cores(1)
-        y_high.start()
-
-    def first_c():
-        product(3)
-        cores(2)
-        x_low.start()
-
-    def first():
-        first_a()
-        first_b()
-        first_c()
-
-    first.parts = (first_a, first_b, first_c)
+
+    def product(i):
+        for copy in left_loads[i]:
+            copy.wait()
+
+        @pl.loop(0, width // tile)
+        def _(n):
+            cols = pl.ds(pl.multiple_of(n * tile, tile), tile)
+            total = dot_nt(left_vmem[0][i], right_vmem[0][cols])
+            for j in range(1, count):
+                total = total + dot_nt(left_vmem[j][i], right_vmem[j][cols])
+            pairs[i, :, :, cols] = total.reshape(2, rows, tile).astype(BF16)
+
+        for k, piece in enumerate(pieces):
+            if piece[0] == i:
+                crossing[k].start()
+
+    def cores(k, step=64):
+        i, first, size = pieces[k]
+        crossing[k].wait_recv()
+
+        @pl.loop(0, size // step)
+        def _(n):
+            at = pl.ds(first + n * step, step)
+            own[i, at] = (pairs[i, c, at].astype(F32) + got[i, at].astype(F32)).astype(BF16)
+
+    def finish():
+        for copy in crossing:
+            copy.wait_send()
+
+    return load, ready, product, cores, finish
+
+
+def axis_steps(own, x_diag, y_diag, x_got, y_got, send, recv):
+    remote = remote_copies(send, recv, place()[3])
+    rows = own.shape[1]
+    half = rows // 2
+    low, high = pl.ds(0, half), pl.ds(half, half)
+    diag_x = remote(0, own.at[0, low], x_diag, "x")
+    diag_y = remote(1, own.at[0, high], y_diag, "y")
+    y_high = remote(2, own.at[1, high], y_got.at[high], "y")
+    x_low = remote(3, own.at[2, low], x_got.at[low], "x")
+    y_low = remote(4, own.at[1, low], y_got.at[low], "y")
+    x_high = remote(5, own.at[2, high], x_got.at[high], "x")
 
     def second():
         diag_x.wait_recv()
-        add_into(own.at[1], 0, half, x_diag, 0)
+        add_rows(own.at[1], 0, half, x_diag, 0)
         y_low.start()
         diag_y.wait_recv()
-        add_into(own.at[2], half, half, y_diag, 0)
+        add_rows(own.at[2], half, half, y_diag, 0)
         x_high.start()
-        cores(3)
-
-    def finish():
+
+    def finish(store, step=32):
         for copy in (y_high, x_low, y_low, x_high):
             copy.wait_recv()
 
         @pl.loop(0, rows // step)
         def _(i):
             at = pl.ds(i * step, step)
-            out_ref[at] = own[3, at].astype(F32) + x_got[at].astype(F32) + y_got[at].astype(F32)
-
-        for copy in (*crossing, diag_x, diag_y, y_high, x_low, y_low, x_high):
+            store(at, own[3, at].astype(F32) + x_got[at].astype(F32) + y_got[at].astype(F32))
+
+        for copy in (diag_x, diag_y, y_high, x_low, y_low, x_high):
             copy.wait_send()
 
+    return diag_x, diag_y, x_low, y_high, second, finish
+
+
+def scatter_steps(windows, lefts, rights, scratch):
+    count = len(windows)
+    product_scratch, axis_scratch = scratch[: 2 * count + 6], scratch[2 * count + 6 :]
+    load, ready, product, cores, crossed = product_steps(
+        windows, lefts, rights, product_scratch[:count], product_scratch[count : 2 * count],
+        *product_scratch[2 * count :],
+    )
+    own = product_scratch[2 * count]
+    diag_x, diag_y, x_low, y_high, second_axis, finish_axis = axis_steps(own, *axis_scratch)
+
+    def first():
+        ready()
+        product(0)
+        cores(0)
+        diag_x.start()
+        cores(1)
+        diag_y.start()
+        product(2)
+        product(1)
+        cores(3)
+        x_low.start()
+        cores(2)
+        y_high.start()
+
+    def second():
+        second_axis()
+        product(3)
+        cores(4)
+
+    def finish(store):
+        finish_axis(store)
+        crossed()
+
     return load, first, second, finish
 
 
-def scatter_scratch(group):
+def product_scratch(group, own=True):
     lefts, rights = [item[0] for item in group], [item[1] for item in group]
     rows, width = lefts[0].shape[0] // 8, rights[0].shape[0]
-    scratch = [
+    return [
         *[pltpu.VMEM((4, 2 * rows, left.shape[1]), BF16) for left in lefts],
         *[pltpu.VMEM((width, left.shape[1]), BF16) for left in lefts],
+        *[pltpu.VMEM((4, rows, width), BF16)] * own,
+        pltpu.VMEM((4, 2, rows, width), BF16),
         pltpu.VMEM((4, rows, width), BF16),
-        pltpu.VMEM((4, rows, width), BF16),
-        pltpu.VMEM((4, rows, width), BF16),
+        pltpu.SemaphoreType.DMA((5 * len(group),)),
+        pltpu.SemaphoreType.DMA((5,)),
+        pltpu.SemaphoreType.DMA((5,)),
+    ]
+
+
+def axis_scratch(rows, width):
+    return [
         pltpu.VMEM((rows // 2, width), BF16),
         pltpu.VMEM((rows // 2, width), BF16),
         pltpu.VMEM((rows, width), BF16),
         pltpu.VMEM((rows, width), BF16),
-        pltpu.SemaphoreType.DMA((5 * len(group),)),
-        pltpu.SemaphoreType.DMA((10,)),
-        pltpu.SemaphoreType.DMA((10,)),
+        pltpu.SemaphoreType.DMA((6,)),
+        pltpu.SemaphoreType.DMA((6,)),
     ]
+
+
+def scatter_scratch(group):
+    lefts, rights = [item[0] for item in group], [item[1] for item in group]
+    rows, width = lefts[0].shape[0] // 8, rights[0].shape[0]
+    scratch = product_scratch(group) + axis_scratch(rows, width)
     return lefts + rights, scratch, jax.ShapeDtypeStruct((rows, width), F32)
 
 
-def scatter_kernel(windows, *refs):
+def middle_kernel(windows, *refs):
     count = len(windows)
-    lefts, rights, out_ref, scratch = refs[:count], refs[count : 2 * count], refs[2 * count], refs[2 * count + 1 :]
-    load, first, second, finish = scatter_steps(
-        windows, lefts, rights, out_ref, scratch[:count], scratch[count : 2 * count], *scratch[2 * count :]
-    )
+    lefts, rights, refs = refs[:count], refs[count : 2 * count], refs[2 * count :]
+    tokens, gain, hidden, inverse, normed, *scratch = refs
+    load, first, second, finish = scatter_steps(windows, lefts, rights, scratch)
+
+    def store(at, branch):
+        total = tokens[at].astype(F32) + branch
+        inv = lax.rsqrt(jnp.mean(total * total, -1, keepdims=True) + EPSILON)
+        hidden[at] = total
+        inverse[at] = inv
+        normed[at] = (total * inv * gain[...].astype(F32)).astype(BF16)
+
     load()
     greet(tuple(place()[3].values()))
     first()
     second()
-    finish()
-
-
-def scatter_products(*group):
-    operands, scratch, total = scatter_scratch(group)
+    finish(store)
+
+
+def middle_back_kernel(windows, *refs):
+    count = len(windows)
+    lefts, rights, refs = refs[:count], refs[count : 2 * count], refs[2 * count :]
+    hidden, inverse, gain, cotangent, factor, dhidden, dbranch, gain_grad, *scratch = refs
+    load, first, second, finish = scatter_steps(windows, lefts, rights, scratch)
+    gain_grad[...] = jnp.zeros_like(gain_grad)
+
+    def store(at, grad):
+        state, inv = hidden[at], inverse[at]
+        gain_grad[...] += jnp.sum(grad * state * inv, 0, keepdims=True)
+        upstream = cotangent[at].astype(F32) * factor[...]
+        total = upstream + norm_back(grad, state, inv, gain[...].astype(F32))
+        dhidden[at] = total
+        dbranch[at] = total.astype(BF16)
+
+    load()
+    greet(tuple(place()[3].values()))
+    first()
+    second()
+    finish(store)
+
+
+def scatter_products(kernel, number, extras, outs, *group):
+    operands, scratch, _ = scatter_scratch(group)
+    whole = pl.BlockSpec(memory_space=pltpu.VMEM)
     return pl.pallas_call(
-        functools.partial(scatter_kernel, [item[2] for item in group]),
-        out_shape=total,
-        in_specs=[pl.BlockSpec(memory_space=pl.ANY)] * len(operands),
-        out_specs=pl.BlockSpec(memory_space=pltpu.VMEM),
+        functools.partial(kernel, [item[2] for item in group]),
+        out_shape=outs,
+        in_specs=[pl.BlockSpec(memory_space=pl.ANY)] * len(operands) + [whole] * len(extras),
+        out_specs=(whole,) * len(outs),
         scratch_shapes=scratch,
         compiler_params=pltpu.CompilerParams(
-            collective_id=10 + sum(item[0].shape[1] for item in group) // 256, has_side_effects=True
+            collective_id=number, has_side_effects=True, vmem_limit_bytes=VMEM_BYTES
         ),
         cost_estimate=micros(48),
         name="scatter_products",
-    )(*operands)
-
-
-def line_scatter_steps(grad_ref, own, from_edge, from_middle, inward, load_sem, send, recv):
+    )(*operands, *extras)
+
+
+def gather_beside_kernel(windows, tile, shard_ref, *refs):
+    count = len(windows)
+    lefts, rights, refs = refs[:count], refs[count : 2 * count], refs[2 * count :]
+    mid, low, dgu, act, out_ref, sums_ref, grad_ref, *scratch = refs
+    size = 2 * count + 5
+    products, (mid_buf, low_buf, dgu_vmem, act_vmem, total, tile_sem, side_sem), sems = (
+        scratch[:size], scratch[size : size + 7], scratch[size + 7 :],
+    )
+    load, ready, product, cores, crossed = product_steps(
+        windows, lefts, rights, products[:count], products[count : 2 * count], sums_ref,
+        *products[2 * count :],
+    )
+    begin, forward, across, finish = gather_steps(shard_ref, out_ref, *sems)
+    tiles = mid.shape[0] // tile
+    sides = [
+        pltpu.make_async_copy(dgu, dgu_vmem, side_sem.at[0]),
+        pltpu.make_async_copy(act, act_vmem, side_sem.at[1]),
+    ]
+
+    def tile_copies(t):
+        rows, slot = pl.ds(t * tile, tile), t % 2
+        return [
+            pltpu.make_async_copy(source.at[rows], buffer.at[slot], tile_sem.at[i, slot])
+            for i, (source, buffer) in enumerate(((mid, mid_buf), (low, low_buf)))
+        ]
+
+    def grads(t):
+        for copy in tile_copies(t):
+            copy.wait()
+        rows, slot = pl.ds(t * tile, tile), t % 2
+        add_products(t, total, 0, mid_buf.at[slot], dgu_vmem[rows])
+        add_products(t, total, dgu_vmem.shape[1], low_buf.at[slot], act_vmem[rows])
+        if t + 2 < tiles:
+            for copy in tile_copies(t + 2):
+                copy.start()
+
+    load()
+    greet(tuple(place()[3].values()))
+    begin()
+    for copy in (*sides, *tile_copies(0), *tile_copies(1)):
+        copy.start()
+    ready()
+    for i in range(4):
+        product(i)
+    forward()
+    for copy in sides:
+        copy.wait()
+    cores(0)
+    cores(1)
+    for t in range(tiles // 2):
+        grads(t)
+    across()
+    for k in range(2, 5):
+        cores(k)
+    for t in range(tiles // 2, tiles):
+        grads(t)
+
+    @pl.loop(0, total.shape[0] // 256)
+    def _(m):
+        at = pl.ds(m * 256, 256)
+        grad_ref[at] = total[at].astype(BF16)
+
+    crossed()
+    finish()
+
+
+def gather_beside(shard, group, mid, low, dgu, act, tile=512):
+    rows, width = shard.shape
+    operands = [item[0] for item in group] + [item[1] for item in group] + [mid, low, dgu, act]
+    cols = dgu.shape[1] + act.shape[1]
+    gathered, sums, grad = pl.pallas_call(
+        functools.partial(gather_beside_kernel, [item[2] for item in group], tile),
+        out_shape=(
+            jax.ShapeDtypeStruct((2, 2, 2, rows, width), shard.dtype),
+            jax.ShapeDtypeStruct((4, rows, width), BF16),
+            jax.ShapeDtypeStruct((width, cols), BF16),
+        ),
+        in_specs=[
+            pl.BlockSpec(memory_space=pltpu.VMEM),
+            *[pl.BlockSpec(memory_space=pl.ANY)] * len(operands),
+        ],
+        out_specs=(
+            pl.BlockSpec(memory_space=pl.ANY),
+            pl.BlockSpec(memory_space=pltpu.VMEM),
+            pl.BlockSpec(memory_space=pltpu.VMEM),
+        ),
+        scratch_shapes=[
+            *product_scratch(group, own=False),
+            pltpu.VMEM((2, tile, width), BF16),
+            pltpu.VMEM((2, tile, width), BF16),
+            pltpu.VMEM(dgu.shape, BF16),
+            pltpu.VMEM(act.shape, BF16),
+            pltpu.VMEM((width, cols), F32),
+            pltpu.SemaphoreType.DMA((2, 2)),
+            pltpu.SemaphoreType.DMA((2,)),
+            *GATHER_SEMAPHORES,
+        ],
+        compiler_params=pltpu.CompilerParams(
+            collective_id=6, has_side_effects=True, vmem_limit_bytes=VMEM_BYTES
+        ),
+        cost_estimate=micros(44),
+        name="gather_beside",
+    )(shard, *operands)
+    return gathered.reshape(8 * rows, width), sums, grad
+
+
+def line_scatter_steps(grad_ref, own, from_edge, from_middle, inward, load_sem, send, recv, part, which):
     z = lax.axis_index("z")
-    rows = own.shape[1]
+    rows, half = own.shape[1], own.shape[1] // 2
     pair, middle = z + 1 - 2 * lax.rem(z, 2), 3 - z
     inner = (z == 1) | (z == 2)
     edge = jnp.logical_not(inner)
     far = middle + 1 - 2 * lax.rem(middle, 2)
+    first = pl.multiple_of(which * half, half)
+    span = pl.ds(first, half)
 
     def block(index):
-        return grad_ref.at[pl.ds(pl.multiple_of(index * rows, rows), rows)]
+        return grad_ref.at[pl.ds(pl.multiple_of(index * rows + first, half), half)]
 
     def remote(index, source, target, peer):
         return pltpu.make_async_remote_copy(
             src_ref=source,
             dst_ref=target,
-            send_sem=send.at[index],
-            recv_sem=recv.at[index],
+            send_sem=send.at[6 * part + index],
+            recv_sem=recv.at[6 * part + index],
             device_id={"z": peer},
             device_id_type=MESH,
         )
 
     indices = (far, middle, pair, z)
     loads = [
-        pltpu.make_async_copy(block(index), own.at[i], load_sem.at[i])
+        pltpu.make_async_copy(block(index), own.at[i, span], load_sem.at[4 * part + i])
         for i, index in enumerate(indices)
     ]
-    edge_far = remote(0, own.at[1], from_edge.at[0], pair)
-    edge_near = remote(1, own.at[0], from_edge.at[1], pair)
-    edge_pair = remote(2, own.at[2], from_edge.at[2], pair)
-    inner_far = remote(3, own.at[0], from_middle.at[0], middle)
-    inner_near = remote(4, own.at[1], from_middle.at[1], middle)
-    outward = remote(5, own.at[2], inward, pair)
+    edge_far = remote(0, own.at[1, span], from_edge.at[0, span], pair)
+    edge_near = remote(1, own.at[0, span], from_edge.at[1, span], pair)
+    edge_pair = remote(2, own.at[2, span], from_edge.at[2, span], pair)
+    inner_far = remote(3, own.at[0, span], from_middle.at[0, span], middle)
+    inner_near = remote(4, own.at[1, span], from_middle.at[1, span], middle)
+    outward = remote(5, own.at[2, span], inward.at[span], pair)
     step = 128
 
     def add_into(target, other):
-        @pl.loop(0, rows // step)
+        @pl.loop(0, half // step)
         def _(i):
-            at = pl.ds(i * step, step)
+            at = pl.ds(first + i * step, step)
             target[at] = (target[at].astype(F32) + other[at].astype(F32)).astype(target.dtype)
 
     def load():
@@ -632,7 +874,7 @@
             for copy in (edge_far, edge_near, edge_pair):
                 copy.wait_send()
 
-    return load, begin, second, third, finish, (pair, middle, inner)
+    return load, begin, second, third, finish
 
 
 def total_steps(near, far, near_send, near_recv, far_send, far_recv):
@@ -690,44 +932,44 @@
 def tail_kernel(windows, *refs):
     count = len(windows)
     lefts, rights, refs = refs[:count], refs[count : 2 * count], refs[2 * count :]
-    grad_ref, tokens_ref, inverse_ref, *refs = refs
+    grad_ref, tokens_ref, inverse_ref, dhidden_ref, gain_ref, *refs = refs
     gains, (out_ref, mine_ref, theirs_ref, total_ref), scratch = refs[:3], refs[3:7], refs[7:]
-    size = 2 * count + 10
-    load, first, second, finish = scatter_steps(
-        windows, lefts, rights, out_ref, scratch[:count], scratch[count : 2 * count], *scratch[2 * count : size]
-    )
+    size = 2 * count + 12
+    load, first, second, finish = scatter_steps(windows, lefts, rights, scratch[:size])
     line, (swap_sem,), total = scratch[size : size + 7], scratch[size + 7 : size + 8], scratch[size + 8 :]
-    line_load, line_begin, line_second, line_third, line_finish, peers = line_scatter_steps(grad_ref, *line)
     near, far = total[:2]
     total_begin, total_second, total_finish, here, others, levels = total_steps(*total)
     y = lax.axis_index("y")
+    lines = [line_scatter_steps(grad_ref, *line, part, which) for part, which in ((0, 1 - y), (1, y))]
     load()
-    line_load()
+    for steps in lines:
+        steps[0]()
     width = out_ref.shape[1]
     near[here, :, pl.ds(width, width)] = gains[0][...]
     head = gains[1].shape[1]
     near[here, :, pl.ds(2 * width, head)] = gains[1][...]
     near[here, :, pl.ds(2 * width + head, head)] = gains[2][...]
     greet(others + levels)
-    line_begin()
+    for steps in lines:
+        steps[1]()
     first()
-    line_second()
+    lines[0][2]()
     second()
-    line_third()
-    finish()
-    rows, step = out_ref.shape[0], 32
-
-    def gain_part(i, part):
-        at = pl.ds(i * step, step)
-        return part + jnp.sum(
-            out_ref[at] * tokens_ref[at].astype(F32) * inverse_ref[at], 0, keepdims=True
-        )
-
-    near[here, :, pl.ds(0, width)] = lax.fori_loop(
-        0, rows // step, gain_part, jnp.zeros((1, width), F32)
-    )
+    lines[0][3]()
+    lines[1][2]()
+    gain_in = near.at[here, :, pl.ds(0, width)]
+    gain_in[...] = jnp.zeros((1, width), F32)
+
+    def store(at, grad):
+        x, inv = tokens_ref[at].astype(F32), inverse_ref[at]
+        gain_in[...] += jnp.sum(grad * x * inv, 0, keepdims=True)
+        back = norm_back(grad, x, inv, gain_ref[...].astype(F32))
+        out_ref[at] = (dhidden_ref[at] + back).astype(BF16)
+
+    finish(store)
     total_begin()
-    line_finish()
+    lines[1][3]()
+    lines[0][4]()
     summed = line[0].at[3]
     half = theirs_ref.shape[0]
     swap = pltpu.make_async_remote_copy(
@@ -740,12 +982,13 @@
     )
     swap.start()
     total_second()
+    lines[1][4]()
     mine_ref[...] = summed[pl.ds(pl.multiple_of(y * half, half), half)]
     total_ref[...] = total_finish()
     swap.wait()
 
 
-def tail(group, grad, tokens, inverse, gains):
+def tail(group, grad, tokens, inverse, dhidden, gain, gains):
     operands, scratch, total = scatter_scratch(group)
     rows, cols = grad.shape[0] // 4, grad.shape[1]
     length = 2 * total.shape[1] + 2 * gains[1].size
@@ -755,12 +998,17 @@
     dma = pltpu.SemaphoreType.DMA
     return pl.pallas_call(
         functools.partial(tail_kernel, [item[2] for item in group]),
-        out_shape=(total, half, half, jax.ShapeDtypeStruct((1, length), F32)),
-        in_specs=[pl.BlockSpec(memory_space=pl.ANY)] * (len(operands) + 1) + [whole] * 5,
+        out_shape=(
+            jax.ShapeDtypeStruct(total.shape, BF16),
+            half,
+            half,
+            jax.ShapeDtypeStruct((1, length), F32),
+        ),
+        in_specs=[pl.BlockSpec(memory_space=pl.ANY)] * (len(operands) + 1) + [whole] * 7,
         out_specs=(whole,) * 4,
         scratch_shapes=[
             *scratch,
-            block(4), block(3), block(2), pltpu.VMEM((rows, cols), BF16), dma((4,)), dma((6,)), dma((6,)),
+            block(4), block(3), block(2), pltpu.VMEM((rows, cols), BF16), dma((8,)), dma((12,)), dma((12,)),
             dma((2,)),
             pltpu.VMEM((8, 1, length), F32), pltpu.VMEM((4, 1, length), F32), dma((7,)), dma((7,)), dma((3,)), dma((3,)),
         ],
@@ -769,7 +1017,7 @@
         ),
         cost_estimate=micros(52),
         name="tail",
-    )(*operands, grad, tokens, inverse, *(gain.reshape(1, -1) for gain in gains))
+    )(*operands, grad, tokens, inverse, dhidden, gain.reshape(1, -1), *(gain.reshape(1, -1) for gain in gains))
 
 
 def swap_y(value):
@@ -978,6 +1226,9 @@
     def _(m):
         at = pl.ds(pl.multiple_of(m * tile, tile), tile)
         part = dot_tn(left_ref[:, at], right)
+        if isinstance(step, int):
+            total_ref[at, cols] = total_ref[at, cols] + part if step else part
+            return
 
         @pl.when(step == 0)
         def _():
@@ -1040,7 +1291,7 @@
     )(normed, branch, weights, attended, gate, mixed)
 
 
-def feed_kernel(count, tile, mid_ref, low_ref, w_ref, act_ref, dgu_ref, grad_ref, total_ref):
+def feed_kernel(count, tile, mid_ref, low_ref, w_ref, act_ref, dgu_ref, *grads):
     step = pl.program_id(0)
 
     @pl.loop(0, count // tile)
@@ -1057,12 +1308,14 @@
         dgu_ref[:, at] = (dact * up * sigma * (1.0 + gate * (1.0 - sigma))).astype(BF16)
         dgu_ref[:, after] = (dact * silu).astype(BF16)
 
-    add_products(step, total_ref, 0, mid_ref, dgu_ref[...])
-    add_products(step, total_ref, 2 * count, low_ref, act_ref[...])
-    store_low(step, total_ref, grad_ref)
-
-
-def feed_forward(mid, low, weights, block=1024):
+    if grads:
+        grad_ref, total_ref = grads
+        add_products(step, total_ref, 0, mid_ref, dgu_ref[...])
+        add_products(step, total_ref, 2 * count, low_ref, act_ref[...])
+        store_low(step, total_ref, grad_ref)
+
+
+def feed_forward(mid, low, weights, grads, block):
     rows, width = mid.shape
     count = weights.shape[1] // 3
     part = lambda cols: pl.BlockSpec((block, cols), lambda i: (i, 0))
@@ -1072,43 +1325,42 @@
         out_shape=(
             jax.ShapeDtypeStruct((rows, count), BF16),
             jax.ShapeDtypeStruct((rows, 2 * count), BF16),
-            jax.ShapeDtypeStruct(weights.shape, BF16),
+            *[jax.ShapeDtypeStruct(weights.shape, BF16)] * grads,
         ),
         grid=(rows // block,),
         in_specs=[part(width), part(width), whole],
-        out_specs=(part(count), part(2 * count), whole),
-        scratch_shapes=[pltpu.VMEM(weights.shape, F32)],
+        out_specs=(part(count), part(2 * count), *[whole] * grads),
+        scratch_shapes=[pltpu.VMEM(weights.shape, F32)] * grads,
         compiler_params=pltpu.CompilerParams(vmem_limit_bytes=VMEM_BYTES),
-        cost_estimate=micros(40),
+        cost_estimate=micros(41 if grads else 14),
         name="feed_forward",
     )(mid, low, weights)
 
 
 def attend_back_kernel(
-    heads, head, block, windows, raw_ref, up_ref, log_ref, qg_ref, kg_ref, cos_ref, sin_ref, *refs
+    heads, head, block, raw_ref, up_ref, log_ref, qg_ref, kg_ref, cos_ref, sin_ref, sums_ref,
+    out_ref, qg_out, kg_out, sum_ref, key_ref, value_ref, dkey_ref, dvalue_ref, own, load_sem, *scratch,
 ):
-    count = len(windows)
-    lefts, rights, refs = refs[:count], refs[count : 2 * count], refs[2 * count :]
-    out_ref, qg_out, kg_out, sum_ref, key_ref, value_ref, dkey_ref, dvalue_ref, *scratch = refs
     seq, step, steps = pl.program_id(0), pl.program_id(1), pl.num_programs(1)
     tick = seq * steps + step
     scaling = head**-0.5
     at = heads * head
     blocks = raw_ref.shape[0] // block
-    load, first, second, finish = scatter_steps(
-        windows, lefts, rights, sum_ref, scratch[:count], scratch[count : 2 * count], *scratch[2 * count :]
-    )
+    diag_x, diag_y, x_low, y_high, second, finish = axis_steps(own, *scratch)
 
     @pl.when(tick == 0)
     def _():
-        load()
-        greet(tuple(place()[3].values()))
+        load = pltpu.make_async_copy(sums_ref, own, load_sem)
+        load.start()
+        device = place()[3]
+        greet((device["y"], device["x"]))
+        load.wait()
+        for copy in (diag_x, diag_y, x_low, y_high):
+            copy.start()
         qg_out[...] = jnp.zeros_like(qg_out)
         kg_out[...] = jnp.zeros_like(kg_out)
 
-    for i, part in enumerate(first.parts):
-        pl.when(tick == i)(part)
-    pl.when(tick == 5)(second)
+    pl.when(tick == 4)(second)
 
     @pl.when(step == 0)
     def _():
@@ -1158,18 +1410,23 @@
         out_ref[:, at + head :] = dvalue_ref[...].astype(BF16)
         kg_out[...] += part
 
-    pl.when(tick == pl.num_programs(0) * steps - 1)(finish)
+    @pl.when(tick == pl.num_programs(0) * steps - 1)
+    def _():
+        def store(rows, value):
+            sum_ref[rows] = value
+
+        finish(store)
 
 
 def attend_back(
-    raw, upstream, logs, query_gain, key_gain, cosine, sine, heads, head, length, group, block=256
+    raw, upstream, logs, query_gain, key_gain, cosine, sine, sums, heads, head, length, block=256
 ):
     rows = raw.shape[0]
-    operands, scratch, total = scatter_scratch(group)
+    total = jax.ShapeDtypeStruct(sums.shape[1:], F32)
     seqs, steps = rows // length, length // block
     whole = lambda shape: pl.BlockSpec(shape, lambda s, i: (0,) * len(shape))
     return pl.pallas_call(
-        functools.partial(attend_back_kernel, heads, head, block, [item[2] for item in group]),
+        functools.partial(attend_back_kernel, heads, head, block),
         out_shape=(
             jax.ShapeDtypeStruct(raw.shape, BF16),
             jax.ShapeDtypeStruct((1, head), F32),
@@ -1185,7 +1442,7 @@
             whole((1, head)),
             whole((length, head)),
             whole((length, head)),
-            *[pl.BlockSpec(memory_space=pl.ANY)] * len(operands),
+            pl.BlockSpec(memory_space=pl.ANY),
         ],
         out_specs=(
             pl.BlockSpec((length, raw.shape[1]), lambda s, i: (s, 0)),
@@ -1198,14 +1455,16 @@
             pltpu.VMEM((length, head), BF16),
             pltpu.VMEM((length, head), F32),
             pltpu.VMEM((length, head), F32),
-            *scratch,
+            pltpu.VMEM(sums.shape, BF16),
+            pltpu.SemaphoreType.DMA,
+            *axis_scratch(*sums.shape[1:]),
         ],
         compiler_params=pltpu.CompilerParams(
             collective_id=5, has_side_effects=True, vmem_limit_bytes=VMEM_BYTES
         ),
-        cost_estimate=micros(48),
+        cost_estimate=micros(40),
         name="attend_back",
-    )(raw, upstream, logs, query_gain, key_gain, cosine, sine, *operands)
+    )(raw, upstream, logs, query_gain, key_gain, cosine, sine, sums)
 
 
 def attention_weights(query_proj, key_proj, value_proj, gating_proj, output_proj):
@@ -1526,37 +1785,21 @@
     q_cols = query_proj.shape[1] // 2
     ff_cols = swiglu_gate.shape[1] // 2
     heads = q_cols // head
-    cosine, sine = rope_tables(jnp.arange(full_len, dtype=jnp.int32), head)
-    cos_rows = jnp.concatenate([cosine, cosine], 1)
-    sin_rows = jnp.concatenate([-sine, sine], 1)
-
-    inputs = tokens.reshape(rows, width).astype(F32)
-    inverse_in = lax.rsqrt(jnp.mean(inputs * inputs, -1, keepdims=True) + EPSILON)
-    gain_in = attention_gain.astype(F32)
-    normed = (inputs * inverse_in * gain_in).astype(BF16)
-
-    domain_table = (
-        domain_ids[:, None] == jnp.arange(domain_counts.shape[0], dtype=jnp.int32)[None, :]
-    ).astype(F32)
-    ratio = (
-        domain_numer.astype(F32) / domain_denom.astype(F32) * LENGTH / domain_counts.astype(F32)
-    )
-    factor = jnp.sum(domain_table * ratio[None, :], 1)
-    upstream = (cotangent.astype(F32) * factor[:, None, None]).reshape(rows, width)
-    out_low = upstream.astype(BF16)
-
-    down_t, output_t = swiglu_down.T, output_proj.T
     split, rest = ff_cols * 2 // 3, ff_cols - ff_cols * 2 // 3
-    (rows_go,) = swap_weights([(gating_proj, 0, q_cols), (output_t, 0, q_cols)])
-    w_go = gather_rows(rows_go)
-    feed = (swiglu_gate, swiglu_up, down_t)
-    normed, out_low, cos_rows, sin_rows, rows_go = lax.optimization_barrier(
-        (normed, out_low, cos_rows, sin_rows, rows_go)
-    )
-    normed_all, w_qkv, (rows_first, rows_last) = gather_and_swap(
-        normed,
-        [(query_proj, 0, q_cols), (key_proj, 0, kv_cols), (value_proj, 0, kv_cols)],
-        [(w, 0, split) for w in feed], [(w, split, rest) for w in feed]
+    tokens, cotangent = tokens.reshape(rows, width), cotangent.reshape(rows, width)
+    (
+        normed_all, w_qkv, w_go, rows_first, rows_last, inverse_in, out_low, factor, cos_rows, sin_rows,
+    ) = opening(
+        tokens,
+        cotangent,
+        attention_gain,
+        (domain_ids, domain_counts, domain_numer, domain_denom),
+        (
+            query_proj, key_proj, value_proj, gating_proj, output_proj, swiglu_gate, swiglu_up, swiglu_down,
+        ),
+        split,
+        full_len,
+        head,
     )
     w_first = gather_rows(rows_first)
     w_last = gather_rows(rows_last)
@@ -1565,23 +1808,35 @@
     qkv, attended, logs, gate_sig, mixed, out_all = attend(
         normed_all, w_qkv, w_go, out_low, query_scale, key_scale, cos_rows, sin_rows, heads, head, full_len
     )
-    branch = scatter_products((mixed, w_go, q_cols))
-    hidden = inputs + branch
-    inverse_mid = lax.rsqrt(jnp.mean(hidden * hidden, -1, keepdims=True) + EPSILON)
-    gain_mid = swiglu_gain.astype(F32)
-    normed_mid = (hidden * inverse_mid * gain_mid).astype(BF16)
+    wide, column = jax.ShapeDtypeStruct((rows, width), F32), jax.ShapeDtypeStruct((rows, 1), F32)
+    low = jax.ShapeDtypeStruct((rows, width), BF16)
+    gain_mid = swiglu_gain.reshape(1, -1)
+    hidden, inverse_mid, normed_mid = scatter_products(
+        middle_kernel, 7, (tokens, gain_mid), (wide, column, low), (mixed, w_go, q_cols)
+    )
     mid_all = gather_tokens(normed_mid)
 
-    act_first, dgu_first, grad_first = feed_forward(mid_all, out_all, w_first)
+    act_first, dgu_first, grad_first = feed_forward(mid_all, out_all, w_first, True, 1024)
     part_first = scatter_grads(grad_first)
     w_last, grad_first = lax.optimization_barrier((w_last, grad_first))
-    act_last, dgu_last, grad_last = feed_forward(mid_all, out_all, w_last)
-    dgu_last, grad_last = lax.optimization_barrier((dgu_last, grad_last))
+    act_last, dgu_last = feed_forward(mid_all, out_all, w_last, False, 512)
+    dhidden, dbranch, grad_gain_mid = scatter_products(
+        middle_back_kernel,
+        8,
+        (hidden, inverse_mid, gain_mid, cotangent, factor),
+        (wide, low, jax.ShapeDtypeStruct((1, width), F32)),
+        (dgu_first, w_first, 0),
+        (dgu_last, w_last, 0),
+    )
+    dbranch_all, ffn_sums, grad_last = gather_beside(
+        dbranch,
+        ((act_first, w_first, 2 * split), (act_last, w_last, 2 * rest)),
+        mid_all,
+        out_all,
+        dgu_last,
+        act_last,
+    )
     part_last = scatter_grads(grad_last)
-    dnormed_mid = scatter_products((dgu_first, w_first, 0), (dgu_last, w_last, 0))
-    grad_gain_mid = jnp.sum(dnormed_mid * hidden * inverse_mid, 0)
-    dhidden = upstream + norm_back(dnormed_mid, hidden, inverse_mid, gain_mid)
-    dbranch_all = gather_tokens(dhidden.astype(BF16))
     dbranch_all, part_first = lax.optimization_barrier((dbranch_all, part_first))
 
     theirs_first = their_rows(part_first)
@@ -1591,33 +1846,40 @@
     dattended, theirs_first, grad_go = lax.optimization_barrier((dattended, theirs_first, grad_go))
     part_go = scatter_grads(grad_go)
     dqkv, grad_query_gain, grad_key_gain, ffn_branch = attend_back(
-        qkv, dattended, logs, query_scale, key_scale, cos_rows, sin_rows, heads, head, full_len,
-        ((act_first, w_first, 2 * split), (act_last, w_last, 2 * rest)),
+        qkv, dattended, logs, query_scale, key_scale, cos_rows, sin_rows, ffn_sums, heads, head, full_len
     )
     grad_query_gain, grad_key_gain = grad_query_gain[0], grad_key_gain[0]
+    dqkv, part_last = lax.optimization_barrier((dqkv, part_last))
+    theirs_last = their_rows(part_last)
+    layer_out = (hidden + ffn_branch).astype(BF16)
     grad_qkv = dot_tn(normed_all, dqkv).astype(BF16)
-    dqkv, grad_qkv, part_last = lax.optimization_barrier((dqkv, grad_qkv, part_last))
-    theirs_last = their_rows(part_last)
-    dnormed, mine_qkv, theirs_qkv, totals = tail(
+    plan = [(0, i * split, split, i, 0, i == 2) for i in range(3)]
+    plan += [(1, i * rest, rest, i, split, i == 2) for i in range(3)]
+    grad_gate, grad_up, grad_down = join_grads(
+        (part_first, part_last),
+        (theirs_first, theirs_last),
+        plan,
+        [weight.shape for weight in (swiglu_gate, swiglu_up, swiglu_down)],
+    )
+    grad_qkv, layer_out, grad_gate, grad_up, grad_down = lax.optimization_barrier(
+        (grad_qkv, layer_out, grad_gate, grad_up, grad_down)
+    )
+    input_grad, mine_qkv, theirs_qkv, totals = tail(
         ((dqkv, w_qkv, 0), (dgating, w_go, 0)),
         grad_qkv,
-        tokens.reshape(rows, width),
+        tokens,
         inverse_in,
+        dhidden,
+        attention_gain,
         (grad_gain_mid, grad_query_gain, grad_key_gain),
     )
-    dnormed, part_go = lax.optimization_barrier((dnormed, part_go))
-    input_grad = (dhidden + norm_back(dnormed, inputs, inverse_in, gain_in)).astype(BF16)
-    layer_out = (hidden + ffn_branch).astype(BF16)
-
-    plan = [(0, i * split, split, i, 0, i == 2) for i in range(3)]
-    plan += [(1, i * rest, rest, i, split, i == 2) for i in range(3)]
-    plan += [(2, 0, q_cols, 3, 0, False), (2, q_cols, q_cols, 4, 0, True)]
-    weights = (swiglu_gate, swiglu_up, swiglu_down, gating_proj, output_proj)
-    grad_gate, grad_up, grad_down, grad_gating, grad_output = join_grads(
-        (part_first, part_last, part_go),
-        (theirs_first, theirs_last, their_rows(part_go)),
-        plan,
-        [weight.shape for weight in weights],
+    input_grad, part_go = lax.optimization_barrier((input_grad, part_go))
+    theirs_go = their_rows(part_go)
+    grad_gating, grad_output = join_grads(
+        (part_go,),
+        (theirs_go,),
+        [(0, 0, q_cols, 0, 0, False), (0, q_cols, q_cols, 1, 0, True)],
+        (gating_proj.shape, output_proj.shape),
     )
     widths, starts = (q_cols, kv_cols, kv_cols), (0, q_cols, q_cols + kv_cols)
     *gain_grads, grad_query, grad_key, grad_value = join_last(

time: 574 us -> 553 us (0.963)
  other arithmetic: 22.5 us -> 1.75 us
  Pallas kernels: 499 us -> 492 us
    pallas_call x2 -> x1, Pallas kernels: 81.2 us -> 40.4 us  [gather_tokens(): pl.pallas_call(functools.partial(gather_kernel, True), out_shape=jax.Shap...]
    pallas_call x5, Pallas kernels: 226 us -> 264 us  [the longest x2 98.7 us: scatter_products(): pl.pallas_call(functools.partial(kernel, [item[2] for item in group]), ou...]
    pallas_call x2, Pallas kernels: 64.3 us -> 54 us  [feed_forward(): pl.pallas_call(functools.partial(feed_kernel, count, 256), out_shape=(jax...]
    convert_element_type x7 -> x1, other arithmetic: 7.42 us -> 1.23 us  [per_device(): layer_out = (hidden + ffn_branch).astype(BF16)]
    pallas_call x1, Pallas kernels: 59 us -> 65.1 us  [tail(): pl.pallas_call(functools.partial(tail_kernel, [item[2] for item in group]...]
    reduce_sum x5 -> x0, other arithmetic: 6.09 us -> none  [the longest x1 2.88 us: per_device(): grad_gain_mid = jnp.sum(dnormed_mid * hidden * inverse_mid, 0)]
  transfers between devices with their start and end apart: 9 -> 8, of which waited for: 3 -> 5; matrix products, arithmetic and copies ran while one was open for 7% -> 3% of each run, Pallas kernels for 85% -> 76%
where the time goes in v1:
time: 553 us; the launch traced here: 544 us
  Pallas kernels  492 us (89%)
  between operations  15.1 us (3%)
  waiting for transfers between devices  11.9 us (2%)
  matrix products  9.91 us (2%)
  local copies, waits for them, and re-layouts  7.61 us (1%)
    pallas_call x2, Pallas kernels, scatter_products(): pl.pallas_call(functools.partial(kernel, [item[2] for item in group]), ou...  98.7 us
    pallas_call x1, Pallas kernels, opening(): pl.pallas_call(functools.partial(opening_kernel, pieces), out_shape=(shap...  79.1 us
    pallas_call x1, Pallas kernels, tail(): pl.pallas_call(functools.partial(tail_kernel, [item[2] for item in group]...  65.1 us
    pallas_call x2, Pallas kernels, feed_forward(): pl.pallas_call(functools.partial(feed_kernel, count, 256), out_shape=(jax...  54 us
    pallas_call x1, Pallas kernels, gather_beside(): pl.pallas_call(functools.partial(gather_beside_kernel, [item[2] for item...  43.7 us
    pallas_call x1, Pallas kernels, attend(): pl.pallas_call(functools.partial(attend_kernel, heads, head, block), out_...  42.7 us
    pallas_call x1, Pallas kernels, attend_back(): pl.pallas_call(functools.partial(attend_back_kernel, heads, head, block),...  42.3 us
    pallas_call x1, Pallas kernels, gather_tokens(): pl.pallas_call(functools.partial(gather_kernel, True), out_shape=jax.Shap...  40.4 us
  transfers between devices with their start and end apart: 8, of which 5 were waited for; matrix products, arithmetic and copies ran while one was open for 3% of the time, Pallas kernels for 76%

profile of v1, /device:TPU:0, one launch (start us, length us, event | category | flops | bytes accessed | tf_op | source)
XLA Modules:
  0.0 543.6 jit_solution(14522741090363498252)
XLA Ops:
  7.9 1.3 reshape.85.gain.refs_8_
  9.2 79.1 %opening.1 = (bf16[2,2,2,256,2048]{4,3,2,1,0:T(8,128)(2,1)}, bf16[2048,512]{1,0:T(8,128)(2,1)}, bf16[2048,512]{1,0:T(8,128)(2,1)}, bf16[512,1536]{1,0:T(8,128)(2...) custom-call(bf16[256,2048]{1,0:T(8,128)(2,1)} %bitcast.34, ...), custom_call_target="tpu_custom_call" | custom-call | bytes 264000000 | tf_op jit(solution)/shard_map/opening/pallas_call | solution.py:401
  90.3 42.7 %attend.1 = (f32[2048,512]{1,0:T(8,128)}, f32[2048,256]{1,0:T(8,128)}, f32[2,2048,1]{2,1,0:T(8,128)}, f32[2048,256]{1,0:T(8,128)}, bf16[2048,256]{1,0:T(8,128)(2,1)}, /*index=5*/bf16[2,2,2,256,2048]{4,3,2,1,0:T(8,128)(2,1)}) custom-call(bf16[2048,2048]{1,0:T(8,128)(2,1)} %bitcast.31, bf16[2048,512]{1,0:T(8,128)(2,1)} %get-tuple-element.83.w_ref.refs_2_, ...), custom_call_target="tpu_custom_call" | custom-call | bytes 138600000 | tf_op jit(solution)/shard_map/attend/pallas_call | solution.py:1181
  132.9 46.1 %scatter_products.2 = (f32[256,2048]{1,0:T(8,128)}, f32[256,1]{1,0:T(8,128)}, bf16[256,2048]{1,0:T(8,128)(2,1)}) custom-call(bf16[2048,256]{1,0:T(8,128)(2,1)} %get-tuple-element.89.refs_0_.mixed_ref, bf16[2048,512]{1,0:T(8,128)(2,1)} %get-tuple-element.84.wg_ref.refs_1_.w_ref.refs_3_, bf16[256,2048]{1,0:T(8,128)(2,1)} %bitcast.35, ...), custom_call_target="tpu_custom_call" | custom-call | bytes 158400000 | tf_op jit(solution)/shard_map/scatter_products/pallas_call | solution.py:668
  179.1 40.4 %gather_tokens.1 = bf16[2,2,2,256,2048]{4,3,2,1,0:T(8,128)(2,1)} custom-call(bf16[256,2048]{1,0:T(8,128)(2,1)} %get-tuple-element.90.refs_0_), custom_call_target="tpu_custom_call" | custom-call | bytes 138600000 | tf_op jit(solution)/shard_map/gather_tokens/pallas_call | solution.py:208
  219.6 41.0 %feed_forward.2 = (bf16[2048,512]{1,0:T(8,128)(2,1)}, bf16[2048,1024]{1,0:T(8,128)(2,1)}, bf16[2048,1536]{1,0:T(8,128)(2,1)}) custom-call(bf16[2048,2048]{1,0:T(8,128)(2,1)} %bitcast.25, bf16[2048,2048]{1,0:T(8,128)(2,1)} %bitcast.28, bf16[2048,1536]{1,0:T(8,128)(2,1)} %all-gather.3.cloned.1.call-done.w_ref.refs_2_), custom_call_target="tpu_custom_call" | custom-call | bytes 135300000 | tf_op jit(solution)/shard_map/feed_forward/pallas_call | solution.py:1323
  260.8 5.5 %all-gather.5.cloned.1.call-done.w_ref.refs_3_ = bf16[2048,768]{1,0:T(8,128)(2,1)} async-done(((bf16[512,768]{1,0:T(8,128)(2,1)}), bf16[2048,768]{1,0:T(8,128)(2,1)}) %all-gather.5.cloned.1.call-update) | async-done | bytes 3145744 | tf_op jit(solution)/shard_map/all_gather | solution.py:1035
  266.3 13.0 %feed_forward.3 = (bf16[2048,256]{1,0:T(8,128)(2,1)}, bf16[2048,512]{1,0:T(8,128)(2,1)}) custom-call(bf16[2048,2048]{1,0:T(8,128)(2,1)} %bitcast.26, bf16[2048,2048]{1,0:T(8,128)(2,1)} %bitcast.29, bf16[2048,768]{1,0:T(8,128)(2,1)} %all-gather.5.cloned.1.call-done.w_ref.refs_3_), custom_call_target="tpu_custom_call" | custom-call | bytes 46200000 | tf_op jit(solution)/shard_map/feed_forward/pallas_call | solution.py:1323
  279.3 52.6 %scatter_products.3 = (f32[256,2048]{1,0:T(8,128)}, bf16[256,2048]{1,0:T(8,128)(2,1)}, f32[1,2048]{1,0:T(1,128)}) custom-call(bf16[2048,1024]{1,0:T(8,128)(2,1)} %get-tuple-element.93.refs_0_, bf16[2048,512]{1,0:T(8,128)(2,1)} %get-tuple-element.97.refs_1_.refs_6_, bf16[2048,1536]{1,0:T(8,128)(2,1)} %all-gather.3.cloned.1.call-done.w_ref.refs_2_, ...), custom_call_target="tpu_custom_call" | custom-call | bytes 158400000 | tf_op jit(solution)/shard_map/scatter_products/pallas_call | solution.py:668
  331.9 43.7 %gather_beside.1 = (bf16[2,2,2,256,2048]{4,3,2,1,0:T(8,128)(2,1)}, bf16[4,256,2048]{2,1,0:T(8,128)(2,1)}, bf16[2048,768]{1,0:T(8,128)(2,1)}) custom-call(bf16[256,2048]{1,0:T(8,128)(2,1)} %get-tuple-element.101.shard_ref, bf16[2048,512]{1,0:T(8,128)(2,1)} %get-tuple-element.102.refs_0_, bf16[2048,256]{1,0:T(8,128)(2,1)} %get-tuple-element.103.refs_1_.refs_7_, ...), custom_call_target="tpu_custom_call" | custom-call | bytes 145200000 | tf_op jit(solution)/shard_map/gather_beside/pallas_call | solution.py:752
  375.9 2.1 reduce-scatter.4.cloned.1.call-done.refs_0_
  378.1 1.2 constant_dynamic-slice_fusion.2
  379.3 1.5 collective-permute-start
  380.8 17.6 %gate_back.1 = (bf16[2048,256]{1,0:T(8,128)(2,1)}, bf16[2048,256]{1,0:T(8,128)(2,1)}, bf16[2048,512]{1,0:T(8,128)(2,1)}) custom-call(bf16[2048,2048]{1,0:T(8,128)(2,1)} %bitcast.32, bf16[2048,2048]{1,0:T(8,128)(2,1)} %bitcast.37, bf16[2048,512]{1,0:T(8,128)(2,1)} %get-tuple-element.84.wg_ref.refs_1_.w_ref.refs_3_, ...), custom_call_target="tpu_custom_call" | custom-call | bytes 82500000 | tf_op jit(solution)/shard_map/gate_back/pallas_call | solution.py:1270
  398.7 42.3 %attend_back.1 = (bf16[2048,512]{1,0:T(8,128)(2,1)}, f32[1,128]{1,0:T(1,128)}, f32[1,128]{1,0:T(1,128)}, f32[256,2048]{1,0:T(8,128)}) custom-call(f32[2048,512]{1,0:T(8,128)} %get-tuple-element.88.raw_ref, bf16[2048,256]{1,0:T(8,128)(2,1)} %get-tuple-element.111.up_ref, f32[2,2048,1]{2,1,0:T(8,128)} %get-tuple-element.112.log_ref, ...), custom_call_target="tpu_custom_call" | custom-call | bytes 132000000 | tf_op jit(solution)/shard_map/attend_back/pallas_call | solution.py:1428
  442.1 1.5 collective-permute-start.1
  443.6 9.9 %convolution_convert_fusion.refs_4_ = bf16[2048,512]{1,0:T(8,128)(2,1)} fusion(bf16[2048,2048]{1,0:T(8,128)(2,1)} %bitcast.33, bf16[2048,512]{1,0:T(8,128)(2,1)} %get-tuple-element.116.refs_0_), kind=kOutput, calls=%fused_computation | convolution fusion | flops 4296015872 | bytes 12582912 | tf_op jit(solution)/shard_map/dot_general | solution.py:31
  453.5 1.2 add_convert_fusion
  455.5 4.5 join_grads.2
  460.0 65.1 %tail.1 = (bf16[256,2048]{1,0:T(8,128)(2,1)}, bf16[256,512]{1,0:T(8,128)(2,1)}, bf16[256,512]{1,0:T(8,128)(2,1)}, f32[1,4352]{1,0:T(1,128)}) custom-call(bf16[2048,512]{1,0:T(8,128)(2,1)} %get-tuple-element.116.refs_0_, bf16[2048,256]{1,0:T(8,128)(2,1)} %get-tuple-element.124.refs_1_, bf16[2048,512]{1,0:T(8,128)(2,1)} %get-tuple-element.83.w_ref.refs_2_, ...), custom_call_target="tpu_custom_call" | custom-call | bytes 171600000 | tf_op jit(solution)/shard_map/tail/pallas_call | solution.py:999
  526.2 1.4 collective-permute-start.2
  527.6 2.1 join_last.1
  529.7 3.1 collective-permute-done.2.refs_1_
  533.5 2.2 join_grads.3
  (38 shorter events, 7.4 us)
Async XLA Ops:
  7.2 212.4 %all-gather.3.cloned.1.call-start = ((), (), s32[]{:S(2)}) async-start(), calls=%async_computation.3 | async-start | bytes 7864320 | tf_op jit(solution)/shard_map/all_gather | solution.py:1035
  88.3 0.9 copy-start.6
  88.3 1.5 copy-start.7
  88.3 1.5 copy-start.8
  88.3 178.0 %all-gather.5.cloned.1.call-start = ((), (), s32[]{:S(2)}) async-start(), calls=%async_computation.4 | async-start | bytes 3932160 | tf_op jit(solution)/shard_map/all_gather | solution.py:1035
  89.1 289.0 %reduce-scatter.4.cloned.1.call-start = ((), (), s32[]{:S(2)}) async-start(), calls=%async_computation.5 | async-start | bytes 7864320 | tf_op jit(solution)/shard_map/reduce_scatter | solution.py:1039
  260.6 180.4 %reduce-scatter.6.cloned.1.call-start = ((), (), s32[]{:S(2)}) async-start(), calls=%async_computation.6 | async-start | bytes 3932160 | tf_op jit(solution)/shard_map/reduce_scatter | solution.py:1039
  375.7 149.5 %reduce-scatter.8.cloned.1.call-start = ((), (), s32[]{:S(2)}) async-start(), calls=%async_computation.7 | async-start | bytes 2621440 | tf_op jit(solution)/shard_map/reduce_scatter | solution.py:1039
  379.3 19.4 %collective-permute-start = (bf16[256,1536]{1,0:T(8,128)(2,1)S(1)}, bf16[256,1536]{1,0:T(8,128)(2,1)S(1)}, u32[]{:S(2)}, u32[]{:S(2)}) collective-permute-start(bf16[256,1536]{1,0:T(8,128)(2,1)S(1)} %constant_dynamic-slice_fusion.2), channel_id=1, source_target_pairs={{0,4},{4,0},{1,5},{5,1},{2,6},{6,2},{3,7},{7,3},{8,12},{12,8},{9,1... | collective-permute-start | bytes 2359304 | tf_op jit(solution)/shard_map/ppermute | solution.py:1024
  398.6 42.3 %copy-start.3 = (bf16[256,1536]{1,0:T(8,128)(2,1)}, bf16[256,1536]{1,0:T(8,128)(2,1)S(1)}, u32[]{:S(2)}) copy-start(bf16[256,1536]{1,0:T(8,128)(2,1)S(1)} %collective-permute-done.refs_2_) | copy-start | bytes 2359300
  442.1 11.5 %copy-start = (f32[256,2048]{1,0:T(8,128)S(1)}, f32[256,2048]{1,0:T(8,128)}, u32[]{:S(2)}) copy-start(f32[256,2048]{1,0:T(8,128)} %get-tuple-element.98.refs_4_) | copy-start | bytes 6291460
  442.1 11.5 %copy-start.1 = (f32[256,2048]{1,0:T(8,128)S(1)}, f32[256,2048]{1,0:T(8,128)}, u32[]{:S(2)}) copy-start(f32[256,2048]{1,0:T(8,128)} %get-tuple-element.117) | copy-start | bytes 6291460
  442.1 12.7 %collective-permute-start.1 = (bf16[256,768]{1,0:T(8,128)(2,1)S(1)}, bf16[256,768]{1,0:T(8,128)(2,1)S(1)}, u32[]{:S(2)}, u32[]{:S(2)}) collective-permute-start(bf16[256,768]{1,0:T(8,128)(2,1)S(1)} %constant_dynamic-slice_fusion.1), channel_id=1, source_target_pairs={{0,4},{4,0},{1,5},{5,1},{2,6},{6,2},{3,7},{7,3},{8,12},{12,8},{9,1... | collective-permute-start | bytes 1179656 | tf_op jit(solution)/shard_map/ppermute | solution.py:1024
  454.8 0.7 copy-start.4
  525.1 10.5 %copy-start.2 = (bf16[256,2048]{1,0:T(8,128)(2,1)S(1)}, bf16[256,2048]{1,0:T(8,128)(2,1)}, u32[]{:S(2)}) copy-start(bf16[256,2048]{1,0:T(8,128)(2,1)} %get-tuple-element.133) | copy-start | bytes 3145732
  526.2 6.6 %collective-permute-start.2 = (bf16[256,512]{1,0:T(8,128)(2,1)S(1)}, bf16[256,512]{1,0:T(8,128)(2,1)S(1)}, u32[]{:S(2)}, u32[]{:S(2)}) collective-permute-start(bf16[256,512]{1,0:T(8,128)(2,1)S(1)} %constant_dynamic-slice_fusion), channel_id=1, source_target_pairs={{0,4},{4,0},{1,5},{5,1},{2,6},{6,2},{3,7},{7,3},{8,12},{12,8},{9,1... | collective-permute-start | bytes 786440 | tf_op jit(solution)/shard_map/ppermute | solution.py:1024
  532.8 0.7 copy-start.5
Sparse Core Ops, SparseCore 0:
  88.4 114.5 all-gather.2
  204.6 61.7 all-gather.4
  268.6 109.3 reduce-scatter.3
  380.2 60.7 reduce-scatter.5
  443.2 61.3 reduce-scatter.7

commit v2 on v1

--- a/solution.py
+++ b/solution.py
@@ -323,7 +323,7 @@
         x = tokens[at].astype(F32)
         inv = lax.rsqrt(jnp.mean(x * x, -1, keepdims=True) + EPSILON)
         inverse[at] = inv
-        normed[at] = (x * inv * gain[...].astype(F32)).astype(BF16)
+        normed[at] = (x * inv * gain[...].astype(F32).reshape(1, -1)).astype(BF16)
 
     def weigh(i):
         at = pl.ds(i * step, step)
@@ -428,7 +428,7 @@
     )(
         tokens,
         cotangent,
-        gain.reshape(1, -1),
+        gain,
         *(domain.reshape(1, -1) for domain in domains),
         jnp.asarray(turns),
         *weights,
@@ -447,7 +447,7 @@
     y, x, c, device = place()
     remote = remote_copies(send, recv, device)
     rows, width = own.shape[1:]
-    half, both, tile = rows // 2, 2 * rows, 512
+    half, both, tile = rows // 2, 2 * rows, 256
     targets = ((1 - y, 1 - x), (1 - y, x), (y, 1 - x), (y, x))
     pieces = ((0, 0, half), (0, half, half), (1, 0, rows), (2, 0, rows), (3, 0, rows))
     count = len(lefts)
@@ -699,21 +699,11 @@
     ]
 
     def tile_copies(t):
-        rows, slot = pl.ds(t * tile, tile), t % 2
+        rows, slot = pl.ds(pl.multiple_of(t * tile, tile), tile), lax.rem(t, 2)
         return [
             pltpu.make_async_copy(source.at[rows], buffer.at[slot], tile_sem.at[i, slot])
             for i, (source, buffer) in enumerate(((mid, mid_buf), (low, low_buf)))
         ]
-
-    def grads(t):
-        for copy in tile_copies(t):
-            copy.wait()
-        rows, slot = pl.ds(t * tile, tile), t % 2
-        add_products(t, total, 0, mid_buf.at[slot], dgu_vmem[rows])
-        add_products(t, total, dgu_vmem.shape[1], low_buf.at[slot], act_vmem[rows])
-        if t + 2 < tiles:
-            for copy in tile_copies(t + 2):
-                copy.start()
 
     load()
     greet(tuple(place()[3].values()))
@@ -728,13 +718,25 @@
         copy.wait()
     cores(0)
     cores(1)
-    for t in range(tiles // 2):
-        grads(t)
-    across()
-    for k in range(2, 5):
-        cores(k)
-    for t in range(tiles // 2, tiles):
-        grads(t)
+
+    @pl.loop(0, tiles)
+    def _(t):
+        for copy in tile_copies(t):
+            copy.wait()
+        rows, slot = pl.ds(pl.multiple_of(t * tile, tile), tile), lax.rem(t, 2)
+        add_products(t, total, 0, mid_buf.at[slot], dgu_vmem.at[rows])
+        add_products(t, total, dgu_vmem.shape[1], low_buf.at[slot], act_vmem.at[rows])
+
+        @pl.when(t + 2 < tiles)
+        def _():
+            for copy in tile_copies(t + 2):
+                copy.start()
+
+        @pl.when(t == tiles // 2 - 1)
+        def _():
+            across()
+            for k in range(2, 5):
+                cores(k)
 
     @pl.loop(0, total.shape[0] // 256)
     def _(m):
@@ -1143,20 +1145,26 @@
     raw_ref[...] = dot_nn(normed_ref[...], w_ref[...])
     here = pl.ds(pl.multiple_of(step * block, block), block)
     cosine, sine = cos_ref[here], sin_ref[here]
+
+    @pl.when(tick == 0)
+    def _():
+        key_ref[...] = jnp.zeros_like(key_ref)
+        value_ref[...] = jnp.zeros_like(value_ref)
+
     key_ref[here] = normed_rope(raw_ref[:, at : at + head], kg_ref[...], cosine, sine)
     value_ref[here] = raw_ref[:, at + head :].astype(BF16)
 
-    for i in range(key_ref.shape[0] // block):
-
-        @pl.when(step == i)
+    for i in range(0, key_ref.shape[0] // block, 2):
+
+        @pl.when(step // 2 == i // 2)
         def _():
-            seen = pl.ds(0, (i + 1) * block)
+            seen = pl.ds(0, (i + 2) * block)
 
             @pl.loop(0, heads)
             def _(h):
                 cols = pl.ds(pl.multiple_of(h * head, head), head)
                 query = normed_rope(raw_ref[:, cols], qg_ref[...], cosine, sine)
-                scores = causal_scores(query, key_ref[seen], i * block, scaling)
+                scores = causal_scores(query, key_ref[seen], step * block, scaling)
                 highest = jnp.max(scores, -1, keepdims=True)
                 exp_vals = jnp.exp(scores - highest)
                 total = jnp.sum(exp_vals, -1, keepdims=True)
@@ -1219,24 +1227,25 @@
     return *outs, gathered.reshape(rows, width)
 
 
-def add_products(step, total_ref, start, left_ref, right, tile=1024):
-    cols = slice(start, start + right.shape[1])
+def add_products(step, total_ref, start, left_ref, right_ref, tile=1024):
+    wide = min(512, right_ref.shape[1])
 
     @pl.loop(0, left_ref.shape[1] // tile)
     def _(m):
         at = pl.ds(pl.multiple_of(m * tile, tile), tile)
-        part = dot_tn(left_ref[:, at], right)
-        if isinstance(step, int):
-            total_ref[at, cols] = total_ref[at, cols] + part if step else part
-            return
-
-        @pl.when(step == 0)
-        def _():
-            total_ref[at, cols] = part
-
-        @pl.when(step > 0)
-        def _():
-            total_ref[at, cols] += part
+
+        @pl.loop(0, right_ref.shape[1] // wide)
+        def _(n):
+            cols = pl.ds(pl.multiple_of(start + n * wide, wide), wide)
+            part = dot_tn(left_ref[:, at], right_ref[:, pl.ds(pl.multiple_of(n * wide, wide), wide)])
+
+            @pl.when(step == 0)
+            def _():
+                total_ref[at, cols] = part
+
+            @pl.when(step > 0)
+            def _():
+                total_ref[at, cols] += part
 
 
 def store_low(step, total_ref, out_ref, tile=256):
@@ -1246,6 +1255,27 @@
         def _(m):
             at = pl.ds(m * tile, tile)
             out_ref[at] = total_ref[at].astype(BF16)
+
+
+def grads_kernel(left_ref, right_ref, out_ref, total_ref):
+    step = pl.program_id(0)
+    add_products(step, total_ref, 0, left_ref, right_ref)
+    store_low(step, total_ref, out_ref)
+
+
+def weight_grads(left, right, block=1024):
+    (rows, width), cols = left.shape, right.shape[1]
+    part = lambda cols: pl.BlockSpec((block, cols), lambda i: (i, 0))
+    return pl.pallas_call(
+        grads_kernel,
+        out_shape=jax.ShapeDtypeStruct((width, cols), BF16),
+        grid=(rows // block,),
+        in_specs=[part(width), part(cols)],
+        out_specs=pl.BlockSpec((width, cols), lambda i: (0, 0)),
+        scratch_shapes=[pltpu.VMEM((width, cols), F32)],
+        cost_estimate=micros(11),
+        name="weight_grads",
+    )(left, right)
 
 
 def gate_back_kernel(
@@ -1256,10 +1286,9 @@
     dmixed = dot_nn(branch_ref[...], w_ref[...])
     gate = gate_ref[...]
     dattended_ref[...] = (dmixed * gate).astype(BF16)
-    dgating = (dmixed * attended_ref[...] * gate * (1.0 - gate)).astype(BF16)
-    dgating_ref[...] = dgating
-    add_products(step, total_ref, 0, normed_ref, dgating)
-    add_products(step, total_ref, dgating.shape[1], branch_ref, mixed_ref[...])
+    dgating_ref[...] = (dmixed * attended_ref[...] * gate * (1.0 - gate)).astype(BF16)
+    add_products(step, total_ref, 0, normed_ref, dgating_ref)
+    add_products(step, total_ref, dgating_ref.shape[1], branch_ref, mixed_ref)
     store_low(step, total_ref, grad_ref)
 
 
@@ -1310,8 +1339,8 @@
 
     if grads:
         grad_ref, total_ref = grads
-        add_products(step, total_ref, 0, mid_ref, dgu_ref[...])
-        add_products(step, total_ref, 2 * count, low_ref, act_ref[...])
+        add_products(step, total_ref, 0, mid_ref, dgu_ref)
+        add_products(step, total_ref, 2 * count, low_ref, act_ref)
         store_low(step, total_ref, grad_ref)
 
 
@@ -1371,18 +1400,20 @@
         dkey_ref[...] = jnp.zeros_like(dkey_ref)
         dvalue_ref[...] = jnp.zeros_like(dvalue_ref)
 
-    for i in range(blocks):
-
-        @pl.when(step == i)
+    rows = pl.ds(pl.multiple_of(step * block, block), block)
+
+    for i in range(0, blocks, 2):
+
+        @pl.when(step // 2 == i // 2)
         def _():
-            rows, seen = pl.ds(i * block, block), pl.ds(0, (i + 1) * block)
+            seen = pl.ds(0, (i + 2) * block)
 
             @pl.loop(0, heads)
             def _(h):
                 cols = pl.ds(pl.multiple_of(h * head, head), head)
                 raw = raw_ref[rows, cols]
                 query = normed_rope(raw, qg_ref[...], cos_ref[rows], sin_ref[rows])
-                scores = causal_scores(query, key_ref[seen], i * block, scaling)
+                scores = causal_scores(query, key_ref[seen], step * block, scaling)
                 probs = jnp.exp(scores - log_ref[h])
                 upstream = up_ref[:, cols]
                 dprobs = dot_nt(upstream, value_ref[seen])
@@ -1852,7 +1883,9 @@
     dqkv, part_last = lax.optimization_barrier((dqkv, part_last))
     theirs_last = their_rows(part_last)
     layer_out = (hidden + ffn_branch).astype(BF16)
-    grad_qkv = dot_tn(normed_all, dqkv).astype(BF16)
+    dqkv, layer_out = lax.optimization_barrier((dqkv, layer_out))
+    grad_qkv = weight_grads(normed_all, dqkv)
+    grad_qkv, theirs_last = lax.optimization_barrier((grad_qkv, theirs_last))
     plan = [(0, i * split, split, i, 0, i == 2) for i in range(3)]
     plan += [(1, i * rest, rest, i, split, i == 2) for i in range(3)]
     grad_gate, grad_up, grad_down = join_grads(

time: 553 us -> 542 us (0.980); the launches traced: 544 us -> 542 us
  Pallas kernels: 492 us -> 502 us
  matrix products: 9.91 us -> 0 us
    pallas_call x0 -> x1, Pallas kernels: none -> 10.1 us  [weight_grads(): pl.pallas_call(grads_kernel, out_shape=jax.ShapeDtypeStruct((width, cols)...]
    dot_general x1 -> x0, matrix products: 9.91 us -> none  [dot_tn(): lax.dot_general(left, right, (((0,), (0,)), ((), ())), preferred_element_...]
  transfers between devices with their start and end apart: 8 -> 8, of which waited for: 5 -> 4; matrix products, arithmetic and copies ran while one was open for 3% -> 1% of each run, Pallas kernels for 76% -> 78%
where the time goes in v2:
time: 542 us
  Pallas kernels  502 us (93%)
  between operations  14.6 us (3%)
  waiting for transfers between devices  9.09 us (2%)
  local copies, waits for them, and re-layouts  7.25 us (1%)
    pallas_call x2, Pallas kernels, scatter_products(): pl.pallas_call(functools.partial(kernel, [item[2] for item in group]), ou...  101 us
    pallas_call x1, Pallas kernels, opening(): pl.pallas_call(functools.partial(opening_kernel, pieces), out_shape=(shap...  79.1 us
    pallas_call x1, Pallas kernels, tail(): pl.pallas_call(functools.partial(tail_kernel, [item[2] for item in group]...  62.5 us
    pallas_call x2, Pallas kernels, feed_forward(): pl.pallas_call(functools.partial(feed_kernel, count, 256), out_shape=(jax...  54.2 us
    pallas_call x1, Pallas kernels, gather_beside(): pl.pallas_call(functools.partial(gather_beside_kernel, [item[2] for item...  43.3 us
    pallas_call x1, Pallas kernels, attend(): pl.pallas_call(functools.partial(attend_kernel, heads, head, block), out_...  42.7 us
    pallas_call x1, Pallas kernels, attend_back(): pl.pallas_call(functools.partial(attend_back_kernel, heads, head, block),...  42.1 us
    pallas_call x1, Pallas kernels, gather_tokens(): pl.pallas_call(functools.partial(gather_kernel, True), out_shape=jax.Shap...  40.4 us
  transfers between devices with their start and end apart: 8, of which 4 were waited for; matrix products, arithmetic and copies ran while one was open for 1% of the time, Pallas kernels for 78%

profile of v2, /device:TPU:0, one launch (start us, length us, event | category | flops | bytes accessed | tf_op | source)
XLA Modules:
  0.0 541.6 jit_solution(4159346655191866307)
XLA Ops:
  7.9 79.1 %opening.1 = (bf16[2,2,2,256,2048]{4,3,2,1,0:T(8,128)(2,1)}, bf16[2048,512]{1,0:T(8,128)(2,1)}, bf16[2048,512]{1,0:T(8,128)(2,1)}, bf16[512,1536]{1,0:T(8,128)(2...) custom-call(bf16[256,2048]{1,0:T(8,128)(2,1)} %bitcast.32, ...), custom_call_target="tpu_custom_call" | custom-call | bytes 264000000 | tf_op jit(solution)/shard_map/opening/pallas_call | solution.py:401
  89.0 42.7 %attend.1 = (f32[2048,512]{1,0:T(8,128)}, f32[2048,256]{1,0:T(8,128)}, f32[2,2048,1]{2,1,0:T(8,128)}, f32[2048,256]{1,0:T(8,128)}, bf16[2048,256]{1,0:T(8,128)(2,1)}, /*index=5*/bf16[2,2,2,256,2048]{4,3,2,1,0:T(8,128)(2,1)}) custom-call(bf16[2048,2048]{1,0:T(8,128)(2,1)} %bitcast.26, bf16[2048,512]{1,0:T(8,128)(2,1)} %get-tuple-element.87.w_ref.refs_2_, ...), custom_call_target="tpu_custom_call" | custom-call | bytes 138600000 | tf_op jit(solution)/shard_map/attend/pallas_call | solution.py:1189
  131.6 47.0 %scatter_products.2 = (f32[256,2048]{1,0:T(8,128)}, f32[256,1]{1,0:T(8,128)}, bf16[256,2048]{1,0:T(8,128)(2,1)}) custom-call(bf16[2048,256]{1,0:T(8,128)(2,1)} %get-tuple-element.93.refs_0_.mixed_ref, bf16[2048,512]{1,0:T(8,128)(2,1)} %get-tuple-element.88.wg_ref.refs_1_.w_ref.refs_3_, bf16[256,2048]{1,0:T(8,128)(2,1)} %bitcast.33, ...), custom_call_target="tpu_custom_call" | custom-call | bytes 158400000 | tf_op jit(solution)/shard_map/scatter_products/pallas_call | solution.py:668
  178.6 40.4 %gather_tokens.1 = bf16[2,2,2,256,2048]{4,3,2,1,0:T(8,128)(2,1)} custom-call(bf16[256,2048]{1,0:T(8,128)(2,1)} %get-tuple-element.94.refs_0_), custom_call_target="tpu_custom_call" | custom-call | bytes 138600000 | tf_op jit(solution)/shard_map/gather_tokens/pallas_call | solution.py:208
  219.1 41.3 %feed_forward.2 = (bf16[2048,512]{1,0:T(8,128)(2,1)}, bf16[2048,1024]{1,0:T(8,128)(2,1)}, bf16[2048,1536]{1,0:T(8,128)(2,1)}) custom-call(bf16[2048,2048]{1,0:T(8,128)(2,1)} %bitcast.23, bf16[2048,2048]{1,0:T(8,128)(2,1)} %bitcast.29, bf16[2048,1536]{1,0:T(8,128)(2,1)} %all-gather.3.cloned.1.call-done.w_ref.refs_2_), custom_call_target="tpu_custom_call" | custom-call | bytes 135300000 | tf_op jit(solution)/shard_map/feed_forward/pallas_call | solution.py:1352
  260.6 4.4 all-gather.5.cloned.1.call-done.w_ref.refs_3_
  265.0 13.0 %feed_forward.3 = (bf16[2048,256]{1,0:T(8,128)(2,1)}, bf16[2048,512]{1,0:T(8,128)(2,1)}) custom-call(bf16[2048,2048]{1,0:T(8,128)(2,1)} %bitcast.24, bf16[2048,2048]{1,0:T(8,128)(2,1)} %bitcast.30, bf16[2048,768]{1,0:T(8,128)(2,1)} %all-gather.5.cloned.1.call-done.w_ref.refs_3_), custom_call_target="tpu_custom_call" | custom-call | bytes 46200000 | tf_op jit(solution)/shard_map/feed_forward/pallas_call | solution.py:1352
  278.0 54.5 %scatter_products.3 = (f32[256,2048]{1,0:T(8,128)}, bf16[256,2048]{1,0:T(8,128)(2,1)}, f32[1,2048]{1,0:T(1,128)}) custom-call(bf16[2048,1024]{1,0:T(8,128)(2,1)} %get-tuple-element.97.refs_0_, bf16[2048,512]{1,0:T(8,128)(2,1)} %get-tuple-element.101.refs_1_.refs_6_, bf16[2048,1536]{1,0:T(8,128)(2,1)} %all-gather.3.cloned.1.call-done.w_ref.refs_2_, ...), custom_call_target="tpu_custom_call" | custom-call | bytes 158400000 | tf_op jit(solution)/shard_map/scatter_products/pallas_call | solution.py:668
  332.5 43.3 %gather_beside.1 = (bf16[2,2,2,256,2048]{4,3,2,1,0:T(8,128)(2,1)}, bf16[4,256,2048]{2,1,0:T(8,128)(2,1)}, bf16[2048,768]{1,0:T(8,128)(2,1)}) custom-call(bf16[256,2048]{1,0:T(8,128)(2,1)} %get-tuple-element.105.shard_ref, bf16[2048,512]{1,0:T(8,128)(2,1)} %get-tuple-element.106.refs_0_, bf16[2048,256]{1,0:T(8,128)(2,1)} %get-tuple-element.107.refs_1_.refs_7_, ...), custom_call_target="tpu_custom_call" | custom-call | bytes 145200000 | tf_op jit(solution)/shard_map/gather_beside/pallas_call | solution.py:754
  376.8 1.2 constant_dynamic-slice_fusion.2
  378.0 1.5 collective-permute-start
  379.5 17.5 %gate_back.1 = (bf16[2048,256]{1,0:T(8,128)(2,1)}, bf16[2048,256]{1,0:T(8,128)(2,1)}, bf16[2048,512]{1,0:T(8,128)(2,1)}) custom-call(bf16[2048,2048]{1,0:T(8,128)(2,1)} %bitcast.27, bf16[2048,2048]{1,0:T(8,128)(2,1)} %bitcast.35, bf16[2048,512]{1,0:T(8,128)(2,1)} %get-tuple-element.88.wg_ref.refs_1_.w_ref.refs_3_, ...), custom_call_target="tpu_custom_call" | custom-call | bytes 82500000 | tf_op jit(solution)/shard_map/gate_back/pallas_call | solution.py:1299
  398.3 42.1 %attend_back.1 = (bf16[2048,512]{1,0:T(8,128)(2,1)}, f32[1,128]{1,0:T(1,128)}, f32[1,128]{1,0:T(1,128)}, f32[256,2048]{1,0:T(8,128)}) custom-call(f32[2048,512]{1,0:T(8,128)} %get-tuple-element.92.raw_ref, bf16[2048,256]{1,0:T(8,128)(2,1)} %get-tuple-element.115.up_ref, f32[2,2048,1]{2,1,0:T(8,128)} %get-tuple-element.116.log_ref, ...), custom_call_target="tpu_custom_call" | custom-call | bytes 132000000 | tf_op jit(solution)/shard_map/attend_back/pallas_call | solution.py:1459
  440.4 1.0 constant_dynamic-slice_fusion.1
  442.3 3.5 add_convert_fusion
  445.8 10.1 %weight_grads.1.refs_4_ = bf16[2048,512]{1,0:T(8,128)(2,1)} custom-call(bf16[2048,2048]{1,0:T(8,128)(2,1)} %bitcast.28, bf16[2048,512]{1,0:T(8,128)(2,1)} %get-tuple-element.122.right_ref.refs_0_), custom_call_target="tpu_custom_call" | custom-call | bytes 36300000 | tf_op jit(solution)/shard_map/weight_grads/pallas_call | solution.py:1269
  456.7 4.5 join_grads.2
  461.2 62.5 %tail.1 = (bf16[256,2048]{1,0:T(8,128)(2,1)}, bf16[256,512]{1,0:T(8,128)(2,1)}, bf16[256,512]{1,0:T(8,128)(2,1)}, f32[1,4352]{1,0:T(1,128)}) custom-call(bf16[2048,512]{1,0:T(8,128)(2,1)} %get-tuple-element.122.right_ref.refs_0_, bf16[2048,256]{1,0:T(8,128)(2,1)} %get-tuple-element.132.refs_1_, bf16[2048,512]{1,0:T(8,128)(2,1)} %get-tuple-element.87.w_ref.refs_2_, ...), custom_call_target="tpu_custom_call" | custom-call | bytes 171600000 | tf_op jit(solution)/shard_map/tail/pallas_call | solution.py:1001
  523.8 1.1 constant_dynamic-slice_fusion
  524.8 1.5 collective-permute-start.2
  526.3 2.1 join_last.1
  528.4 2.9 collective-permute-done.2.refs_1_
  532.0 2.2 join_grads.3
  534.1 1.0 copy.35
  (36 shorter events, 6.8 us)
Async XLA Ops:
  7.2 211.9 %all-gather.3.cloned.1.call-start = ((), (), s32[]{:S(2)}) async-start(), calls=%async_computation.3 | async-start | bytes 7864320 | tf_op jit(solution)/shard_map/all_gather | solution.py:1037
  87.0 0.9 copy-start.5
  87.0 1.5 copy-start.6
  87.0 1.5 copy-start.7
  87.0 178.0 %all-gather.5.cloned.1.call-start = ((), (), s32[]{:S(2)}) async-start(), calls=%async_computation.4 | async-start | bytes 3932160 | tf_op jit(solution)/shard_map/all_gather | solution.py:1037
  87.8 289.0 %reduce-scatter.4.cloned.1.call-start = ((), (), s32[]{:S(2)}) async-start(), calls=%async_computation.5 | async-start | bytes 7864320 | tf_op jit(solution)/shard_map/reduce_scatter | solution.py:1041
  260.4 180.1 %reduce-scatter.6.cloned.1.call-start = ((), (), s32[]{:S(2)}) async-start(), calls=%async_computation.6 | async-start | bytes 3932160 | tf_op jit(solution)/shard_map/reduce_scatter | solution.py:1041
  375.8 147.9 %reduce-scatter.8.cloned.1.call-start = ((), (), s32[]{:S(2)}) async-start(), calls=%async_computation.7 | async-start | bytes 2621440 | tf_op jit(solution)/shard_map/reduce_scatter | solution.py:1041
  378.0 19.4 %collective-permute-start = (bf16[256,1536]{1,0:T(8,128)(2,1)S(1)}, bf16[256,1536]{1,0:T(8,128)(2,1)S(1)}, u32[]{:S(2)}, u32[]{:S(2)}) collective-permute-start(bf16[256,1536]{1,0:T(8,128)(2,1)S(1)} %constant_dynamic-slice_fusion.2), channel_id=1, source_target_pairs={{0,4},{4,0},{1,5},{5,1},{2,6},{6,2},{3,7},{7,3},{8,12},{12,8},{9,1... | collective-permute-start | bytes 2359304 | tf_op jit(solution)/shard_map/ppermute | solution.py:1026
  397.0 0.7 copy-start.4
  397.3 43.1 %copy-start.1 = (bf16[256,1536]{1,0:T(8,128)(2,1)}, bf16[256,1536]{1,0:T(8,128)(2,1)S(1)}, u32[]{:S(2)}) copy-start(bf16[256,1536]{1,0:T(8,128)(2,1)S(1)} %collective-permute-done.refs_2_) | copy-start | bytes 2359300
  441.5 14.4 %collective-permute-start.1 = (bf16[256,768]{1,0:T(8,128)(2,1)S(1)}, bf16[256,768]{1,0:T(8,128)(2,1)S(1)}, u32[]{:S(2)}, u32[]{:S(2)}) collective-permute-start(bf16[256,768]{1,0:T(8,128)(2,1)S(1)} %constant_dynamic-slice_fusion.1), channel_id=1, source_target_pairs={{0,4},{4,0},{1,5},{5,1},{2,6},{6,2},{3,7},{7,3},{8,12},{12,8},{9,1... | collective-permute-start | bytes 1179656 | tf_op jit(solution)/shard_map/ppermute | solution.py:1026
  455.9 0.7 copy-start.2
  523.7 10.4 %copy-start = (bf16[256,2048]{1,0:T(8,128)(2,1)S(1)}, bf16[256,2048]{1,0:T(8,128)(2,1)}, u32[]{:S(2)}) copy-start(bf16[256,2048]{1,0:T(8,128)(2,1)} %get-tuple-element.141) | copy-start | bytes 3145732
  524.8 6.4 %collective-permute-start.2 = (bf16[256,512]{1,0:T(8,128)(2,1)S(1)}, bf16[256,512]{1,0:T(8,128)(2,1)S(1)}, u32[]{:S(2)}, u32[]{:S(2)}) collective-permute-start(bf16[256,512]{1,0:T(8,128)(2,1)S(1)} %constant_dynamic-slice_fusion), channel_id=1, source_target_pairs={{0,4},{4,0},{1,5},{5,1},{2,6},{6,2},{3,7},{7,3},{8,12},{12,8},{9,1... | collective-permute-start | bytes 786440 | tf_op jit(solution)/shard_map/ppermute | solution.py:1026
  531.3 0.7 copy-start.3
Sparse Core Ops, SparseCore 0:
  87.1 114.5 all-gather.2
  203.3 61.7 all-gather.4
  267.3 109.3 reduce-scatter.3
  378.9 60.7 reduce-scatter.5
  441.9 59.1 reduce-scatter.7

commit v3 on v2

--- a/solution.py
+++ b/solution.py
@@ -193,30 +193,6 @@
     return begin, here, finish
 
 
-def gather_kernel(split, *refs):
-    source, out, *sems = refs
-    begin, forward, across, finish = gather_steps(source, out, *sems, split)
-    greet(tuple(place()[3].values()))
-    begin()
-    forward()
-    across()
-    finish()
-
-
-def gather_tokens(shard):
-    rows, width = shard.shape
-    return pl.pallas_call(
-        functools.partial(gather_kernel, True),
-        out_shape=jax.ShapeDtypeStruct((2, 2, 2, rows, width), shard.dtype),
-        in_specs=[pl.BlockSpec(memory_space=pltpu.VMEM)],
-        out_specs=pl.BlockSpec(memory_space=pl.ANY),
-        scratch_shapes=list(GATHER_SEMAPHORES),
-        compiler_params=pltpu.CompilerParams(collective_id=1, has_side_effects=True),
-        cost_estimate=micros(42),
-        name="gather_tokens",
-    )(shard).reshape(8 * rows, width)
-
-
 def line_steps(rows_ref, out_ref, local_sem, send, recv, part, which):
     z = lax.axis_index("z")
     rows, half = rows_ref.shape[0], rows_ref.shape[0] // 2
@@ -299,9 +275,57 @@
     pl.semaphore_wait(barrier, jnp.where(inner, count + 1, count))
 
 
+LINE_SEMAPHORES = (
+    pltpu.SemaphoreType.DMA((2,)),
+    pltpu.SemaphoreType.DMA((10,)),
+    pltpu.SemaphoreType.DMA((10,)),
+)
+
+
+def both_halves(rows_ref, out_ref, *sems):
+    y = lax.axis_index("y")
+    return [line_steps(rows_ref, out_ref, *sems, part, which) for part, which in ((0, y), (1, 1 - y))]
+
+
+def gather_kernel(source, rows_ref, out, line_ref, *sems):
+    begin, forward, across, finish = gather_steps(source, out, *sems[:3])
+    lines = both_halves(rows_ref, line_ref, *sems[3:])
+    greet_line(tuple(place()[3].values()), *lines[0][4]())
+    for steps in lines:
+        steps[0]()
+    begin()
+    for steps in lines:
+        steps[1]()
+    forward()
+    lines[0][2]()
+    across()
+    lines[1][2]()
+    finish()
+    for steps in lines:
+        steps[3]()
+
+
+def gather_tokens(shard, line):
+    rows, width = shard.shape
+    gathered, lined = pl.pallas_call(
+        gather_kernel,
+        out_shape=(
+            jax.ShapeDtypeStruct((2, 2, 2, rows, width), shard.dtype),
+            jax.ShapeDtypeStruct((4 * line.shape[0], line.shape[1]), line.dtype),
+        ),
+        in_specs=[pl.BlockSpec(memory_space=pltpu.VMEM)] * 2,
+        out_specs=(pl.BlockSpec(memory_space=pl.ANY),) * 2,
+        scratch_shapes=[*GATHER_SEMAPHORES, *LINE_SEMAPHORES],
+        compiler_params=pltpu.CompilerParams(collective_id=1, has_side_effects=True),
+        cost_estimate=micros(42),
+        name="gather_tokens",
+    )(shard, line)
+    return gathered.reshape(8 * rows, width), lined
+
+
 def opening_kernel(pieces, tokens, cotangent, gain, ids, counts, numer, denom, turns, *refs):
     sources, refs = list(refs[:8]), refs[8:]
-    out, line_q, line_g, first, last, inverse, low, factor, cosine, sine, *refs = refs
+    out, line_q, line_g, first, last_gu, last_d, inverse, low, factor, cosine, sine, *refs = refs
     rows_q, rows_g, normed, output_t, down_t, *sems = refs
     begin, forward, across, finish = gather_steps(normed, out, *sems[:3], False)
     y = lax.axis_index("y")
@@ -313,7 +337,7 @@
     output_ref, down_ref = sources[4], sources[7]
     sources[4], sources[7] = output_t, down_t
     swaps = [
-        swap_steps(pieces, sources, (rows_q, rows_g, first, last), *sems[9:], wanted)
+        swap_steps(pieces, sources, (rows_q, rows_g, first, last_gu, last_d), *sems[9:], wanted)
         for wanted in (lambda out: out == 0, lambda out: out == 1, lambda out: out > 1)
     ]
     step = 64
@@ -338,11 +362,12 @@
 
     greet_line(tuple(place()[3].values()), *steps[0][4]())
     swaps[0][0]()
+    swaps[0][1]()
+    steps[0][0]()
     output_t[...] = output_ref[...].astype(F32).T.astype(BF16)
     swaps[1][0]()
-    for i in range(2):
-        swaps[i][1]()
-        steps[i][0]()
+    swaps[1][1]()
+    steps[1][0]()
     pl.loop(0, tokens.shape[0] // step)(norm)
     begin()
     for i in range(2):
@@ -359,11 +384,11 @@
         at = pl.ds(pl.multiple_of(i * 256, 256), 256)
         down_t[:, at] = down_ref[at].astype(F32).T.astype(BF16)
 
+    steps[2][1]()
+    steps[3][1]()
     forward()
     across()
     swaps[2][0]()
-    steps[2][1]()
-    steps[3][1]()
     steps[0][2]()
     steps[1][2]()
     pl.loop(0, tokens.shape[0] // step)(weigh)
@@ -384,7 +409,8 @@
         [(i, 0, halves[i]) for i in (0, 1, 2)],
         [(i, 0, halves[i]) for i in (3, 4)],
         [(i, 0, split) for i in (5, 6, 7)],
-        [(i, split, halves[i] - split) for i in (5, 6, 7)],
+        [(i, split, halves[i] - split) for i in (5, 6)],
+        [(7, split, halves[7] - split)],
     )
     pieces, widths = [], []
     for group in groups:
@@ -411,7 +437,7 @@
             shape((full_len, head), F32),
         ),
         in_specs=[whole] * (8 + len(weights)),
-        out_specs=(*[loose] * 5, *[whole] * 5),
+        out_specs=(*[loose] * 6, *[whole] * 5),
         scratch_shapes=[
             *[pltpu.VMEM((2 * rows, size), BF16) for size in widths[:2]],
             pltpu.VMEM((rows, width), BF16),
@@ -1320,50 +1346,107 @@
     )(normed, branch, weights, attended, gate, mixed)
 
 
-def feed_kernel(count, tile, mid_ref, low_ref, w_ref, act_ref, dgu_ref, *grads):
-    step = pl.program_id(0)
-
+def feed_units(count, tile, mid_ref, low_ref, gu_ref, down_ref, first, act_ref, dgu_ref):
     @pl.loop(0, count // tile)
     def _(j):
         start = pl.multiple_of(j * tile, tile)
         at, after = pl.ds(start, tile), pl.ds(pl.multiple_of(count + start, tile), tile)
-        last = pl.ds(pl.multiple_of(2 * count + start, tile), tile)
-        gate = dot_nn(mid_ref[...], w_ref[:, at])
-        up = dot_nn(mid_ref[...], w_ref[:, after])
-        dact = dot_nn(low_ref[...], w_ref[:, last])
+        last = pl.ds(pl.multiple_of(first + start, tile), tile)
+        gate = dot_nn(mid_ref[...], gu_ref[:, at])
+        up = dot_nn(mid_ref[...], gu_ref[:, after])
+        dact = dot_nn(low_ref[...], down_ref[:, last])
         sigma = jax.nn.sigmoid(gate)
         silu = gate * sigma
         act_ref[:, at] = (silu * up).astype(BF16)
         dgu_ref[:, at] = (dact * up * sigma * (1.0 + gate * (1.0 - sigma))).astype(BF16)
         dgu_ref[:, after] = (dact * silu).astype(BF16)
 
-    if grads:
-        grad_ref, total_ref = grads
-        add_products(step, total_ref, 0, mid_ref, dgu_ref)
-        add_products(step, total_ref, 2 * count, low_ref, act_ref)
-        store_low(step, total_ref, grad_ref)
-
-
-def feed_forward(mid, low, weights, grads, block):
+
+def feed_kernel(count, tile, mid_ref, low_ref, gu_ref, down_ref, act_ref, dgu_ref):
+    feed_units(count, tile, mid_ref, low_ref, gu_ref, down_ref, 0, act_ref, dgu_ref)
+
+
+def feed_grads_kernel(
+    count, tile, mid_ref, low_ref, w_ref, rows_ref, act_ref, dgu_ref, grad_ref, line_ref, total_ref, *sems
+):
+    step = pl.program_id(0)
+    lines = both_halves(rows_ref, line_ref, *sems)
+
+    @pl.when(step == 0)
+    def _():
+        greet_line((), *lines[0][4]())
+        for steps in lines:
+            steps[0]()
+
+    feed_units(count, tile, mid_ref, low_ref, w_ref, w_ref, 2 * count, act_ref, dgu_ref)
+
+    @pl.when(step == 0)
+    def _():
+        lines[0][1]()
+
+    @pl.when(step == pl.num_programs(0) - 1)
+    def _():
+        lines[1][2]()
+
+    add_products(step, total_ref, 0, mid_ref, dgu_ref)
+    add_products(step, total_ref, 2 * count, low_ref, act_ref)
+
+    @pl.when(step == 0)
+    def _():
+        lines[1][1]()
+        lines[0][2]()
+
+    store_low(step, total_ref, grad_ref)
+
+    @pl.when(step == pl.num_programs(0) - 1)
+    def _():
+        for steps in lines:
+            steps[3]()
+
+
+def feed_forward(mid, low, weights, down, block=512):
+    rows, width = mid.shape
+    count = down.shape[1]
+    part = lambda cols: pl.BlockSpec((block, cols), lambda i: (i, 0))
+    whole = lambda array: pl.BlockSpec(array.shape, lambda i: (0, 0), pipeline_mode=pl.Buffered(1))
+    return pl.pallas_call(
+        functools.partial(feed_kernel, count, 256),
+        out_shape=(
+            jax.ShapeDtypeStruct((rows, count), BF16),
+            jax.ShapeDtypeStruct((rows, 2 * count), BF16),
+        ),
+        grid=(rows // block,),
+        in_specs=[part(width), part(width), whole(weights), whole(down)],
+        out_specs=(part(count), part(2 * count)),
+        compiler_params=pltpu.CompilerParams(vmem_limit_bytes=VMEM_BYTES),
+        cost_estimate=micros(14),
+        name="feed_forward",
+    )(mid, low, weights, down)
+
+
+def feed_forward_grads(mid, low, weights, line, block=1024):
     rows, width = mid.shape
     count = weights.shape[1] // 3
     part = lambda cols: pl.BlockSpec((block, cols), lambda i: (i, 0))
     whole = pl.BlockSpec(weights.shape, lambda i: (0, 0), pipeline_mode=pl.Buffered(1))
     return pl.pallas_call(
-        functools.partial(feed_kernel, count, 256),
+        functools.partial(feed_grads_kernel, count, 256),
         out_shape=(
             jax.ShapeDtypeStruct((rows, count), BF16),
             jax.ShapeDtypeStruct((rows, 2 * count), BF16),
-            *[jax.ShapeDtypeStruct(weights.shape, BF16)] * grads,
+            jax.ShapeDtypeStruct(weights.shape, BF16),
+            jax.ShapeDtypeStruct((4 * line.shape[0], line.shape[1]), BF16),
         ),
         grid=(rows // block,),
-        in_specs=[part(width), part(width), whole],
-        out_specs=(part(count), part(2 * count), *[whole] * grads),
-        scratch_shapes=[pltpu.VMEM(weights.shape, F32)] * grads,
-        compiler_params=pltpu.CompilerParams(vmem_limit_bytes=VMEM_BYTES),
-        cost_estimate=micros(41 if grads else 14),
-        name="feed_forward",
-    )(mid, low, weights)
+        in_specs=[part(width), part(width), whole, pl.BlockSpec(memory_space=pltpu.VMEM)],
+        out_specs=(part(count), part(2 * count), whole, pl.BlockSpec(memory_space=pl.ANY)),
+        scratch_shapes=[pltpu.VMEM(weights.shape, F32), *LINE_SEMAPHORES],
+        compiler_params=pltpu.CompilerParams(
+            collective_id=9, has_side_effects=True, vmem_limit_bytes=VMEM_BYTES
+        ),
+        cost_estimate=micros(41),
+        name="feed_forward_grads",
+    )(mid, low, weights, line)
 
 
 def attend_back_kernel(
@@ -1819,7 +1902,7 @@
     split, rest = ff_cols * 2 // 3, ff_cols - ff_cols * 2 // 3
     tokens, cotangent = tokens.reshape(rows, width), cotangent.reshape(rows, width)
     (
-        normed_all, w_qkv, w_go, rows_first, rows_last, inverse_in, out_low, factor, cos_rows, sin_rows,
+        normed_all, w_qkv, w_go, rows_first, rows_gu, rows_d, inverse_in, out_low, factor, cos_rows, sin_rows,
     ) = opening(
         tokens,
         cotangent,
@@ -1833,7 +1916,6 @@
         head,
     )
     w_first = gather_rows(rows_first)
-    w_last = gather_rows(rows_last)
 
     query_scale, key_scale = query_gain.astype(F32)[None], key_gain.astype(F32)[None]
     qkv, attended, logs, gate_sig, mixed, out_all = attend(
@@ -1845,23 +1927,22 @@
     hidden, inverse_mid, normed_mid = scatter_products(
         middle_kernel, 7, (tokens, gain_mid), (wide, column, low), (mixed, w_go, q_cols)
     )
-    mid_all = gather_tokens(normed_mid)
-
-    act_first, dgu_first, grad_first = feed_forward(mid_all, out_all, w_first, True, 1024)
+    mid_all, w_last_d = gather_tokens(normed_mid, rows_d)
+
+    act_first, dgu_first, grad_first, w_last_gu = feed_forward_grads(mid_all, out_all, w_first, rows_gu)
     part_first = scatter_grads(grad_first)
-    w_last, grad_first = lax.optimization_barrier((w_last, grad_first))
-    act_last, dgu_last = feed_forward(mid_all, out_all, w_last, False, 512)
+    act_last, dgu_last = feed_forward(mid_all, out_all, w_last_gu, w_last_d)
     dhidden, dbranch, grad_gain_mid = scatter_products(
         middle_back_kernel,
         8,
         (hidden, inverse_mid, gain_mid, cotangent, factor),
         (wide, low, jax.ShapeDtypeStruct((1, width), F32)),
         (dgu_first, w_first, 0),
-        (dgu_last, w_last, 0),
+        (dgu_last, w_last_gu, 0),
     )
     dbranch_all, ffn_sums, grad_last = gather_beside(
         dbranch,
-        ((act_first, w_first, 2 * split), (act_last, w_last, 2 * rest)),
+        ((act_first, w_first, 2 * split), (act_last, w_last_d, 0)),
         mid_all,
         out_all,
         dgu_last,

time: 542 us -> 539 us (level)
    pallas_call x1 -> x2, Pallas kernels: 40.4 us -> 87.6 us  [the longest x1 46.4 us: feed_forward_grads(): pl.pallas_call(functools.partial(feed_grads_kernel, count, 256), out_shap...]
    pallas_call x2 -> x1, Pallas kernels: 54.2 us -> 12.3 us  [feed_forward(): pl.pallas_call(functools.partial(feed_kernel, count, 256), out_shape=(jax...]
  transfers between devices with their start and end apart: 8 -> 7, of which waited for: 4 -> 2; matrix products, arithmetic and copies ran while one was open for 1% -> 1% of each run, Pallas kernels for 78% -> 70%
where the time goes in v3:
time: 539 us; the launch traced here: 538 us
  Pallas kernels  505 us (94%)
  between operations  14.6 us (3%)
  local copies, waits for them, and re-layouts  7 us (1%)
    pallas_call x2, Pallas kernels, scatter_products(): pl.pallas_call(functools.partial(kernel, [item[2] for item in group]), ou...  99.2 us
    pallas_call x1, Pallas kernels, opening(): pl.pallas_call(functools.partial(opening_kernel, pieces), out_shape=(shap...  77.5 us
    pallas_call x1, Pallas kernels, tail(): pl.pallas_call(functools.partial(tail_kernel, [item[2] for item in group]...  61.1 us
    pallas_call x1, Pallas kernels, feed_forward_grads(): pl.pallas_call(functools.partial(feed_grads_kernel, count, 256), out_shap...  46.4 us
    pallas_call x1, Pallas kernels, gather_beside(): pl.pallas_call(functools.partial(gather_beside_kernel, [item[2] for item...  44.8 us
    pallas_call x1, Pallas kernels, attend(): pl.pallas_call(functools.partial(attend_kernel, heads, head, block), out_...  43.4 us
    pallas_call x1, Pallas kernels, attend_back(): pl.pallas_call(functools.partial(attend_back_kernel, heads, head, block),...  41.9 us
    pallas_call x1, Pallas kernels, gather_tokens(): pl.pallas_call(gather_kernel, out_shape=(jax.ShapeDtypeStruct((2, 2, 2, r...  41.2 us
  transfers between devices with their start and end apart: 7, of which 2 were waited for; matrix products, arithmetic and copies ran while one was open for 1% of the time, Pallas kernels for 70%

profile of v3, /device:TPU:0, one launch (start us, length us, event | category | flops | bytes accessed | tf_op | source)
XLA Modules:
  0.0 538.4 jit_solution(1546749614142645237)
XLA Ops:
  7.9 77.5 %opening.1 = (bf16[2,2,2,256,2048]{4,3,2,1,0:T(8,128)(2,1)}, bf16[2048,512]{1,0:T(8,128)(2,1)}, bf16[2048,512]{1,0:T(8,128)(2,1)}, bf16[512,1536]{1,0:T(8,128)(2...) custom-call(bf16[256,2048]{1,0:T(8,128)(2,1)} %bitcast.32, ...), custom_call_target="tpu_custom_call" | custom-call | bytes 264000000 | tf_op jit(solution)/shard_map/opening/pallas_call | solution.py:427
  86.6 43.4 %attend.1 = (f32[2048,512]{1,0:T(8,128)}, f32[2048,256]{1,0:T(8,128)}, f32[2,2048,1]{2,1,0:T(8,128)}, f32[2048,256]{1,0:T(8,128)}, bf16[2048,256]{1,0:T(8,128)(2,1)}, /*index=5*/bf16[2,2,2,256,2048]{4,3,2,1,0:T(8,128)(2,1)}) custom-call(bf16[2048,2048]{1,0:T(8,128)(2,1)} %bitcast.23, bf16[2048,512]{1,0:T(8,128)(2,1)} %get-tuple-element.90.w_ref.refs_2_, ...), custom_call_target="tpu_custom_call" | custom-call | bytes 138600000 | tf_op jit(solution)/shard_map/attend/pallas_call | solution.py:1215
  130.0 46.1 %scatter_products.2 = (f32[256,2048]{1,0:T(8,128)}, f32[256,1]{1,0:T(8,128)}, bf16[256,2048]{1,0:T(8,128)(2,1)}) custom-call(bf16[2048,256]{1,0:T(8,128)(2,1)} %get-tuple-element.96.refs_0_.mixed_ref, bf16[2048,512]{1,0:T(8,128)(2,1)} %get-tuple-element.91.wg_ref.refs_1_.w_ref.refs_3_, bf16[256,2048]{1,0:T(8,128)(2,1)} %bitcast.33, ...), custom_call_target="tpu_custom_call" | custom-call | bytes 158400000 | tf_op jit(solution)/shard_map/scatter_products/pallas_call | solution.py:694
  176.1 41.2 %gather_tokens.1 = (bf16[2,2,2,256,2048]{4,3,2,1,0:T(8,128)(2,1)}, bf16[2048,256]{1,0:T(8,128)(2,1)}) custom-call(bf16[256,2048]{1,0:T(8,128)(2,1)} %get-tuple-element.97.source, bf16[512,256]{1,0:T(8,128)(2,1)} %get-tuple-element.98.rows_ref), custom_call_target="tpu_custom_call" | custom-call | bytes 138600000 | tf_op jit(solution)/shard_map/gather_tokens/pallas_call | solution.py:310
  217.4 46.4 %feed_forward_grads.1 = (bf16[2048,512]{1,0:T(8,128)(2,1)}, bf16[2048,1024]{1,0:T(8,128)(2,1)}, bf16[2048,1536]{1,0:T(8,128)(2,1)}, bf16[2048,512]{1,0:T(8,128)(2,1)}) custom-call(bf16[2048,2048]{1,0:T(8,128)(2,1)} %bitcast.29, bf16[2048,2048]{1,0:T(8,128)(2,1)} %bitcast.26, bf16[2048,1536]{1,0:T(8,128)(2,1)} %all-gather.2.cloned.1.call-done.w_ref.refs_2_, ...), custom_call_target="tpu_custom_call" | custom-call | bytes 135300000 | tf_op jit(solution)/shard_map/feed_forward_grads/pallas_call | solution.py:1432
  264.0 12.3 %feed_forward.1 = (bf16[2048,256]{1,0:T(8,128)(2,1)}, bf16[2048,512]{1,0:T(8,128)(2,1)}) custom-call(bf16[2048,2048]{1,0:T(8,128)(2,1)} %bitcast.30, bf16[2048,2048]{1,0:T(8,128)(2,1)} %bitcast.27, bf16[2048,512]{1,0:T(8,128)(2,1)} %get-tuple-element.104.gu_ref.refs_3_, bf16[2048,256]{1,0:T(8,128)(2,1)} %get-tuple-element.105.down_ref.refs_3_), custom_call_target="tpu_custom_call" | custom-call | bytes 46200000 | tf_op jit(solution)/shard_map/feed_forward/pallas_call | solution.py:1412
  276.3 53.1 %scatter_products.3 = (f32[256,2048]{1,0:T(8,128)}, bf16[256,2048]{1,0:T(8,128)(2,1)}, f32[1,2048]{1,0:T(1,128)}) custom-call(bf16[2048,1024]{1,0:T(8,128)(2,1)} %get-tuple-element.103.refs_0_, bf16[2048,512]{1,0:T(8,128)(2,1)} %get-tuple-element.106.refs_1_.refs_6_, bf16[2048,1536]{1,0:T(8,128)(2,1)} %all-gather.2.cloned.1.call-done.w_ref.refs_2_, ...), custom_call_target="tpu_custom_call" | custom-call | bytes 158400000 | tf_op jit(solution)/shard_map/scatter_products/pallas_call | solution.py:694
  329.5 44.8 %gather_beside.1 = (bf16[2,2,2,256,2048]{4,3,2,1,0:T(8,128)(2,1)}, bf16[4,256,2048]{2,1,0:T(8,128)(2,1)}, bf16[2048,768]{1,0:T(8,128)(2,1)}) custom-call(bf16[256,2048]{1,0:T(8,128)(2,1)} %get-tuple-element.110.shard_ref, bf16[2048,512]{1,0:T(8,128)(2,1)} %get-tuple-element.111.refs_0_, bf16[2048,256]{1,0:T(8,128)(2,1)} %get-tuple-element.112.refs_1_.refs_7_, ...), custom_call_target="tpu_custom_call" | custom-call | bytes 145200000 | tf_op jit(solution)/shard_map/gather_beside/pallas_call | solution.py:780
  374.6 1.2 constant_dynamic-slice_fusion.2
  375.8 1.0 collective-permute-start
  376.8 17.9 %gate_back.1 = (bf16[2048,256]{1,0:T(8,128)(2,1)}, bf16[2048,256]{1,0:T(8,128)(2,1)}, bf16[2048,512]{1,0:T(8,128)(2,1)}) custom-call(bf16[2048,2048]{1,0:T(8,128)(2,1)} %bitcast.24, bf16[2048,2048]{1,0:T(8,128)(2,1)} %bitcast.35, bf16[2048,512]{1,0:T(8,128)(2,1)} %get-tuple-element.91.wg_ref.refs_1_.w_ref.refs_3_, ...), custom_call_target="tpu_custom_call" | custom-call | bytes 82500000 | tf_op jit(solution)/shard_map/gate_back/pallas_call | solution.py:1325
  396.4 41.9 %attend_back.1 = (bf16[2048,512]{1,0:T(8,128)(2,1)}, f32[1,128]{1,0:T(1,128)}, f32[1,128]{1,0:T(1,128)}, f32[256,2048]{1,0:T(8,128)}) custom-call(f32[2048,512]{1,0:T(8,128)} %get-tuple-element.95.raw_ref, bf16[2048,256]{1,0:T(8,128)(2,1)} %get-tuple-element.121.up_ref, f32[2,2048,1]{2,1,0:T(8,128)} %get-tuple-element.122.log_ref, ...), custom_call_target="tpu_custom_call" | custom-call | bytes 132000000 | tf_op jit(solution)/shard_map/attend_back/pallas_call | solution.py:1542
  438.3 1.0 constant_dynamic-slice_fusion.1
  439.4 1.1 collective-permute-start.1
  440.5 3.5 add_convert_fusion
  443.9 10.2 %weight_grads.1.refs_4_ = bf16[2048,512]{1,0:T(8,128)(2,1)} custom-call(bf16[2048,2048]{1,0:T(8,128)(2,1)} %bitcast.25, bf16[2048,512]{1,0:T(8,128)(2,1)} %get-tuple-element.128.right_ref.refs_0_), custom_call_target="tpu_custom_call" | custom-call | bytes 36300000 | tf_op jit(solution)/shard_map/weight_grads/pallas_call | solution.py:1295
  454.9 4.5 join_grads.2
  459.3 61.1 %tail.1 = (bf16[256,2048]{1,0:T(8,128)(2,1)}, bf16[256,512]{1,0:T(8,128)(2,1)}, bf16[256,512]{1,0:T(8,128)(2,1)}, f32[1,4352]{1,0:T(1,128)}) custom-call(bf16[2048,512]{1,0:T(8,128)(2,1)} %get-tuple-element.128.right_ref.refs_0_, bf16[2048,256]{1,0:T(8,128)(2,1)} %get-tuple-element.138.refs_1_, bf16[2048,512]{1,0:T(8,128)(2,1)} %get-tuple-element.90.w_ref.refs_2_, ...), custom_call_target="tpu_custom_call" | custom-call | bytes 171600000 | tf_op jit(solution)/shard_map/tail/pallas_call | solution.py:1027
  520.5 1.1 constant_dynamic-slice_fusion
  521.6 1.5 collective-permute-start.2
  523.1 2.1 join_last.1
  525.2 2.8 collective-permute-done.2.refs_1_
  528.7 2.2 join_grads.3
  530.9 1.0 copy.35
  (33 shorter events, 4.9 us)
Async XLA Ops:
  7.2 210.2 %all-gather.2.cloned.1.call-start = ((), (), s32[]{:S(2)}) async-start(), calls=%async_computation.3 | async-start | bytes 7864320 | tf_op jit(solution)/shard_map/all_gather | solution.py:1063
  7.9 77.6 %copy-start.5 = (bf16[2048]{0:T(1024)(128)(2,1)S(1)}, bf16[2048]{0:T(1024)(128)(2,1)}, u32[]{:S(2)}) copy-start(bf16[2048]{0:T(1024)(128)(2,1)} %param.33) | copy-start | bytes 12292
  7.9 78.2 %copy-start.6 = (bf16[128]{0:T(256)(128)(2,1)S(1)}, bf16[128]{0:T(256)(128)(2,1)}, u32[]{:S(2)}) copy-start(bf16[128]{0:T(256)(128)(2,1)} %param.27) | copy-start | bytes 772
  7.9 78.2 %copy-start.7 = (bf16[128]{0:T(256)(128)(2,1)S(1)}, bf16[128]{0:T(256)(128)(2,1)}, u32[]{:S(2)}) copy-start(bf16[128]{0:T(256)(128)(2,1)} %param.26) | copy-start | bytes 772
  85.4 289.2 %reduce-scatter.4.cloned.1.call-start = ((), (), s32[]{:S(2)}) async-start(), calls=%async_computation.4 | async-start | bytes 7864320 | tf_op jit(solution)/shard_map/reduce_scatter | solution.py:1067
  263.8 174.5 %reduce-scatter.6.cloned.1.call-start = ((), (), s32[]{:S(2)}) async-start(), calls=%async_computation.5 | async-start | bytes 3932160 | tf_op jit(solution)/shard_map/reduce_scatter | solution.py:1067
  374.3 146.3 %reduce-scatter.8.cloned.1.call-start = ((), (), s32[]{:S(2)}) async-start(), calls=%async_computation.6 | async-start | bytes 2621440 | tf_op jit(solution)/shard_map/reduce_scatter | solution.py:1067
  375.8 19.9 %collective-permute-start = (bf16[256,1536]{1,0:T(8,128)(2,1)S(1)}, bf16[256,1536]{1,0:T(8,128)(2,1)S(1)}, u32[]{:S(2)}, u32[]{:S(2)}) collective-permute-start(bf16[256,1536]{1,0:T(8,128)(2,1)S(1)} %constant_dynamic-slice_fusion.2), channel_id=1, source_target_pairs={{0,4},{4,0},{1,5},{5,1},{2,6},{6,2},{3,7},{7,3},{8,12},{12,8},{9,1... | collective-permute-start | bytes 2359304 | tf_op jit(solution)/shard_map/ppermute | solution.py:1052
  394.7 1.0 copy-start.4
  395.7 42.6 %copy-start.1 = (bf16[256,1536]{1,0:T(8,128)(2,1)}, bf16[256,1536]{1,0:T(8,128)(2,1)S(1)}, u32[]{:S(2)}) copy-start(bf16[256,1536]{1,0:T(8,128)(2,1)S(1)} %collective-permute-done.refs_2_) | copy-start | bytes 2359300
  439.4 14.8 %collective-permute-start.1 = (bf16[256,768]{1,0:T(8,128)(2,1)S(1)}, bf16[256,768]{1,0:T(8,128)(2,1)S(1)}, u32[]{:S(2)}, u32[]{:S(2)}) collective-permute-start(bf16[256,768]{1,0:T(8,128)(2,1)S(1)} %constant_dynamic-slice_fusion.1), channel_id=1, source_target_pairs={{0,4},{4,0},{1,5},{5,1},{2,6},{6,2},{3,7},{7,3},{8,12},{12,8},{9,1... | collective-permute-start | bytes 1179656 | tf_op jit(solution)/shard_map/ppermute | solution.py:1052
  454.1 0.7 copy-start.2
  520.5 10.4 %copy-start = (bf16[256,2048]{1,0:T(8,128)(2,1)S(1)}, bf16[256,2048]{1,0:T(8,128)(2,1)}, u32[]{:S(2)}) copy-start(bf16[256,2048]{1,0:T(8,128)(2,1)} %get-tuple-element.147) | copy-start | bytes 3145732
  521.6 6.4 %collective-permute-start.2 = (bf16[256,512]{1,0:T(8,128)(2,1)S(1)}, bf16[256,512]{1,0:T(8,128)(2,1)S(1)}, u32[]{:S(2)}, u32[]{:S(2)}) collective-permute-start(bf16[256,512]{1,0:T(8,128)(2,1)S(1)} %constant_dynamic-slice_fusion), channel_id=1, source_target_pairs={{0,4},{4,0},{1,5},{5,1},{2,6},{6,2},{3,7},{7,3},{8,12},{12,8},{9,1... | collective-permute-start | bytes 786440 | tf_op jit(solution)/shard_map/ppermute | solution.py:1052
  528.0 0.7 copy-start.3
Sparse Core Ops, SparseCore 0:
  85.5 126.3 all-gather.1
  263.9 109.4 reduce-scatter.3
  375.7 60.7 reduce-scatter.5
  438.7 58.9 reduce-scatter.7

commit v4 on v3

--- a/solution.py
+++ b/solution.py
@@ -551,27 +551,41 @@
     diag_y = remote(1, own.at[0, high], y_diag, "y")
     y_high = remote(2, own.at[1, high], y_got.at[high], "y")
     x_low = remote(3, own.at[2, low], x_got.at[low], "x")
-    y_low = remote(4, own.at[1, low], y_got.at[low], "y")
-    x_high = remote(5, own.at[2, high], x_got.at[high], "x")
+    size = half // 2
+    spans = [pl.ds(i * size, size) for i in range(4)]
+    y_low = [remote(4 + i, own.at[1, spans[i]], y_got.at[spans[i]], "y") for i in range(2)]
+    x_high = [remote(6 + i, own.at[2, spans[2 + i]], x_got.at[spans[2 + i]], "x") for i in range(2)]
 
     def second():
         diag_x.wait_recv()
-        add_rows(own.at[1], 0, half, x_diag, 0)
-        y_low.start()
+        for i in range(2):
+            add_rows(own.at[1], i * size, size, x_diag, i * size)
+            y_low[i].start()
         diag_y.wait_recv()
-        add_rows(own.at[2], half, half, y_diag, 0)
-        x_high.start()
+        for i in range(2):
+            add_rows(own.at[2], half + i * size, size, y_diag, i * size)
+            x_high[i].start()
 
     def finish(store, step=32):
-        for copy in (y_high, x_low, y_low, x_high):
-            copy.wait_recv()
-
-        @pl.loop(0, rows // step)
-        def _(i):
-            at = pl.ds(i * step, step)
-            store(at, own[3, at].astype(F32) + x_got[at].astype(F32) + y_got[at].astype(F32))
-
-        for copy in (diag_x, diag_y, y_high, x_low, y_low, x_high):
+        needed = ((x_low, y_low[0]), (y_high, x_high[0]), (y_low[1],), (x_high[1],))
+
+        @pl.loop(0, 4)
+        def _(part):
+            for k, copies in enumerate(needed):
+
+                @pl.when(part == k)
+                def _():
+                    for copy in copies:
+                        copy.wait_recv()
+
+            start = lax.rem(part, 2) * half + lax.div(part, 2) * size
+
+            @pl.loop(0, size // step)
+            def _(i):
+                at = pl.ds(pl.multiple_of(start + i * step, step), step)
+                store(at, own[3, at].astype(F32) + x_got[at].astype(F32) + y_got[at].astype(F32))
+
+        for copy in (diag_x, diag_y, y_high, x_low, *y_low, *x_high):
             copy.wait_send()
 
     return diag_x, diag_y, x_low, y_high, second, finish
@@ -634,8 +648,8 @@
         pltpu.VMEM((rows // 2, width), BF16),
         pltpu.VMEM((rows, width), BF16),
         pltpu.VMEM((rows, width), BF16),
-        pltpu.SemaphoreType.DMA((6,)),
-        pltpu.SemaphoreType.DMA((6,)),
+        pltpu.SemaphoreType.DMA((8,)),
+        pltpu.SemaphoreType.DMA((8,)),
     ]
 
 
@@ -1367,41 +1381,13 @@
 
 
 def feed_grads_kernel(
-    count, tile, mid_ref, low_ref, w_ref, rows_ref, act_ref, dgu_ref, grad_ref, line_ref, total_ref, *sems
+    count, tile, mid_ref, low_ref, w_ref, act_ref, dgu_ref, grad_ref, total_ref
 ):
     step = pl.program_id(0)
-    lines = both_halves(rows_ref, line_ref, *sems)
-
-    @pl.when(step == 0)
-    def _():
-        greet_line((), *lines[0][4]())
-        for steps in lines:
-            steps[0]()
-
     feed_units(count, tile, mid_ref, low_ref, w_ref, w_ref, 2 * count, act_ref, dgu_ref)
-
-    @pl.when(step == 0)
-    def _():
-        lines[0][1]()
-
-    @pl.when(step == pl.num_programs(0) - 1)
-    def _():
-        lines[1][2]()
-
     add_products(step, total_ref, 0, mid_ref, dgu_ref)
     add_products(step, total_ref, 2 * count, low_ref, act_ref)
-
-    @pl.when(step == 0)
-    def _():
-        lines[1][1]()
-        lines[0][2]()
-
     store_low(step, total_ref, grad_ref)
-
-    @pl.when(step == pl.num_programs(0) - 1)
-    def _():
-        for steps in lines:
-            steps[3]()
 
 
 def feed_forward(mid, low, weights, down, block=512):
@@ -1424,7 +1410,7 @@
     )(mid, low, weights, down)
 
 
-def feed_forward_grads(mid, low, weights, line, block=1024):
+def feed_forward_grads(mid, low, weights, block=1024):
     rows, width = mid.shape
     count = weights.shape[1] // 3
     part = lambda cols: pl.BlockSpec((block, cols), lambda i: (i, 0))
@@ -1435,18 +1421,15 @@
             jax.ShapeDtypeStruct((rows, count), BF16),
             jax.ShapeDtypeStruct((rows, 2 * count), BF16),
             jax.ShapeDtypeStruct(weights.shape, BF16),
-            jax.ShapeDtypeStruct((4 * line.shape[0], line.shape[1]), BF16),
         ),
         grid=(rows // block,),
-        in_specs=[part(width), part(width), whole, pl.BlockSpec(memory_space=pltpu.VMEM)],
-        out_specs=(part(count), part(2 * count), whole, pl.BlockSpec(memory_space=pl.ANY)),
-        scratch_shapes=[pltpu.VMEM(weights.shape, F32), *LINE_SEMAPHORES],
-        compiler_params=pltpu.CompilerParams(
-            collective_id=9, has_side_effects=True, vmem_limit_bytes=VMEM_BYTES
-        ),
+        in_specs=[part(width), part(width), whole],
+        out_specs=(part(count), part(2 * count), whole),
+        scratch_shapes=[pltpu.VMEM(weights.shape, F32)],
+        compiler_params=pltpu.CompilerParams(vmem_limit_bytes=VMEM_BYTES),
         cost_estimate=micros(41),
         name="feed_forward_grads",
-    )(mid, low, weights, line)
+    )(mid, low, weights)
 
 
 def attend_back_kernel(
@@ -1916,6 +1899,7 @@
         head,
     )
     w_first = gather_rows(rows_first)
+    w_last_gu = gather_rows(rows_gu)
 
     query_scale, key_scale = query_gain.astype(F32)[None], key_gain.astype(F32)[None]
     qkv, attended, logs, gate_sig, mixed, out_all = attend(
@@ -1929,8 +1913,9 @@
     )
     mid_all, w_last_d = gather_tokens(normed_mid, rows_d)
 
-    act_first, dgu_first, grad_first, w_last_gu = feed_forward_grads(mid_all, out_all, w_first, rows_gu)
+    act_first, dgu_first, grad_first = feed_forward_grads(mid_all, out_all, w_first)
     part_first = scatter_grads(grad_first)
+    w_last_gu, grad_first = lax.optimization_barrier((w_last_gu, grad_first))
     act_last, dgu_last = feed_forward(mid_all, out_all, w_last_gu, w_last_d)
     dhidden, dbranch, grad_gain_mid = scatter_products(
         middle_back_kernel,

time: 539 us -> 535 us (level)
  Pallas kernels: 505 us -> 499 us
  transfers between devices with their start and end apart: 7 -> 8, of which waited for: 2 -> 2; matrix products, arithmetic and copies ran while one was open for 1% -> 1% of each run, Pallas kernels for 70% -> 79%
where the time goes in v4:
time: 535 us; the launch traced here: 534 us
  Pallas kernels  499 us (93%)
  between operations  14.6 us (3%)
  local copies, waits for them, and re-layouts  7 us (1%)
    pallas_call x2, Pallas kernels, scatter_products(): pl.pallas_call(functools.partial(kernel, [item[2] for item in group]), ou...  99.2 us
    pallas_call x1, Pallas kernels, opening(): pl.pallas_call(functools.partial(opening_kernel, pieces), out_shape=(shap...  77.5 us
    pallas_call x1, Pallas kernels, tail(): pl.pallas_call(functools.partial(tail_kernel, [item[2] for item in group]...  61.9 us
    pallas_call x1, Pallas kernels, gather_beside(): pl.pallas_call(functools.partial(gather_beside_kernel, [item[2] for item...  43.6 us
    pallas_call x1, Pallas kernels, attend(): pl.pallas_call(functools.partial(attend_kernel, heads, head, block), out_...  43.4 us
    pallas_call x1, Pallas kernels, feed_forward_grads(): pl.pallas_call(functools.partial(feed_grads_kernel, count, 256), out_shap...  41.6 us
    pallas_call x1, Pallas kernels, attend_back(): pl.pallas_call(functools.partial(attend_back_kernel, heads, head, block),...  41.6 us
    pallas_call x1, Pallas kernels, gather_tokens(): pl.pallas_call(gather_kernel, out_shape=(jax.ShapeDtypeStruct((2, 2, 2, r...  41.2 us
  transfers between devices with their start and end apart: 8, of which 2 were waited for; matrix products, arithmetic and copies ran while one was open for 1% of the time, Pallas kernels for 79%

profile of v4, /device:TPU:0, one launch (start us, length us, event | category | flops | bytes accessed | tf_op | source)
XLA Modules:
  0.0 534.3 jit_solution(10770203425668853005)
XLA Ops:
  7.9 77.5 %opening.1 = (bf16[2,2,2,256,2048]{4,3,2,1,0:T(8,128)(2,1)}, bf16[2048,512]{1,0:T(8,128)(2,1)}, bf16[2048,512]{1,0:T(8,128)(2,1)}, bf16[512,1536]{1,0:T(8,128)(2...) custom-call(bf16[256,2048]{1,0:T(8,128)(2,1)} %bitcast.32, ...), custom_call_target="tpu_custom_call" | custom-call | bytes 264000000 | tf_op jit(solution)/shard_map/opening/pallas_call | solution.py:427
  87.3 43.4 %attend.1 = (f32[2048,512]{1,0:T(8,128)}, f32[2048,256]{1,0:T(8,128)}, f32[2,2048,1]{2,1,0:T(8,128)}, f32[2048,256]{1,0:T(8,128)}, bf16[2048,256]{1,0:T(8,128)(2,1)}, /*index=5*/bf16[2,2,2,256,2048]{4,3,2,1,0:T(8,128)(2,1)}) custom-call(bf16[2048,2048]{1,0:T(8,128)(2,1)} %bitcast.23, bf16[2048,512]{1,0:T(8,128)(2,1)} %get-tuple-element.90.w_ref.refs_2_, ...), custom_call_target="tpu_custom_call" | custom-call | bytes 138600000 | tf_op jit(solution)/shard_map/attend/pallas_call | solution.py:1229
  130.8 45.4 %scatter_products.2 = (f32[256,2048]{1,0:T(8,128)}, f32[256,1]{1,0:T(8,128)}, bf16[256,2048]{1,0:T(8,128)(2,1)}) custom-call(bf16[2048,256]{1,0:T(8,128)(2,1)} %get-tuple-element.96.refs_0_.mixed_ref, bf16[2048,512]{1,0:T(8,128)(2,1)} %get-tuple-element.91.wg_ref.refs_1_.w_ref.refs_3_, bf16[256,2048]{1,0:T(8,128)(2,1)} %bitcast.33, ...), custom_call_target="tpu_custom_call" | custom-call | bytes 158400000 | tf_op jit(solution)/shard_map/scatter_products/pallas_call | solution.py:708
  176.2 41.2 %gather_tokens.1 = (bf16[2,2,2,256,2048]{4,3,2,1,0:T(8,128)(2,1)}, bf16[2048,256]{1,0:T(8,128)(2,1)}) custom-call(bf16[256,2048]{1,0:T(8,128)(2,1)} %get-tuple-element.97.source, bf16[512,256]{1,0:T(8,128)(2,1)} %get-tuple-element.98.rows_ref), custom_call_target="tpu_custom_call" | custom-call | bytes 138600000 | tf_op jit(solution)/shard_map/gather_tokens/pallas_call | solution.py:310
  217.5 41.6 %feed_forward_grads.1 = (bf16[2048,512]{1,0:T(8,128)(2,1)}, bf16[2048,1024]{1,0:T(8,128)(2,1)}, bf16[2048,1536]{1,0:T(8,128)(2,1)}) custom-call(bf16[2048,2048]{1,0:T(8,128)(2,1)} %bitcast.29, bf16[2048,2048]{1,0:T(8,128)(2,1)} %bitcast.26, bf16[2048,1536]{1,0:T(8,128)(2,1)} %all-gather.3.cloned.1.call-done.w_ref.refs_2_), custom_call_target="tpu_custom_call" | custom-call | bytes 135300000 | tf_op jit(solution)/shard_map/feed_forward_grads/pallas_call | solution.py:1418
  259.4 12.9 %feed_forward.1 = (bf16[2048,256]{1,0:T(8,128)(2,1)}, bf16[2048,512]{1,0:T(8,128)(2,1)}) custom-call(bf16[2048,2048]{1,0:T(8,128)(2,1)} %bitcast.30, bf16[2048,2048]{1,0:T(8,128)(2,1)} %bitcast.27, bf16[2048,512]{1,0:T(8,128)(2,1)} %all-gather.5.cloned.1.call-done.gu_ref.refs_3_, bf16[2048,256]{1,0:T(8,128)(2,1)} %get-tuple-element.106.down_ref.refs_3_), custom_call_target="tpu_custom_call" | custom-call | bytes 46200000 | tf_op jit(solution)/shard_map/feed_forward/pallas_call | solution.py:1398
  272.3 53.8 %scatter_products.3 = (f32[256,2048]{1,0:T(8,128)}, bf16[256,2048]{1,0:T(8,128)(2,1)}, f32[1,2048]{1,0:T(1,128)}) custom-call(bf16[2048,1024]{1,0:T(8,128)(2,1)} %get-tuple-element.102.refs_0_, bf16[2048,512]{1,0:T(8,128)(2,1)} %get-tuple-element.107.refs_1_.refs_6_, bf16[2048,1536]{1,0:T(8,128)(2,1)} %all-gather.3.cloned.1.call-done.w_ref.refs_2_, ...), custom_call_target="tpu_custom_call" | custom-call | bytes 158400000 | tf_op jit(solution)/shard_map/scatter_products/pallas_call | solution.py:708
  326.1 43.6 %gather_beside.1 = (bf16[2,2,2,256,2048]{4,3,2,1,0:T(8,128)(2,1)}, bf16[4,256,2048]{2,1,0:T(8,128)(2,1)}, bf16[2048,768]{1,0:T(8,128)(2,1)}) custom-call(bf16[256,2048]{1,0:T(8,128)(2,1)} %get-tuple-element.111.shard_ref, bf16[2048,512]{1,0:T(8,128)(2,1)} %get-tuple-element.112.refs_0_, bf16[2048,256]{1,0:T(8,128)(2,1)} %get-tuple-element.113.refs_1_.refs_7_, ...), custom_call_target="tpu_custom_call" | custom-call | bytes 145200000 | tf_op jit(solution)/shard_map/gather_beside/pallas_call | solution.py:794
  370.0 1.2 constant_dynamic-slice_fusion.2
  371.2 1.0 collective-permute-start
  372.3 17.6 %gate_back.1 = (bf16[2048,256]{1,0:T(8,128)(2,1)}, bf16[2048,256]{1,0:T(8,128)(2,1)}, bf16[2048,512]{1,0:T(8,128)(2,1)}) custom-call(bf16[2048,2048]{1,0:T(8,128)(2,1)} %bitcast.24, bf16[2048,2048]{1,0:T(8,128)(2,1)} %bitcast.35, bf16[2048,512]{1,0:T(8,128)(2,1)} %get-tuple-element.91.wg_ref.refs_1_.w_ref.refs_3_, ...), custom_call_target="tpu_custom_call" | custom-call | bytes 82500000 | tf_op jit(solution)/shard_map/gate_back/pallas_call | solution.py:1339
  389.9 1.3 collective-permute-done.refs_2_
  391.9 41.6 %attend_back.1 = (bf16[2048,512]{1,0:T(8,128)(2,1)}, f32[1,128]{1,0:T(1,128)}, f32[1,128]{1,0:T(1,128)}, f32[256,2048]{1,0:T(8,128)}) custom-call(f32[2048,512]{1,0:T(8,128)} %get-tuple-element.95.raw_ref, bf16[2048,256]{1,0:T(8,128)(2,1)} %get-tuple-element.121.up_ref, f32[2,2048,1]{2,1,0:T(8,128)} %get-tuple-element.122.log_ref, ...), custom_call_target="tpu_custom_call" | custom-call | bytes 132000000 | tf_op jit(solution)/shard_map/attend_back/pallas_call | solution.py:1525
  433.5 1.0 constant_dynamic-slice_fusion.1
  434.5 1.1 collective-permute-start.1
  435.6 3.5 add_convert_fusion
  439.0 10.3 %weight_grads.1.refs_4_ = bf16[2048,512]{1,0:T(8,128)(2,1)} custom-call(bf16[2048,2048]{1,0:T(8,128)(2,1)} %bitcast.25, bf16[2048,512]{1,0:T(8,128)(2,1)} %get-tuple-element.128.right_ref.refs_0_), custom_call_target="tpu_custom_call" | custom-call | bytes 36300000 | tf_op jit(solution)/shard_map/weight_grads/pallas_call | solution.py:1309
  450.0 4.5 join_grads.2
  454.5 61.9 %tail.1 = (bf16[256,2048]{1,0:T(8,128)(2,1)}, bf16[256,512]{1,0:T(8,128)(2,1)}, bf16[256,512]{1,0:T(8,128)(2,1)}, f32[1,4352]{1,0:T(1,128)}) custom-call(bf16[2048,512]{1,0:T(8,128)(2,1)} %get-tuple-element.128.right_ref.refs_0_, bf16[2048,256]{1,0:T(8,128)(2,1)} %get-tuple-element.138.refs_1_, bf16[2048,512]{1,0:T(8,128)(2,1)} %get-tuple-element.90.w_ref.refs_2_, ...), custom_call_target="tpu_custom_call" | custom-call | bytes 171600000 | tf_op jit(solution)/shard_map/tail/pallas_call | solution.py:1041
  516.4 1.1 constant_dynamic-slice_fusion
  517.5 1.5 collective-permute-start.2
  519.0 2.1 join_last.1
  521.1 2.8 collective-permute-done.2.refs_1_
  524.6 2.2 join_grads.3
  (36 shorter events, 5.7 us)
Async XLA Ops:
  7.2 210.3 %all-gather.3.cloned.1.call-start = ((), (), s32[]{:S(2)}) async-start(), calls=%async_computation.3 | async-start | bytes 7864320 | tf_op jit(solution)/shard_map/all_gather | solution.py:1077
  85.3 0.9 copy-start.5
  85.4 1.5 copy-start.6
  85.4 1.5 copy-start.7
  85.4 173.9 %all-gather.5.cloned.1.call-start = ((), (), s32[]{:S(2)}) async-start(), calls=%async_computation.4 | async-start | bytes 2621440 | tf_op jit(solution)/shard_map/all_gather | solution.py:1077
  86.2 283.9 %reduce-scatter.4.cloned.1.call-start = ((), (), s32[]{:S(2)}) async-start(), calls=%async_computation.5 | async-start | bytes 7864320 | tf_op jit(solution)/shard_map/reduce_scatter | solution.py:1081
  259.1 174.4 %reduce-scatter.6.cloned.1.call-start = ((), (), s32[]{:S(2)}) async-start(), calls=%async_computation.6 | async-start | bytes 3932160 | tf_op jit(solution)/shard_map/reduce_scatter | solution.py:1081
  369.7 146.7 %reduce-scatter.8.cloned.1.call-start = ((), (), s32[]{:S(2)}) async-start(), calls=%async_computation.7 | async-start | bytes 2621440 | tf_op jit(solution)/shard_map/reduce_scatter | solution.py:1081
  371.2 19.9 %collective-permute-start = (bf16[256,1536]{1,0:T(8,128)(2,1)S(1)}, bf16[256,1536]{1,0:T(8,128)(2,1)S(1)}, u32[]{:S(2)}, u32[]{:S(2)}) collective-permute-start(bf16[256,1536]{1,0:T(8,128)(2,1)S(1)} %constant_dynamic-slice_fusion.2), channel_id=1, source_target_pairs={{0,4},{4,0},{1,5},{5,1},{2,6},{6,2},{3,7},{7,3},{8,12},{12,8},{9,1... | collective-permute-start | bytes 2359304 | tf_op jit(solution)/shard_map/ppermute | solution.py:1066
  389.9 1.3 copy-start.4
  391.2 42.3 %copy-start.1 = (bf16[256,1536]{1,0:T(8,128)(2,1)}, bf16[256,1536]{1,0:T(8,128)(2,1)S(1)}, u32[]{:S(2)}) copy-start(bf16[256,1536]{1,0:T(8,128)(2,1)S(1)} %collective-permute-done.refs_2_) | copy-start | bytes 2359300
  434.5 14.8 %collective-permute-start.1 = (bf16[256,768]{1,0:T(8,128)(2,1)S(1)}, bf16[256,768]{1,0:T(8,128)(2,1)S(1)}, u32[]{:S(2)}, u32[]{:S(2)}) collective-permute-start(bf16[256,768]{1,0:T(8,128)(2,1)S(1)} %constant_dynamic-slice_fusion.1), channel_id=1, source_target_pairs={{0,4},{4,0},{1,5},{5,1},{2,6},{6,2},{3,7},{7,3},{8,12},{12,8},{9,1... | collective-permute-start | bytes 1179656 | tf_op jit(solution)/shard_map/ppermute | solution.py:1066
  449.3 0.7 copy-start.2
  516.4 10.4 %copy-start = (bf16[256,2048]{1,0:T(8,128)(2,1)S(1)}, bf16[256,2048]{1,0:T(8,128)(2,1)}, u32[]{:S(2)}) copy-start(bf16[256,2048]{1,0:T(8,128)(2,1)} %get-tuple-element.147) | copy-start | bytes 3145732
  517.5 6.4 %collective-permute-start.2 = (bf16[256,512]{1,0:T(8,128)(2,1)S(1)}, bf16[256,512]{1,0:T(8,128)(2,1)S(1)}, u32[]{:S(2)}, u32[]{:S(2)}) collective-permute-start(bf16[256,512]{1,0:T(8,128)(2,1)S(1)} %constant_dynamic-slice_fusion), channel_id=1, source_target_pairs={{0,4},{4,0},{1,5},{5,1},{2,6},{6,2},{3,7},{7,3},{8,12},{12,8},{9,1... | collective-permute-start | bytes 786440 | tf_op jit(solution)/shard_map/ppermute | solution.py:1066
  523.9 0.7 copy-start.3
Sparse Core Ops, SparseCore 0:
  85.5 126.3 all-gather.2
  213.5 44.1 all-gather.4
  259.9 109.4 reduce-scatter.3
  371.6 60.7 reduce-scatter.5
  434.5 58.8 reduce-scatter.7

commit v5 on v4

--- a/solution.py
+++ b/solution.py
@@ -473,7 +473,8 @@
     y, x, c, device = place()
     remote = remote_copies(send, recv, device)
     rows, width = own.shape[1:]
-    half, both, tile = rows // 2, 2 * rows, 256
+    half, both = rows // 2, 2 * rows
+    tile = 512 if sum(ref.shape[2] for ref in left_vmem) <= 256 else 256
     targets = ((1 - y, 1 - x), (1 - y, x), (y, 1 - x), (y, x))
     pieces = ((0, 0, half), (0, half, half), (1, 0, rows), (2, 0, rows), (3, 0, rows))
     count = len(lefts)
@@ -1390,7 +1391,7 @@
     store_low(step, total_ref, grad_ref)
 
 
-def feed_forward(mid, low, weights, down, block=512):
+def feed_forward(mid, low, weights, down, block=256):
     rows, width = mid.shape
     count = down.shape[1]
     part = lambda cols: pl.BlockSpec((block, cols), lambda i: (i, 0))

time: 535 us -> 535 us (level)
  no operation moved by 1% of the time
where the time goes in v5:
time: 535 us
  Pallas kernels  500 us (93%)
  between operations  14.6 us (3%)
  local copies, waits for them, and re-layouts  7 us (1%)
    pallas_call x2, Pallas kernels, scatter_products(): pl.pallas_call(functools.partial(kernel, [item[2] for item in group]), ou...  98.2 us
    pallas_call x1, Pallas kernels, opening(): pl.pallas_call(functools.partial(opening_kernel, pieces), out_shape=(shap...  77.5 us
    pallas_call x1, Pallas kernels, tail(): pl.pallas_call(functools.partial(tail_kernel, [item[2] for item in group]...  61.8 us
    pallas_call x1, Pallas kernels, gather_beside(): pl.pallas_call(functools.partial(gather_beside_kernel, [item[2] for item...  43.6 us
    pallas_call x1, Pallas kernels, attend(): pl.pallas_call(functools.partial(attend_kernel, heads, head, block), out_...  43.4 us
    pallas_call x1, Pallas kernels, feed_forward_grads(): pl.pallas_call(functools.partial(feed_grads_kernel, count, 256), out_shap...  41.7 us
    pallas_call x1, Pallas kernels, attend_back(): pl.pallas_call(functools.partial(attend_back_kernel, heads, head, block),...  41.5 us
    pallas_call x1, Pallas kernels, gather_tokens(): pl.pallas_call(gather_kernel, out_shape=(jax.ShapeDtypeStruct((2, 2, 2, r...  41.2 us
  transfers between devices with their start and end apart: 8, of which 2 were waited for; matrix products, arithmetic and copies ran while one was open for 1% of the time, Pallas kernels for 79%

profile of v5, /device:TPU:0, one launch (start us, length us, event | category | flops | bytes accessed | tf_op | source)
XLA Modules:
  0.0 534.6 jit_solution(17927423454624431386)
XLA Ops:
  7.9 77.5 %opening.1 = (bf16[2,2,2,256,2048]{4,3,2,1,0:T(8,128)(2,1)}, bf16[2048,512]{1,0:T(8,128)(2,1)}, bf16[2048,512]{1,0:T(8,128)(2,1)}, bf16[512,1536]{1,0:T(8,128)(2...) custom-call(bf16[256,2048]{1,0:T(8,128)(2,1)} %bitcast.32, ...), custom_call_target="tpu_custom_call" | custom-call | bytes 264000000 | tf_op jit(solution)/shard_map/opening/pallas_call | solution.py:427
  87.3 43.4 %attend.1 = (f32[2048,512]{1,0:T(8,128)}, f32[2048,256]{1,0:T(8,128)}, f32[2,2048,1]{2,1,0:T(8,128)}, f32[2048,256]{1,0:T(8,128)}, bf16[2048,256]{1,0:T(8,128)(2,1)}, /*index=5*/bf16[2,2,2,256,2048]{4,3,2,1,0:T(8,128)(2,1)}) custom-call(bf16[2048,2048]{1,0:T(8,128)(2,1)} %bitcast.23, bf16[2048,512]{1,0:T(8,128)(2,1)} %get-tuple-element.90.w_ref.refs_2_, ...), custom_call_target="tpu_custom_call" | custom-call | bytes 138600000 | tf_op jit(solution)/shard_map/attend/pallas_call | solution.py:1230
  130.8 44.6 %scatter_products.2 = (f32[256,2048]{1,0:T(8,128)}, f32[256,1]{1,0:T(8,128)}, bf16[256,2048]{1,0:T(8,128)(2,1)}) custom-call(bf16[2048,256]{1,0:T(8,128)(2,1)} %get-tuple-element.96.refs_0_.mixed_ref, bf16[2048,512]{1,0:T(8,128)(2,1)} %get-tuple-element.91.wg_ref.refs_1_.w_ref.refs_3_, bf16[256,2048]{1,0:T(8,128)(2,1)} %bitcast.33, ...), custom_call_target="tpu_custom_call" | custom-call | bytes 158400000 | tf_op jit(solution)/shard_map/scatter_products/pallas_call | solution.py:709
  175.4 41.2 %gather_tokens.1 = (bf16[2,2,2,256,2048]{4,3,2,1,0:T(8,128)(2,1)}, bf16[2048,256]{1,0:T(8,128)(2,1)}) custom-call(bf16[256,2048]{1,0:T(8,128)(2,1)} %get-tuple-element.97.source, bf16[512,256]{1,0:T(8,128)(2,1)} %get-tuple-element.98.rows_ref), custom_call_target="tpu_custom_call" | custom-call | bytes 138600000 | tf_op jit(solution)/shard_map/gather_tokens/pallas_call | solution.py:310
  216.7 41.7 %feed_forward_grads.1 = (bf16[2048,512]{1,0:T(8,128)(2,1)}, bf16[2048,1024]{1,0:T(8,128)(2,1)}, bf16[2048,1536]{1,0:T(8,128)(2,1)}) custom-call(bf16[2048,2048]{1,0:T(8,128)(2,1)} %bitcast.29, bf16[2048,2048]{1,0:T(8,128)(2,1)} %bitcast.26, bf16[2048,1536]{1,0:T(8,128)(2,1)} %all-gather.3.cloned.1.call-done.w_ref.refs_2_), custom_call_target="tpu_custom_call" | custom-call | bytes 135300000 | tf_op jit(solution)/shard_map/feed_forward_grads/pallas_call | solution.py:1419
  258.7 14.1 %feed_forward.1 = (bf16[2048,256]{1,0:T(8,128)(2,1)}, bf16[2048,512]{1,0:T(8,128)(2,1)}) custom-call(bf16[2048,2048]{1,0:T(8,128)(2,1)} %bitcast.30, bf16[2048,2048]{1,0:T(8,128)(2,1)} %bitcast.27, bf16[2048,512]{1,0:T(8,128)(2,1)} %all-gather.5.cloned.1.call-done.gu_ref.refs_3_, bf16[2048,256]{1,0:T(8,128)(2,1)} %get-tuple-element.106.down_ref.refs_3_), custom_call_target="tpu_custom_call" | custom-call | bytes 46200000 | tf_op jit(solution)/shard_map/feed_forward/pallas_call | solution.py:1399
  272.8 53.6 %scatter_products.3 = (f32[256,2048]{1,0:T(8,128)}, bf16[256,2048]{1,0:T(8,128)(2,1)}, f32[1,2048]{1,0:T(1,128)}) custom-call(bf16[2048,1024]{1,0:T(8,128)(2,1)} %get-tuple-element.102.refs_0_, bf16[2048,512]{1,0:T(8,128)(2,1)} %get-tuple-element.107.refs_1_.refs_6_, bf16[2048,1536]{1,0:T(8,128)(2,1)} %all-gather.3.cloned.1.call-done.w_ref.refs_2_, ...), custom_call_target="tpu_custom_call" | custom-call | bytes 158400000 | tf_op jit(solution)/shard_map/scatter_products/pallas_call | solution.py:709
  326.4 43.6 %gather_beside.1 = (bf16[2,2,2,256,2048]{4,3,2,1,0:T(8,128)(2,1)}, bf16[4,256,2048]{2,1,0:T(8,128)(2,1)}, bf16[2048,768]{1,0:T(8,128)(2,1)}) custom-call(bf16[256,2048]{1,0:T(8,128)(2,1)} %get-tuple-element.111.shard_ref, bf16[2048,512]{1,0:T(8,128)(2,1)} %get-tuple-element.112.refs_0_, bf16[2048,256]{1,0:T(8,128)(2,1)} %get-tuple-element.113.refs_1_.refs_7_, ...), custom_call_target="tpu_custom_call" | custom-call | bytes 145200000 | tf_op jit(solution)/shard_map/gather_beside/pallas_call | solution.py:795
  370.4 1.2 constant_dynamic-slice_fusion.2
  371.6 1.0 collective-permute-start
  372.5 17.6 %gate_back.1 = (bf16[2048,256]{1,0:T(8,128)(2,1)}, bf16[2048,256]{1,0:T(8,128)(2,1)}, bf16[2048,512]{1,0:T(8,128)(2,1)}) custom-call(bf16[2048,2048]{1,0:T(8,128)(2,1)} %bitcast.24, bf16[2048,2048]{1,0:T(8,128)(2,1)} %bitcast.35, bf16[2048,512]{1,0:T(8,128)(2,1)} %get-tuple-element.91.wg_ref.refs_1_.w_ref.refs_3_, ...), custom_call_target="tpu_custom_call" | custom-call | bytes 82500000 | tf_op jit(solution)/shard_map/gate_back/pallas_call | solution.py:1340
  390.2 1.3 collective-permute-done.refs_2_
  392.2 41.5 %attend_back.1 = (bf16[2048,512]{1,0:T(8,128)(2,1)}, f32[1,128]{1,0:T(1,128)}, f32[1,128]{1,0:T(1,128)}, f32[256,2048]{1,0:T(8,128)}) custom-call(f32[2048,512]{1,0:T(8,128)} %get-tuple-element.95.raw_ref, bf16[2048,256]{1,0:T(8,128)(2,1)} %get-tuple-element.121.up_ref, f32[2,2048,1]{2,1,0:T(8,128)} %get-tuple-element.122.log_ref, ...), custom_call_target="tpu_custom_call" | custom-call | bytes 132000000 | tf_op jit(solution)/shard_map/attend_back/pallas_call | solution.py:1526
  433.8 1.0 constant_dynamic-slice_fusion.1
  434.8 1.1 collective-permute-start.1
  435.9 3.5 add_convert_fusion
  439.4 10.3 %weight_grads.1.refs_4_ = bf16[2048,512]{1,0:T(8,128)(2,1)} custom-call(bf16[2048,2048]{1,0:T(8,128)(2,1)} %bitcast.25, bf16[2048,512]{1,0:T(8,128)(2,1)} %get-tuple-element.128.right_ref.refs_0_), custom_call_target="tpu_custom_call" | custom-call | bytes 36300000 | tf_op jit(solution)/shard_map/weight_grads/pallas_call | solution.py:1310
  450.4 4.5 join_grads.2
  454.8 61.8 %tail.1 = (bf16[256,2048]{1,0:T(8,128)(2,1)}, bf16[256,512]{1,0:T(8,128)(2,1)}, bf16[256,512]{1,0:T(8,128)(2,1)}, f32[1,4352]{1,0:T(1,128)}) custom-call(bf16[2048,512]{1,0:T(8,128)(2,1)} %get-tuple-element.128.right_ref.refs_0_, bf16[2048,256]{1,0:T(8,128)(2,1)} %get-tuple-element.138.refs_1_, bf16[2048,512]{1,0:T(8,128)(2,1)} %get-tuple-element.90.w_ref.refs_2_, ...), custom_call_target="tpu_custom_call" | custom-call | bytes 171600000 | tf_op jit(solution)/shard_map/tail/pallas_call | solution.py:1042
  516.7 1.1 constant_dynamic-slice_fusion
  517.8 1.5 collective-permute-start.2
  519.3 2.1 join_last.1
  521.4 2.8 collective-permute-done.2.refs_1_
  524.9 2.2 join_grads.3
  (36 shorter events, 5.7 us)
Async XLA Ops:
  7.2 209.5 %all-gather.3.cloned.1.call-start = ((), (), s32[]{:S(2)}) async-start(), calls=%async_computation.3 | async-start | bytes 7864320 | tf_op jit(solution)/shard_map/all_gather | solution.py:1078
  85.3 0.9 copy-start.5
  85.4 1.5 copy-start.6
  85.4 1.5 copy-start.7
  85.4 173.3 %all-gather.5.cloned.1.call-start = ((), (), s32[]{:S(2)}) async-start(), calls=%async_computation.4 | async-start | bytes 2621440 | tf_op jit(solution)/shard_map/all_gather | solution.py:1078
  86.2 284.2 %reduce-scatter.4.cloned.1.call-start = ((), (), s32[]{:S(2)}) async-start(), calls=%async_computation.5 | async-start | bytes 7864320 | tf_op jit(solution)/shard_map/reduce_scatter | solution.py:1082
  258.4 175.3 %reduce-scatter.6.cloned.1.call-start = ((), (), s32[]{:S(2)}) async-start(), calls=%async_computation.6 | async-start | bytes 3932160 | tf_op jit(solution)/shard_map/reduce_scatter | solution.py:1082
  370.1 146.7 %reduce-scatter.8.cloned.1.call-start = ((), (), s32[]{:S(2)}) async-start(), calls=%async_computation.7 | async-start | bytes 2621440 | tf_op jit(solution)/shard_map/reduce_scatter | solution.py:1082
  371.6 19.9 %collective-permute-start = (bf16[256,1536]{1,0:T(8,128)(2,1)S(1)}, bf16[256,1536]{1,0:T(8,128)(2,1)S(1)}, u32[]{:S(2)}, u32[]{:S(2)}) collective-permute-start(bf16[256,1536]{1,0:T(8,128)(2,1)S(1)} %constant_dynamic-slice_fusion.2), channel_id=1, source_target_pairs={{0,4},{4,0},{1,5},{5,1},{2,6},{6,2},{3,7},{7,3},{8,12},{12,8},{9,1... | collective-permute-start | bytes 2359304 | tf_op jit(solution)/shard_map/ppermute | solution.py:1067
  390.2 1.4 copy-start.4
  391.5 42.2 %copy-start.1 = (bf16[256,1536]{1,0:T(8,128)(2,1)}, bf16[256,1536]{1,0:T(8,128)(2,1)S(1)}, u32[]{:S(2)}) copy-start(bf16[256,1536]{1,0:T(8,128)(2,1)S(1)} %collective-permute-done.refs_2_) | copy-start | bytes 2359300
  434.8 14.8 %collective-permute-start.1 = (bf16[256,768]{1,0:T(8,128)(2,1)S(1)}, bf16[256,768]{1,0:T(8,128)(2,1)S(1)}, u32[]{:S(2)}, u32[]{:S(2)}) collective-permute-start(bf16[256,768]{1,0:T(8,128)(2,1)S(1)} %constant_dynamic-slice_fusion.1), channel_id=1, source_target_pairs={{0,4},{4,0},{1,5},{5,1},{2,6},{6,2},{3,7},{7,3},{8,12},{12,8},{9,1... | collective-permute-start | bytes 1179656 | tf_op jit(solution)/shard_map/ppermute | solution.py:1067
  449.6 0.7 copy-start.2
  516.7 10.4 %copy-start = (bf16[256,2048]{1,0:T(8,128)(2,1)S(1)}, bf16[256,2048]{1,0:T(8,128)(2,1)}, u32[]{:S(2)}) copy-start(bf16[256,2048]{1,0:T(8,128)(2,1)} %get-tuple-element.147) | copy-start | bytes 3145732
  517.8 6.4 %collective-permute-start.2 = (bf16[256,512]{1,0:T(8,128)(2,1)S(1)}, bf16[256,512]{1,0:T(8,128)(2,1)S(1)}, u32[]{:S(2)}, u32[]{:S(2)}) collective-permute-start(bf16[256,512]{1,0:T(8,128)(2,1)S(1)} %constant_dynamic-slice_fusion), channel_id=1, source_target_pairs={{0,4},{4,0},{1,5},{5,1},{2,6},{6,2},{3,7},{7,3},{8,12},{12,8},{9,1... | collective-permute-start | bytes 786440 | tf_op jit(solution)/shard_map/ppermute | solution.py:1067
  524.2 0.7 copy-start.3
Sparse Core Ops, SparseCore 0:
  85.5 126.6 all-gather.2
  213.8 44.0 all-gather.4
  260.2 109.4 reduce-scatter.3
  371.9 60.7 reduce-scatter.5
  434.8 58.9 reduce-scatter.7
